TPU v7x, 256 devices: a whole 4x4x8 slice. The times are simulated.
256 devices in a mesh: epoch: 32 (over x, z), param: 8 (over y, core).
Axes of the slice: x: 4, y: 4, z: 8, core: 2. Of those that a mesh axis runs over, the one named last changes fastest.
Arguments:
- initial_carry: float32 [48, 8192], P(None, 'param'), may hold values from -6 to 6
- forcing: bfloat16 [128, 48, 8192], P('epoch', None, 'param'), may hold values from -2.390625 to 2.390625
- transition: float32 [128, 6, 6, 8], P('epoch'), may hold values from -0.2 to 1.2
- partials: float32 [6, 4096], P(None, 'epoch'), may hold values from -40 to 40
- arc_of_row: int32 [4096], P('epoch'), may hold values from 0 to 7
- counts: int32 [128], P('epoch'), may hold values from 8 to 32
Outputs:
- packed: float32 [4096, 8192], P('epoch', 'param')
- r_rows: float32 [512, 8192], P(None, 'param')
Inputs may be any that keep to these rules, and one draw needn't show every extreme that they name: Rows of block j at positions counts[j] and beyond carry no observation.
All inputs are finite; a program needn't handle non-finite values.
Results may differ from a plain program's by a relative error of at most 0.0003.
Values sent between devices are 32-bit elements; how exact they have to be, the bound alone decides.
No kernel may reach another device: no remote copies, remote signals or barrier semaphores. Data moves between devices by JAX's collectives and lax.ppermute only.
A program may use at most 64 MiB of HBM per device.

v0:
```python
import math

import jax
import jax.numpy as jnp
from jax import lax
from jax.experimental import pallas as pl
from jax.experimental.pallas import tpu as pltpu
from jax.sharding import Mesh
from jax.sharding import PartitionSpec as P


PANEL = 512
X, Z, Y, C = 4, 8, 4, 2
STATE, ARCS = 6, 8
S = STATE * ARCS
PACK = S + 8
HI = lax.Precision.HIGHEST
VMEM = pl.BlockSpec(memory_space=pltpu.VMEM)
SMEM = pl.BlockSpec(memory_space=pltpu.SMEM)


def call(kernel, out, n, cost, smem=()):
    flops, size = cost
    return pl.pallas_call(
        kernel,
        out_shape=out,
        in_specs=[SMEM if i in smem else VMEM for i in range(n)],
        out_specs=VMEM if not isinstance(out, (tuple, list)) else [VMEM] * len(out),
        cost_estimate=pl.CostEstimate(flops=flops, bytes_accessed=size, transcendentals=0),
    )


def dot(a, b, ca=1, cb=0):
    return lax.dot_general(a, b, (((ca,), (cb,)), ((), ())), precision=HI, preferred_element_type=jnp.float32)


def coefficients(tile):
    spread = lambda k: jnp.broadcast_to(tile[:, k : k + 1], (ARCS, 128))
    return [[spread(c * STATE + d) for d in range(STATE)] for c in range(STATE)]


def moved(coefficient, parts):
    out = []
    for row in coefficient:
        total = row[0] * parts[0]
        for d in range(1, STATE):
            total = total + row[d] * parts[d]
        out.append(total)
    return out


def split(value):
    return [value[c * ARCS : (c + 1) * ARCS] for c in range(STATE)]


def opened(tile):
    return [tile] + [pltpu.roll(tile, 128 - c * STATE, 1) for c in range(1, STATE)]


def closed(parts):
    lane = lax.broadcasted_iota(jnp.int32, (ARCS, 128), 1)
    parts = [jnp.where(lane < STATE, part, 0.0) for part in parts]
    out = parts[0]
    for c in range(1, STATE):
        out = out + pltpu.roll(parts[c], c * STATE, 1)
    return out


def offsets_kernel(d_ref, f_ref, o_ref):
    forced = lambda j, z: split(f_ref[j, :, z * 128 : (z + 1) * 128].astype(jnp.float32))
    whole = opened(d_ref[0])
    for j in range(1, d_ref.shape[0]):
        coefficient = coefficients(d_ref[j])
        for z in range(Z):
            parts = forced(0, z) if j == 1 else split(o_ref[z, :S, :])
            parts = moved(coefficient, parts)
            o_ref[z, :S, :] = jnp.concatenate([u + v for u, v in zip(parts, forced(j, z))], 0)
        whole = moved(coefficient, whole)
    whole = closed(whole)
    for z in range(Z):
        o_ref[z, S:, :] = whole


def totals_kernel(r_ref, o_ref):
    total = split(r_ref[0, :S, :])
    whole = opened(r_ref[0, S:, :])
    for z in range(1, Z):
        coefficient = coefficients(r_ref[z, S:, :])
        total = [u + v for u, v in zip(moved(coefficient, total), split(r_ref[z, :S, :]))]
        whole = moved(coefficient, whole)
    o_ref[:S, :] = jnp.concatenate(total, 0)
    o_ref[S:, :] = closed(whole)


def incoming_kernel(at_ref, t1, t2, t3, r_ref, i_ref, o_ref):
    x = at_ref[0]
    carry = split(i_ref[:, pl.ds(pl.multiple_of(at_ref[1] * 128, 128), 128)])
    for s, ref in ((3, t3), (2, t2), (1, t1)):
        after = moved(coefficients(ref[S:, :]), carry)
        carry = [jnp.where(s <= x, u + v, w) for u, v, w in zip(after, split(ref[:S, :]), carry)]
    for z in range(Z):
        o_ref[z] = jnp.concatenate(carry, 0)
        if z < Z - 1:
            after = moved(coefficients(r_ref[z, S:, :]), carry)
            carry = [u + v for u, v in zip(after, split(r_ref[z, :S, :]))]


def design_kernel(n_ref, i_ref, d_ref, f_ref, p_ref, a_ref, o_ref, h_ref, c_ref):
    blocks = d_ref.shape[0]
    rows = p_ref.shape[1]
    length = rows // blocks
    lane = lax.broadcasted_iota(jnp.int32, (ARCS, rows), 1)
    arc = lax.broadcasted_iota(jnp.int32, (ARCS, rows), 0)
    chosen = arc == a_ref[...]
    weights = []
    for j in range(blocks):
        live = (lane >= j * length) & (lane < j * length + jnp.minimum(n_ref[j], length)) & chosen
        for c in range(STATE):
            weights.append(jnp.where(live, p_ref[c : c + 1, :], 0.0))
    weights = jnp.concatenate(weights, 0)
    for j in range(blocks):
        coefficient = coefficients(d_ref[j])
        for z in range(Z):
            at = slice(z * 128, (z + 1) * 128)
            before = i_ref[z] if j == 0 else c_ref[(j - 1) * S : j * S, at]
            parts = zip(moved(coefficient, split(before)), split(f_ref[j, :, at].astype(jnp.float32)))
            c_ref[j * S : (j + 1) * S, at] = jnp.concatenate([u + v for u, v in parts], 0)
    out = dot(weights, c_ref[...], 0, 0)
    o_ref[...] = out
    h_ref[...] = out[:, :PANEL]


def first_factor_kernel(at_ref, g_ref, m_ref, x_ref, z_ref):
    n = z_ref.shape[0]
    half = n // C
    for c in range(C):
        source = m_ref if c else g_ref
        row = pl.multiple_of(lax.rem(at_ref[3] + c, C) * half, half)
        for u in range(Y):
            column = pl.multiple_of(lax.rem(at_ref[2] + Y - u, Y) * 128, 128)
            z_ref[pl.ds(row, half), pl.ds(column, 128)] = source[u]
    factor_blocks(0, 2, x_ref, z_ref)


def second_factor_kernel(z_in, x_in, x_ref, z_ref):
    z_ref[...] = z_in[...]
    x_ref[: PANEL // 2] = x_in[...]
    factor_blocks(2, 4, x_ref, z_ref)


def factor_blocks(first_block, end_block, x_ref, z_ref):
    n = z_ref.shape[0]
    sub = lax.broadcasted_iota(jnp.int32, (8, 128), 0)
    lane = lax.broadcasted_iota(jnp.int32, (8, 128), 1)
    row_n = lax.broadcasted_iota(jnp.int32, (n, 128), 0)
    col_n = lax.broadcasted_iota(jnp.int32, (n, n), 1)
    row_nn = lax.broadcasted_iota(jnp.int32, (n, n), 0)
    col_b = lax.broadcasted_iota(jnp.int32, (128, n), 1)
    i128 = lax.broadcasted_iota(jnp.int32, (128, 128), 0)
    j128 = lax.broadcasted_iota(jnp.int32, (128, 128), 1)
    wide = lambda v: jnp.broadcast_to(v, (1, 128))
    tile = lambda v: jnp.broadcast_to(v, (8, 128))

    def block(k, _):
        at = pl.multiple_of(k * 128, 128)
        part = [z_ref[pl.ds(at + 8 * g, 8), pl.ds(at, 128)] for g in range(16)]
        for q in range(0, 128, 2):
            gq, sq = q // 8, q % 8
            first, second = part[gq][sq : sq + 1, :], part[gq][sq + 1 : sq + 2, :]
            a, b, c = wide(first[:, q : q + 1]), wide(second[:, q : q + 1]), wide(second[:, q + 1 : q + 2])
            inverse = 1.0 / (a * c - b * b)
            l1 = lane[:1]
            one = jnp.where(l1 == q, c, jnp.where(l1 == q + 1, -b, c * first - b * second)) * inverse
            two = jnp.where(l1 == q, -b, jnp.where(l1 == q + 1, a, a * second - b * first)) * inverse
            one, two = tile(one), tile(two)
            pair = (lane == q) | (lane == q + 1)
            for g in range(gq, 16):
                if g == gq and sq == 6:
                    continue
                left, right = tile(part[g][:, q : q + 1]), tile(part[g][:, q + 1 : q + 2])
                if g == gq:
                    below = sub > sq + 1
                    left, right = jnp.where(below, left, 0.0), jnp.where(below, right, 0.0)
                    kept = jnp.where(pair & below, 0.0, part[g])
                else:
                    kept = jnp.where(pair, 0.0, part[g])
                part[g] = (kept - left * one) - right * two
        done = jnp.concatenate(part, 0)
        odd = lax.rem(i128, 2) == 1
        diag = jnp.sum(jnp.where(i128 == j128, done, 0.0), axis=1, keepdims=True)
        beside = jnp.sum(jnp.where((j128 == i128 - 1) & odd, done, 0.0), axis=1, keepdims=True)
        unit = jnp.where(i128 == j128, 1.0, jnp.where(j128 < i128 - jnp.where(odd, 1, 0), done, 0.0))
        above = pltpu.roll(unit, 1, 0)
        ratio = jnp.where(odd[:, :1], beside / pltpu.roll(diag, 1, 0), 0.0)
        unit = unit - ratio * above
        pivots = diag - ratio * beside
        scale = lax.rsqrt(pivots)
        scale = scale * (1.5 - 0.5 * pivots * scale * scale)
        own = unit * scale
        across = dot(own, z_ref[pl.ds(at, 128), :])
        left = jnp.concatenate([own] * (n // 128), 1)
        inside = (col_b >= at) & (col_b < at + 128)
        across = jnp.where(inside, left, across)
        x_ref[pl.ds(at, 128), :] = jnp.where(col_b < at + 128, across, 0.0)
        down = z_ref[:, pl.ds(at, 128)]
        down = dot(jnp.where(row_n >= at + 128, down, 0.0), own, 1, 1)
        z = z_ref[...]
        z = jnp.where((col_n >= at) & (col_n < at + 128) & (row_nn >= at + 128), 0.0, z)
        z_ref[...] = z - dot(down, across)
        return 0

    lax.fori_loop(first_block, end_block, block, 0)


def factor_start(at, gram, mate):
    n = PANEL
    return pl.pallas_call(
        first_factor_kernel,
        out_shape=[jax.ShapeDtypeStruct((n // 2, n), jnp.float32), jax.ShapeDtypeStruct((n, n), jnp.float32)],
        in_specs=[SMEM, VMEM, VMEM],
        out_specs=[VMEM, VMEM],
        cost_estimate=pl.CostEstimate(flops=2 * 10**10, bytes_accessed=n * n * 8, transcendentals=0),
    )(at, gram, mate)


def factor_end(z, x):
    n = PANEL
    return pl.pallas_call(
        second_factor_kernel,
        out_shape=jax.ShapeDtypeStruct((n, n), jnp.float32),
        in_specs=[VMEM, VMEM],
        out_specs=VMEM,
        scratch_shapes=[pltpu.VMEM((n, n), jnp.float32)],
        cost_estimate=pl.CostEstimate(flops=2 * 10**10, bytes_accessed=n * n * 8, transcendentals=0),
    )(z, x)


def final_kernel(at_ref, l_ref, p_ref, m_ref, a_ref, b0, b1, b2, b3, o_ref, r_ref, ga_ref, gb_ref):
    root = math.sqrt(X * Z * p_ref.shape[0])
    x, p = at_ref[0], at_ref[2] * C + at_ref[3]
    mid, width = ga_ref.shape[1], m_ref.shape[1]
    step = PANEL // X
    tile = step // Z
    inverse = l_ref[...]
    basis = dot(p_ref[...], inverse, 1, 1)
    for s, ref in enumerate((b0, b1, b2, b3)):
        row = pl.multiple_of(lax.rem(x + X - s, X) * step, step)
        gb_ref[pl.ds(row, step), :] = ref[...]
        for z in range(Z):
            ga_ref[pl.ds(pl.multiple_of(row + z * tile, tile), tile), :] = a_ref[z, s]
    for lo, hi, source in ((0, mid, ga_ref), (mid, width, gb_ref)):
        rows = dot(inverse, source[...])
        r_ref[:, lo:hi] = rows * (1.0 / root)
        updated = m_ref[:, lo:hi] - dot(basis, rows)
        cut = min(hi, PANEL) - lo
        if cut > 0:
            o_ref[:, lo : lo + cut] = jnp.where(p == 0, basis[:, lo : lo + cut] * root, updated[:, :cut])
            if lo + cut < hi:
                o_ref[:, lo + cut : hi] = updated[:, cut:]
        else:
            o_ref[:, lo:hi] = updated


def exchanged(blocks, axis):
    return lax.all_to_all(blocks, axis, 0, 0, tiled=False)


def everywhere(block, axis, size):
    return exchanged(jnp.broadcast_to(block[None], (size,) + block.shape), axis)


def shift(block, axis, size, by):
    return lax.ppermute(block, axis, [(i, (i + by) % size) for i in range(size)])


def collected(block, axis, size):
    return jnp.stack([block] + [shift(block, axis, size, k) for k in range(1, size)], 0)


def local(initial_carry, forcing, transition, partials, arc_of_row, counts):
    f32 = jnp.float32
    x, z = lax.axis_index("x"), lax.axis_index("z")
    p = lax.axis_index(("y", "core"))
    width = initial_carry.shape[1]
    rows = partials.shape[1]
    blocks = transition.shape[0]
    core, y = lax.axis_index("core"), lax.axis_index("y")
    at = jnp.stack([x, z, y, core])
    maps = transition.transpose(0, 3, 1, 2).reshape(blocks, ARCS, STATE * STATE)
    maps = jnp.pad(maps, ((0, 0), (0, 0), (0, 128 - STATE * STATE)))

    packed = call(offsets_kernel, jax.ShapeDtypeStruct((Z, PACK, 128), f32), 2, (10**7, 10**6))(maps, forcing)
    received = exchanged(packed, "z")
    total = call(totals_kernel, jax.ShapeDtypeStruct((PACK, 128), f32), 1, (10**6, 10**5))(received)
    totals = [shift(total, "x", X, k) for k in range(1, X)]
    incoming = call(incoming_kernel, jax.ShapeDtypeStruct((Z, S, 128), f32), 6, (10**6, 10**5), (0,))(
        at, *totals, received, initial_carry
    )
    incoming = exchanged(incoming, "z")
    matrix, panel = pl.pallas_call(
        design_kernel,
        out_shape=[jax.ShapeDtypeStruct((rows, width), f32), jax.ShapeDtypeStruct((rows, PANEL), f32)],
        in_specs=[SMEM] + [VMEM] * 5,
        out_specs=[VMEM, VMEM],
        scratch_shapes=[pltpu.VMEM((blocks * S, width), f32)],
        cost_estimate=pl.CostEstimate(flops=10**8, bytes_accessed=10**6, transcendentals=0),
    )(counts, incoming, maps, forcing, partials, arc_of_row[None, :])

    both = ("y", "core")
    right = lax.ppermute(panel, both, [(0, 2)])
    left = lax.ppermute(panel, both, [(0, 6)])
    panel = jnp.where(p == 2, right, jnp.where(p == 6, left, panel))
    far = lax.ppermute(panel, both, [(2, 4)])
    panel = jnp.where(p == 4, far, panel)
    other = lax.ppermute(panel, both, [(0, 1), (2, 3), (4, 5), (6, 7)])
    panel = jnp.where(lax.axis_index("core") == 1, other, panel)

    half, quarter, step = PANEL // C, PANEL // Y, PANEL // X
    tile, mid = step // Z, 3 * width // 8
    gram = dot(
        lax.dynamic_slice(panel, (0, core * half), (rows, half)),
        lax.dynamic_slice(panel, (0, y * quarter), (rows, quarter)),
        0, 0,
    )
    gram, panel = lax.optimization_barrier((gram, panel))
    gram = exchanged(gram.reshape(X * Z, half // X // Z, quarter), ("x", "z"))
    gram = gram.sum(0)
    turned = lax.dynamic_slice(jnp.concatenate([panel, panel], 1), (0, x * step), (rows, PANEL))
    far, near, last, own = [dot(turned[:, k * step : (k + 1) * step], matrix, 0, 0) for k in (2, 1, 3, 0)]
    right, left = shift(far[:, : width // 2], "x", X, 1), shift(far[:, width // 2 :], "x", X, -1)
    right = jnp.concatenate([near[:, : width // 2] + right, near[:, width // 2 :]], 1)
    left = jnp.concatenate([last[:, : width // 2], last[:, width // 2 :] + left], 1)
    products = own + shift(right, "x", X, 1) + shift(left, "x", X, -1)

    gram = everywhere(gram, ("x", "z"), X * Z).reshape(half, quarter)
    gram, products = lax.optimization_barrier((gram, products))
    gram = collected(gram, "y", Y)
    mate = lax.ppermute(gram, "core", [(0, 1), (1, 0)])

    products = exchanged(products.reshape(Z, tile, width), "z").sum(0)
    a, b = products[:, :mid], products[:, mid:]
    b = everywhere(b, "z", Z).reshape(step, width - mid)
    a = collected(a, "x", X)
    a = everywhere(a, "z", Z)
    b = [b] + [shift(b, "x", X, k) for k in range(1, X)]

    upper, rest = factor_start(at, gram, mate)
    inverse = factor_end(rest, upper)
    return pl.pallas_call(
        final_kernel,
        out_shape=[jax.ShapeDtypeStruct((rows, width), f32), jax.ShapeDtypeStruct((PANEL, width), f32)],
        in_specs=[SMEM] + [VMEM] * 8,
        out_specs=[VMEM, VMEM],
        scratch_shapes=[pltpu.VMEM((PANEL, mid), f32), pltpu.VMEM((PANEL, width - mid), f32)],
        cost_estimate=pl.CostEstimate(flops=4 * 10**9, bytes_accessed=6 * 10**6, transcendentals=0),
    )(at, inverse, panel, matrix, a, *b)


def solution(mesh):
    mesh = Mesh(mesh.devices.reshape(X, Z, Y, C), ("x", "z", "y", "core"))
    e, q = ("x", "z"), ("y", "core")
    return jax.shard_map(
        local,
        mesh=mesh,
        in_specs=(P(None, q), P(e, None, q), P(e, None, None, None), P(None, e), P(e), P(e)),
        out_specs=(P(e, q), P(None, q)),
        check_vma=False,
    )
```

profile of v0, /device:TPU:8, one launch (start us, length us, event | category | flops | bytes accessed | tf_op | source)
XLA Modules:
  0.0 204.3 jit_solution(4925568511339898946)
XLA Ops:
  0.6 1.0 copy.10
  2.2 2.1 %shard_map.77 = f32[8,56,128]{2,1,0:T(8,128)} custom-call(f32[4,8,128]{2,1,0:T(8,128)} %pad.4.d_ref, bf16[4,48,1024]{2,1,0:T(8,128)(2,1)} %f_ref.3), custom_call_target="tpu_custom_call" | custom-call | flops 10000000 | bytes 1000000 | tf_op jit(solution)/shard_map/pallas_call | solution.py:292
  4.3 8.5 %all-to-all-start = ((f32[8,56,128]{2,1,0:T(8,128)}), f32[8,56,128]{2,1,0:T(8,128)S(1)}, u32[]{:S(2)}, u32[]{:S(2)}) async-start(f32[8,56,128]{2,1,0:T(8,128)} %shard_map.77), calls=%async_computation | async-start | bytes 458752 | tf_op jit(solution)/shard_map/all_to_all | solution.py:265
  12.8 11.2 %all-to-all-done.r_ref = f32[8,56,128]{2,1,0:T(8,128)S(1)} async-done(((f32[8,56,128]{2,1,0:T(8,128)}), f32[8,56,128]{2,1,0:T(8,128)S(1)}, u32[]{:S(2)}, u32[]{:S(2)}) %all-to-all-start) | async-done | bytes 229408 | tf_op jit(solution)/shard_map/all_to_all | solution.py:265
  24.7 2.1 %shard_map.78 = f32[56,128]{1,0:T(8,128)} custom-call(f32[8,56,128]{2,1,0:T(8,128)} %copy-done.1), custom_call_target="tpu_custom_call" | custom-call | flops 1000000 | bytes 100000 | tf_op jit(solution)/shard_map/pallas_call | solution.py:294
  26.8 2.8 %collective-permute-start.2 = (f32[56,128]{1,0:T(8,128)}, f32[56,128]{1,0:T(8,128)S(1)}, u32[]{:S(2)}, u32[]{:S(2)}) collective-permute-start(f32[56,128]{1,0:T(8,128)} %shard_map.78), channel_id=1, source_target_pairs={{0,192},{64,0},{128,64},{192,128},{1,193},{65,1},{129,65},{193,129... | collective-permute-start | bytes 86024 | tf_op jit(solution)/shard_map/ppermute | solution.py:273
  29.6 0.8 collective-permute-start.1
  30.4 0.9 collective-permute-start
  31.8 3.3 %collective-permute-done.1.t2 = f32[56,128]{1,0:T(8,128)S(1)} collective-permute-done((f32[56,128]{1,0:T(8,128)}, f32[56,128]{1,0:T(8,128)S(1)}, u32[]{:S(2)}, u32[]{:S(2)}) %collective-permute-start.1) | collective-permute-done | bytes 28704 | tf_op jit(solution)/shard_map/ppermute | solution.py:273
  36.3 2.5 %shard_map.79 = f32[8,48,128]{2,1,0:T(8,128)} custom-call(s32[4]{0:T(128)} %pad_add_fusion.at_ref, f32[56,128]{1,0:T(8,128)} %copy-done.8, f32[56,128]{1,0:T(8,128)} %copy-done.7, f32[56,128]{1,0:T(8,128)} %copy-done.6, f32[8,56,128]{2,1,0:T(8,128)} %copy-done.1, f32[48,1024]{1,0:T(8,128)} %i_ref.1), custom_call_target="tpu_custom_call" | custom-call | flops 1000000 | bytes 100000 | tf_op jit(solution)/shard_map/pallas_call | solution.py:296
  38.8 13.8 %all_to_all.35.i_ref = f32[8,48,128]{2,1,0:T(8,128)} all-to-all(f32[8,48,128]{2,1,0:T(8,128)} %shard_map.79), channel_id=1, replica_groups=mesh['x'=4,'z'=8,'y'=4,'core'=2] {'z'}, dimensions={0} | all-to-all | bytes 393216 | tf_op jit(solution)/shard_map/all_to_all | solution.py:265
  52.6 3.0 %shard_map.80 = (f32[128,1024]{1,0:T(8,128)}, f32[128,512]{1,0:T(8,128)}) custom-call(s32[4]{0:T(128)} %n_ref.1, f32[8,48,128]{2,1,0:T(8,128)} %all_to_all.35.i_ref, f32[4,8,128]{2,1,0:T(8,128)} %pad.4.d_ref, bf16[4,48,1024]{2,1,0:T(8,128)(2,1)} %f_ref.3, f32[6,128]{1,0:T(8,128)} %p_ref.1, s32[1,128]{1,0:T(1,128)} %bitcast.41), custom_call_target="tpu_custom_call" | custom-call | flops 100000000 | bytes 1000000 | tf_op jit(solution)/shard_map/pallas_call | solution.py:300
  55.6 0.8 collective-permute-start.4
  56.4 1.3 collective-permute-start.3
  57.7 9.2 %collective-permute-done.3 = f32[128,512]{1,0:T(8,128)S(1)} collective-permute-done((f32[128,512]{1,0:T(8,128)}, f32[128,512]{1,0:T(8,128)S(1)}, u32[]{:S(2)}, u32[]{:S(2)}) %collective-permute-start.3) | collective-permute-done | bytes 262176 | tf_op jit(solution)/shard_map/ppermute | solution.py:310
  66.9 1.0 select_select_fusion
  67.9 1.3 collective-permute-start.5
  69.3 3.9 %collective-permute-done.5 = f32[128,512]{1,0:T(8,128)S(1)} collective-permute-done((f32[128,512]{1,0:T(8,128)S(1)}, f32[128,512]{1,0:T(8,128)S(1)}, u32[]{:S(2)}, u32[]{:S(2)}) %collective-permute-start.5) | collective-permute-done | bytes 262176 | tf_op jit(solution)/shard_map/ppermute | solution.py:313
  73.1 1.3 collective-permute-start.6
  74.5 1.1 collective-permute-done.6
  76.8 0.9 collective-permute-start.9
  78.3 1.3 collective-permute-start.7
  80.3 5.2 %collective-permute-done.9 = f32[128,512]{1,0:T(8,128)S(1)} collective-permute-done((f32[128,512]{1,0:T(8,128)S(1)}, f32[128,512]{1,0:T(8,128)S(1)}, u32[]{:S(2)}, u32[]{:S(2)}) %collective-permute-start.9) | collective-permute-done | bytes 262176 | tf_op jit(solution)/shard_map/ppermute | solution.py:273
  85.6 2.1 %collective-permute-start.10 = (f32[128,1024]{1,0:T(8,128)S(1)}, f32[128,1024]{1,0:T(8,128)S(1)}, u32[]{:S(2)}, u32[]{:S(2)}) collective-permute-start(f32[128,1024]{1,0:T(8,128)S(1)} %pad_maximum_fusion.1), channel_id=1, source_target_pairs={{0,192},{64,0},{128,64},{192,128},{1,193},{65,1},{129,65},{193,129... | collective-permute-start | bytes 1572872 | tf_op jit(solution)/shard_map/ppermute | solution.py:273
  88.1 15.7 %all_to_all.36 = f32[32,8,128]{2,1,0:T(8,128)S(1)} all-to-all(f32[32,8,128]{2,1,0:T(8,128)S(1)} %bitcast.25), channel_id=1, replica_groups=mesh['x'=4,'z'=8,'y'=4,'core'=2] {'x','z'}, dimensions={0} | all-to-all | bytes 262144 | tf_op jit(solution)/shard_map/all_to_all | solution.py:265
  104.5 4.0 %all-to-all-start.3 = ((f32[32,8,128]{2,1,0:T(8,128)}), f32[32,8,128]{2,1,0:T(8,128)S(1)}, u32[]{:S(2)}, u32[]{:S(2)}) async-start(f32[32,8,128]{2,1,0:T(8,128)} %broadcast_in_dim.9), calls=%async_computation.3 | async-start | bytes 262144 | tf_op jit(solution)/shard_map/all_to_all | solution.py:265
  108.6 1.4 fusion
  110.0 8.8 %all-to-all-done.3 = f32[32,8,128]{2,1,0:T(8,128)S(1)} async-done(((f32[32,8,128]{2,1,0:T(8,128)}), f32[32,8,128]{2,1,0:T(8,128)S(1)}, u32[]{:S(2)}, u32[]{:S(2)}) %all-to-all-start.3) | async-done | bytes 131104 | tf_op jit(solution)/shard_map/all_to_all | solution.py:265
  118.8 3.5 %all-to-all-start.4 = ((f32[8,16,1024]{2,1,0:T(8,128)}), f32[8,16,1024]{2,1,0:T(8,128)S(1)}, u32[]{:S(2)}, u32[]{:S(2)}) async-start(f32[8,16,1024]{2,1,0:T(8,128)} %bitcast.13), calls=%async_computation.4 | async-start | bytes 1048576 | tf_op jit(solution)/shard_map/all_to_all | solution.py:265
  122.4 3.9 %collective-permute-start.12 = (f32[256,128]{1,0:T(8,128)S(1)}, f32[256,128]{1,0:T(8,128)S(1)}, u32[]{:S(2)}, u32[]{:S(2)}) collective-permute-start(f32[256,128]{1,0:T(8,128)S(1)} %bitcast.27), channel_id=1, source_target_pairs={{0,4},{2,6},{4,0},{6,2},{1,5},{3,7},{5,1},{7,3},{8,12},{10,14},{12... | collective-permute-start | bytes 393224 | tf_op jit(solution)/shard_map/ppermute | solution.py:273
  126.3 1.7 collective-permute-done.13
  128.0 2.6 %collective-permute-done.12 = f32[256,128]{1,0:T(8,128)S(1)} collective-permute-done((f32[256,128]{1,0:T(8,128)S(1)}, f32[256,128]{1,0:T(8,128)S(1)}, u32[]{:S(2)}, u32[]{:S(2)}) %collective-permute-start.12) | collective-permute-done | bytes 131104 | tf_op jit(solution)/shard_map/ppermute | solution.py:273
  130.6 0.8 collective-permute-done.11
  131.6 5.5 %all-to-all-done.4 = f32[8,16,1024]{2,1,0:T(8,128)S(1)} async-done(((f32[8,16,1024]{2,1,0:T(8,128)}), f32[8,16,1024]{2,1,0:T(8,128)S(1)}, u32[]{:S(2)}, u32[]{:S(2)}) %all-to-all-start.4) | async-done | bytes 524320 | tf_op jit(solution)/shard_map/all_to_all | solution.py:265
  137.1 1.5 collective-permute-start.16
  139.2 2.7 %collective-permute-start.17 = (f32[16,384]{1,0:T(8,128)S(1)}, f32[16,384]{1,0:T(8,128)S(1)}, u32[]{:S(2)}, u32[]{:S(2)}) collective-permute-start(f32[16,384]{1,0:T(8,128)S(1)} %get-tuple-element.25), channel_id=1, source_target_pairs={{0,192},{64,0},{128,64},{192,128},{1,193},{65,1},{129,65},{193,129... | collective-permute-start | bytes 73736 | tf_op jit(solution)/shard_map/ppermute | solution.py:273
  141.9 0.7 broadcast_in_dim.11
  142.6 3.4 %all-to-all-start.6 = ((f32[8,16,640]{2,1,0:T(8,128)}), f32[8,16,640]{2,1,0:T(8,128)S(1)}, u32[]{:S(2)}, u32[]{:S(2)}) async-start(f32[8,16,640]{2,1,0:T(8,128)} %broadcast_in_dim.11), calls=%async_computation.6 | async-start | bytes 655360 | tf_op jit(solution)/shard_map/all_to_all | solution.py:265
  146.1 0.8 copy-done.9
  146.9 17.8 %shard_map.81 = (f32[256,512]{1,0:T(8,128)}, f32[512,512]{1,0:T(8,128)}) custom-call(s32[4]{0:T(128)} %pad_add_fusion.at_ref, f32[4,256,128]{2,1,0:T(8,128)} %copy-done.4, f32[4,256,128]{2,1,0:T(8,128)} %copy-done.9), custom_call_target="tpu_custom_call" | custom-call | flops 20000000000 | bytes 2097152 | tf_op jit(solution)/shard_map/pallas_call | solution.py:217
  164.7 1.0 broadcast_in_dim.10
  165.7 7.1 %all-to-all-start.5 = ((f32[8,4,16,384]{3,2,1,0:T(8,128)}), f32[8,4,16,384]{3,2,1,0:T(8,128)S(1)}, u32[]{:S(2)}, u32[]{:S(2)}) async-start(f32[8,4,16,384]{3,2,1,0:T(8,128)} %broadcast_in_dim.10), calls=%async_computation.5 | async-start | bytes 1572864 | tf_op jit(solution)/shard_map/all_to_all | solution.py:265
  173.5 0.7 collective-permute-start.19
  174.2 0.9 collective-permute-start.18
  175.2 16.9 %shard_map.82.l_ref = f32[512,512]{1,0:T(8,128)} custom-call(f32[512,512]{1,0:T(8,128)} %get-tuple-element.15.z_in, f32[256,512]{1,0:T(8,128)} %get-tuple-element.16.x_in), custom_call_target="tpu_custom_call" | custom-call | flops 20000000000 | bytes 2097152 | tf_op jit(solution)/shard_map/pallas_call | solution.py:228
  192.1 1.1 all-to-all-done.5.a_ref
  193.3 0.9 copy-done.3
  194.2 10.1 %shard_map.83 = (f32[128,1024]{1,0:T(8,128)}, f32[512,1024]{1,0:T(8,128)}) custom-call(s32[4]{0:T(128)} %pad_add_fusion.at_ref, f32[512,512]{1,0:T(8,128)} %shard_map.82.l_ref, f32[128,512]{1,0:T(8,128)} %copy-done.2, f32[128,1024]{1,0:T(8,128)} %get-tuple-element.13.m_ref, f32[8,4,16,384]{3,2,1,0:T(8,128)} %copy-done.3, f32[128,640]{1,0:T(8,128)} %bitcast.33, ...), custom_call_target="tpu_custom_call" | custom-call | flops 4000000000 | bytes 6000000 | tf_op jit(solution)/shard_map/pallas_call | solution.py:349
  (65 shorter events, 8.3 us)
Async XLA Ops:
  4.3 19.6 %all-to-all-start = ((f32[8,56,128]{2,1,0:T(8,128)}), f32[8,56,128]{2,1,0:T(8,128)S(1)}, u32[]{:S(2)}, u32[]{:S(2)}) async-start(f32[8,56,128]{2,1,0:T(8,128)} %shard_map.77), calls=%async_computation | async-start | bytes 458752 | tf_op jit(solution)/shard_map/all_to_all | solution.py:265
  24.0 0.7 copy-start.1
  26.8 5.0 %collective-permute-start.2 = (f32[56,128]{1,0:T(8,128)}, f32[56,128]{1,0:T(8,128)S(1)}, u32[]{:S(2)}, u32[]{:S(2)}) collective-permute-start(f32[56,128]{1,0:T(8,128)} %shard_map.78), channel_id=1, source_target_pairs={{0,192},{64,0},{128,64},{192,128},{1,193},{65,1},{129,65},{193,129... | collective-permute-start | bytes 86024 | tf_op jit(solution)/shard_map/ppermute | solution.py:273
  29.6 5.6 %collective-permute-start.1 = (f32[56,128]{1,0:T(8,128)}, f32[56,128]{1,0:T(8,128)S(1)}, u32[]{:S(2)}, u32[]{:S(2)}) collective-permute-start(f32[56,128]{1,0:T(8,128)} %shard_map.78), channel_id=1, source_target_pairs={{0,128},{64,192},{128,0},{192,64},{1,129},{65,193},{129,1},{193,65... | collective-permute-start | bytes 86024 | tf_op jit(solution)/shard_map/ppermute | solution.py:273
  30.4 5.3 %collective-permute-start = (f32[56,128]{1,0:T(8,128)}, f32[56,128]{1,0:T(8,128)S(1)}, u32[]{:S(2)}, u32[]{:S(2)}) collective-permute-start(f32[56,128]{1,0:T(8,128)} %shard_map.78), channel_id=1, source_target_pairs={{0,64},{64,128},{128,192},{192,0},{1,65},{65,129},{129,193},{193,1... | collective-permute-start | bytes 86024 | tf_op jit(solution)/shard_map/ppermute | solution.py:273
  31.8 3.8 %copy-start.6 = (f32[56,128]{1,0:T(8,128)}, f32[56,128]{1,0:T(8,128)S(1)}, u32[]{:S(2)}) copy-start(f32[56,128]{1,0:T(8,128)S(1)} %collective-permute-done.2.t3) | copy-start | bytes 86020
  35.1 0.6 copy-start.7
  35.7 0.6 copy-start.8
  55.6 20.5 %copy-start = (f32[128,1024]{1,0:T(8,128)S(1)}, f32[128,1024]{1,0:T(8,128)}, u32[]{:S(2)}) copy-start(f32[128,1024]{1,0:T(8,128)} %get-tuple-element.13.m_ref) | copy-start | bytes 1572868
  55.6 2.1 %collective-permute-start.4 = (f32[128,512]{1,0:T(8,128)}, f32[128,512]{1,0:T(8,128)S(1)}, u32[]{:S(2)}, u32[]{:S(2)}) collective-permute-start(f32[128,512]{1,0:T(8,128)} %get-tuple-element.10), channel_id=1, source_target_pairs={{0,6},{8,14},{16,22},{24,30},{32,38},{40,46},{48,54},{56,62},{64,7... | collective-permute-start | bytes 786440 | tf_op jit(solution)/shard_map/ppermute | solution.py:311
  56.4 10.5 %collective-permute-start.3 = (f32[128,512]{1,0:T(8,128)}, f32[128,512]{1,0:T(8,128)S(1)}, u32[]{:S(2)}, u32[]{:S(2)}) collective-permute-start(f32[128,512]{1,0:T(8,128)} %get-tuple-element.10), channel_id=1, source_target_pairs={{0,2},{8,10},{16,18},{24,26},{32,34},{40,42},{48,50},{56,58},{64,6... | collective-permute-start | bytes 786440 | tf_op jit(solution)/shard_map/ppermute | solution.py:310
  67.9 5.2 %collective-permute-start.5 = (f32[128,512]{1,0:T(8,128)S(1)}, f32[128,512]{1,0:T(8,128)S(1)}, u32[]{:S(2)}, u32[]{:S(2)}) collective-permute-start(f32[128,512]{1,0:T(8,128)S(1)} %select_select_fusion), channel_id=1, source_target_pairs={{2,4},{10,12},{18,20},{26,28},{34,36},{42,44},{50,52},{58,60},{66,... | collective-permute-start | bytes 786440 | tf_op jit(solution)/shard_map/ppermute | solution.py:313
  73.1 2.4 %collective-permute-start.6 = (f32[128,512]{1,0:T(8,128)S(1)}, f32[128,512]{1,0:T(8,128)S(1)}, u32[]{:S(2)}, u32[]{:S(2)}) collective-permute-start(f32[128,512]{1,0:T(8,128)S(1)} %broadcast_select_fusion), channel_id=1, source_target_pairs={{0,1},{2,3},{4,5},{6,7},{8,9},{10,11},{12,13},{14,15},{16,17},{18,... | collective-permute-start | bytes 786440 | tf_op jit(solution)/shard_map/ppermute | solution.py:315
  75.6 4.6 %copy-start.2 = (f32[128,512]{1,0:T(8,128)}, f32[128,512]{1,0:T(8,128)S(1)}, u32[]{:S(2)}) copy-start(f32[128,512]{1,0:T(8,128)S(1)} %broadcast_select_fusion.1.p_ref) | copy-start | bytes 786436
  76.8 8.7 %collective-permute-start.9 = (f32[128,512]{1,0:T(8,128)S(1)}, f32[128,512]{1,0:T(8,128)S(1)}, u32[]{:S(2)}, u32[]{:S(2)}) collective-permute-start(f32[128,512]{1,0:T(8,128)S(1)} %get-tuple-element.21), channel_id=1, source_target_pairs={{0,192},{64,0},{128,64},{192,128},{1,193},{65,1},{129,65},{193,129... | collective-permute-start | bytes 786440 | tf_op jit(solution)/shard_map/ppermute | solution.py:273
  78.3 9.6 %collective-permute-start.7 = (f32[128,512]{1,0:T(8,128)S(1)}, f32[128,512]{1,0:T(8,128)S(1)}, u32[]{:S(2)}, u32[]{:S(2)}) collective-permute-start(f32[128,512]{1,0:T(8,128)S(1)} %get-tuple-element.20), channel_id=1, source_target_pairs={{0,64},{64,128},{128,192},{192,0},{1,65},{65,129},{129,193},{193,1... | collective-permute-start | bytes 786440 | tf_op jit(solution)/shard_map/ppermute | solution.py:273
  85.6 23.0 %collective-permute-start.10 = (f32[128,1024]{1,0:T(8,128)S(1)}, f32[128,1024]{1,0:T(8,128)S(1)}, u32[]{:S(2)}, u32[]{:S(2)}) collective-permute-start(f32[128,1024]{1,0:T(8,128)S(1)} %pad_maximum_fusion.1), channel_id=1, source_target_pairs={{0,192},{64,0},{128,64},{192,128},{1,193},{65,1},{129,65},{193,129... | collective-permute-start | bytes 1572872 | tf_op jit(solution)/shard_map/ppermute | solution.py:273
  88.0 20.5 %collective-permute-start.8 = (f32[128,1024]{1,0:T(8,128)S(1)}, f32[128,1024]{1,0:T(8,128)S(1)}, u32[]{:S(2)}, u32[]{:S(2)}) collective-permute-start(f32[128,1024]{1,0:T(8,128)S(1)} %pad_maximum_fusion), channel_id=1, source_target_pairs={{0,64},{64,128},{128,192},{192,0},{1,65},{65,129},{129,193},{193,1... | collective-permute-start | bytes 1572872 | tf_op jit(solution)/shard_map/ppermute | solution.py:273
  104.5 14.3 %all-to-all-start.3 = ((f32[32,8,128]{2,1,0:T(8,128)}), f32[32,8,128]{2,1,0:T(8,128)S(1)}, u32[]{:S(2)}, u32[]{:S(2)}) async-start(f32[32,8,128]{2,1,0:T(8,128)} %broadcast_in_dim.9), calls=%async_computation.3 | async-start | bytes 262144 | tf_op jit(solution)/shard_map/all_to_all | solution.py:265
  118.8 18.3 %all-to-all-start.4 = ((f32[8,16,1024]{2,1,0:T(8,128)}), f32[8,16,1024]{2,1,0:T(8,128)S(1)}, u32[]{:S(2)}, u32[]{:S(2)}) async-start(f32[8,16,1024]{2,1,0:T(8,128)} %bitcast.13), calls=%async_computation.4 | async-start | bytes 1048576 | tf_op jit(solution)/shard_map/all_to_all | solution.py:265
  122.3 5.8 %collective-permute-start.13 = (f32[256,128]{1,0:T(8,128)S(1)}, f32[256,128]{1,0:T(8,128)S(1)}, u32[]{:S(2)}, u32[]{:S(2)}) collective-permute-start(f32[256,128]{1,0:T(8,128)S(1)} %bitcast.26), channel_id=1, source_target_pairs={{0,6},{2,0},{4,2},{6,4},{1,7},{3,1},{5,3},{7,5},{8,14},{10,8},{12,... | collective-permute-start | bytes 393224 | tf_op jit(solution)/shard_map/ppermute | solution.py:273
  122.4 8.3 %collective-permute-start.12 = (f32[256,128]{1,0:T(8,128)S(1)}, f32[256,128]{1,0:T(8,128)S(1)}, u32[]{:S(2)}, u32[]{:S(2)}) collective-permute-start(f32[256,128]{1,0:T(8,128)S(1)} %bitcast.27), channel_id=1, source_target_pairs={{0,4},{2,6},{4,0},{6,2},{1,5},{3,7},{5,1},{7,3},{8,12},{10,14},{12... | collective-permute-start | bytes 393224 | tf_op jit(solution)/shard_map/ppermute | solution.py:273
  126.3 5.1 %collective-permute-start.11 = (f32[256,128]{1,0:T(8,128)S(1)}, f32[256,128]{1,0:T(8,128)S(1)}, u32[]{:S(2)}, u32[]{:S(2)}) collective-permute-start(f32[256,128]{1,0:T(8,128)S(1)} %bitcast.28), channel_id=1, source_target_pairs={{0,2},{2,4},{4,6},{6,0},{1,3},{3,5},{5,7},{7,1},{8,10},{10,12},{12... | collective-permute-start | bytes 393224 | tf_op jit(solution)/shard_map/ppermute | solution.py:273
  131.4 14.6 %copy-start.4 = (f32[4,256,128]{2,1,0:T(8,128)}, f32[4,256,128]{2,1,0:T(8,128)S(1)}, u32[]{:S(2)}) copy-start(f32[4,256,128]{2,1,0:T(8,128)S(1)} %pad_maximum_fusion.2.g_ref) | copy-start | bytes 1572868
  131.5 14.6 %collective-permute-start.14 = (f32[4,256,128]{2,1,0:T(8,128)S(1)}, f32[4,256,128]{2,1,0:T(8,128)S(1)}, u32[]{:S(2)}, u32[]{:S(2)}) collective-permute-start(f32[4,256,128]{2,1,0:T(8,128)S(1)} %pad_maximum_fusion.2.g_ref), channel_id=1, source_target_pairs={{0,1},{1,0},{2,3},{3,2},{4,5},{5,4},{6,7},{7,6},{8,9},{9,8},{10,11... | collective-permute-start | bytes 1572872 | tf_op jit(solution)/shard_map/ppermute | solution.py:338
  137.1 27.5 %collective-permute-start.16 = (f32[16,384]{1,0:T(8,128)S(1)}, f32[16,384]{1,0:T(8,128)S(1)}, u32[]{:S(2)}, u32[]{:S(2)}) collective-permute-start(f32[16,384]{1,0:T(8,128)S(1)} %get-tuple-element.25), channel_id=1, source_target_pairs={{0,128},{64,192},{128,0},{192,64},{1,129},{65,193},{129,1},{193,65... | collective-permute-start | bytes 73736 | tf_op jit(solution)/shard_map/ppermute | solution.py:273
  138.6 26.0 %collective-permute-start.15 = (f32[16,384]{1,0:T(8,128)S(1)}, f32[16,384]{1,0:T(8,128)S(1)}, u32[]{:S(2)}, u32[]{:S(2)}) collective-permute-start(f32[16,384]{1,0:T(8,128)S(1)} %get-tuple-element.25), channel_id=1, source_target_pairs={{0,64},{64,128},{128,192},{192,0},{1,65},{65,129},{129,193},{193,1... | collective-permute-start | bytes 73736 | tf_op jit(solution)/shard_map/ppermute | solution.py:273
  139.2 25.5 %collective-permute-start.17 = (f32[16,384]{1,0:T(8,128)S(1)}, f32[16,384]{1,0:T(8,128)S(1)}, u32[]{:S(2)}, u32[]{:S(2)}) collective-permute-start(f32[16,384]{1,0:T(8,128)S(1)} %get-tuple-element.25), channel_id=1, source_target_pairs={{0,192},{64,0},{128,64},{192,128},{1,193},{65,1},{129,65},{193,129... | collective-permute-start | bytes 73736 | tf_op jit(solution)/shard_map/ppermute | solution.py:273
  142.6 22.1 %all-to-all-start.6 = ((f32[8,16,640]{2,1,0:T(8,128)}), f32[8,16,640]{2,1,0:T(8,128)S(1)}, u32[]{:S(2)}, u32[]{:S(2)}) async-start(f32[8,16,640]{2,1,0:T(8,128)} %broadcast_in_dim.11), calls=%async_computation.6 | async-start | bytes 655360 | tf_op jit(solution)/shard_map/all_to_all | solution.py:265
  146.1 0.8 copy-start.9
  164.7 27.4 %copy-start.5 = (f32[8,16,640]{2,1,0:T(8,128)}, f32[8,16,640]{2,1,0:T(8,128)S(1)}, u32[]{:S(2)}) copy-start(f32[8,16,640]{2,1,0:T(8,128)S(1)} %all-to-all-done.6) | copy-start | bytes 983044
  165.7 27.6 %all-to-all-start.5 = ((f32[8,4,16,384]{3,2,1,0:T(8,128)}), f32[8,4,16,384]{3,2,1,0:T(8,128)S(1)}, u32[]{:S(2)}, u32[]{:S(2)}) async-start(f32[8,4,16,384]{3,2,1,0:T(8,128)} %broadcast_in_dim.10), calls=%async_computation.5 | async-start | bytes 1572864 | tf_op jit(solution)/shard_map/all_to_all | solution.py:265
  172.8 19.3 %collective-permute-start.20 = (f32[128,640]{1,0:T(8,128)S(1)}, f32[128,640]{1,0:T(8,128)S(1)}, u32[]{:S(2)}, u32[]{:S(2)}) collective-permute-start(f32[128,640]{1,0:T(8,128)S(1)} %bitcast.30), channel_id=1, source_target_pairs={{0,192},{64,0},{128,64},{192,128},{1,193},{65,1},{129,65},{193,129... | collective-permute-start | bytes 983048 | tf_op jit(solution)/shard_map/ppermute | solution.py:273
  173.5 18.6 %collective-permute-start.19 = (f32[128,640]{1,0:T(8,128)S(1)}, f32[128,640]{1,0:T(8,128)S(1)}, u32[]{:S(2)}, u32[]{:S(2)}) collective-permute-start(f32[128,640]{1,0:T(8,128)S(1)} %bitcast.31), channel_id=1, source_target_pairs={{0,128},{64,192},{128,0},{192,64},{1,129},{65,193},{129,1},{193,65... | collective-permute-start | bytes 983048 | tf_op jit(solution)/shard_map/ppermute | solution.py:273
  174.2 17.9 %collective-permute-start.18 = (f32[128,640]{1,0:T(8,128)S(1)}, f32[128,640]{1,0:T(8,128)S(1)}, u32[]{:S(2)}, u32[]{:S(2)}) collective-permute-start(f32[128,640]{1,0:T(8,128)S(1)} %bitcast.32), channel_id=1, source_target_pairs={{0,64},{64,128},{128,192},{192,0},{1,65},{65,129},{129,193},{193,1... | collective-permute-start | bytes 983048 | tf_op jit(solution)/shard_map/ppermute | solution.py:273
  192.1 1.2 copy-start.10
  192.1 1.2 copy-start.11
  192.1 1.1 copy-start.12
  193.3 0.9 copy-start.3
where the time goes:
time: 208 us; the launch traced here: 204 us
  waiting for transfers between devices  55.2 us (27%)
  Pallas kernels  54.5 us (26%)
  starting transfers between devices  51.3 us (25%)
  blocking collectives  29.4 us (14%)
  local copies, waits for them, and re-layouts  7.11 us (3%)
  matrix products  3.71 us (2%)
    all_to_all x2, blocking collectives, exchanged(): return lax.all_to_all(blocks, axis, 0, 0, tiled=False)  29.4 us
    all_to_all x5, waiting for transfers between devices, exchanged(): return lax.all_to_all(blocks, axis, 0, 0, tiled=False)  26.6 us
    all_to_all x5, starting transfers between devices, exchanged(): return lax.all_to_all(blocks, axis, 0, 0, tiled=False)  26.5 us
    ppermute x16, starting transfers between devices, shift(): lax.ppermute(block, axis, [(i, (i + by) % size) for i in range(size)])  19.9 us
    pallas_call x1, Pallas kernels, factor_start(): pl.pallas_call(first_factor_kernel, out_shape=[jax.ShapeDtypeStruct((n //...  17.8 us
    pallas_call x1, Pallas kernels, factor_end(): pl.pallas_call(second_factor_kernel, out_shape=jax.ShapeDtypeStruct((n, n...  16.9 us
    ppermute x16, waiting for transfers between devices, shift(): lax.ppermute(block, axis, [(i, (i + by) % size) for i in range(size)])  14.4 us
    pallas_call x1, Pallas kernels, local(): pl.pallas_call(final_kernel, out_shape=[jax.ShapeDtypeStruct((rows, width...  10.1 us
  transfers between devices with their start and end apart: 26, of which 14 were waited for; matrix products, arithmetic and copies ran while one was open for 2% of the time, Pallas kernels for 17%

commit v1 on v0

v1 whole, which is shorter than its diff:
```python
import math

import jax
import jax.numpy as jnp
from jax import lax
from jax.experimental import pallas as pl
from jax.experimental.pallas import tpu as pltpu
from jax.sharding import Mesh
from jax.sharding import PartitionSpec as P


PANEL = 512
X, Z, Y, C = 4, 8, 4, 2
STATE, ARCS = 6, 8
S = STATE * ARCS
PACK = S + 8
LIMIT = 12 * 2**20
HI = lax.Precision.HIGHEST
VMEM = pl.BlockSpec(memory_space=pltpu.VMEM)
SMEM = pl.BlockSpec(memory_space=pltpu.SMEM)


def call(kernel, out, n, cost, smem=()):
    flops, size = cost
    return pl.pallas_call(
        kernel,
        out_shape=out,
        in_specs=[SMEM if i in smem else VMEM for i in range(n)],
        out_specs=VMEM if not isinstance(out, (tuple, list)) else [VMEM] * len(out),
        compiler_params=pltpu.CompilerParams(vmem_limit_bytes=LIMIT),
        cost_estimate=pl.CostEstimate(flops=flops, bytes_accessed=size, transcendentals=0),
    )


def dot(a, b, ca=1, cb=0):
    return lax.dot_general(a, b, (((ca,), (cb,)), ((), ())), precision=HI, preferred_element_type=jnp.float32)


def coefficients(tile):
    spread = lambda k: jnp.broadcast_to(tile[:, k : k + 1], (ARCS, 128))
    return [[spread(c * STATE + d) for d in range(STATE)] for c in range(STATE)]


def moved(coefficient, parts):
    out = []
    for row in coefficient:
        total = row[0] * parts[0]
        for d in range(1, STATE):
            total = total + row[d] * parts[d]
        out.append(total)
    return out


def split(value):
    return [value[c * ARCS : (c + 1) * ARCS] for c in range(STATE)]


def opened(tile):
    return [tile] + [pltpu.roll(tile, 128 - c * STATE, 1) for c in range(1, STATE)]


def closed(parts):
    lane = lax.broadcasted_iota(jnp.int32, (ARCS, 128), 1)
    parts = [jnp.where(lane < STATE, part, 0.0) for part in parts]
    out = parts[0]
    for c in range(1, STATE):
        out = out + pltpu.roll(parts[c], c * STATE, 1)
    return out


def offsets_kernel(d_ref, f_ref, o_ref):
    forced = lambda j, z: split(f_ref[j, :, z * 128 : (z + 1) * 128].astype(jnp.float32))
    whole = opened(d_ref[0])
    for j in range(1, d_ref.shape[0]):
        coefficient = coefficients(d_ref[j])
        for z in range(Z):
            parts = forced(0, z) if j == 1 else split(o_ref[z, :S, :])
            parts = moved(coefficient, parts)
            o_ref[z, :S, :] = jnp.concatenate([u + v for u, v in zip(parts, forced(j, z))], 0)
        whole = moved(coefficient, whole)
    whole = closed(whole)
    for z in range(Z):
        o_ref[z, S:, :] = whole


def totals_kernel(r_ref, o_ref):
    total = split(r_ref[0, :S, :])
    whole = opened(r_ref[0, S:, :])
    for z in range(1, Z):
        coefficient = coefficients(r_ref[z, S:, :])
        total = [u + v for u, v in zip(moved(coefficient, total), split(r_ref[z, :S, :]))]
        whole = moved(coefficient, whole)
    o_ref[:S, :] = jnp.concatenate(total, 0)
    o_ref[S:, :] = closed(whole)


def incoming_kernel(at_ref, t1, t2, t3, r_ref, i_ref, o_ref):
    x = at_ref[0]
    carry = split(i_ref[:, pl.ds(pl.multiple_of(at_ref[1] * 128, 128), 128)])
    for s, ref in ((3, t3), (2, t2), (1, t1)):
        after = moved(coefficients(ref[S:, :]), carry)
        carry = [jnp.where(s <= x, u + v, w) for u, v, w in zip(after, split(ref[:S, :]), carry)]
    for z in range(Z):
        o_ref[z] = jnp.concatenate(carry, 0)
        if z < Z - 1:
            after = moved(coefficients(r_ref[z, S:, :]), carry)
            carry = [u + v for u, v in zip(after, split(r_ref[z, :S, :]))]


def design_kernel(n_ref, i_ref, d_ref, f_ref, p_ref, a_ref, o_ref, h_ref, c_ref):
    blocks = d_ref.shape[0]
    rows = p_ref.shape[1]
    length = rows // blocks
    lane = lax.broadcasted_iota(jnp.int32, (ARCS, rows), 1)
    arc = lax.broadcasted_iota(jnp.int32, (ARCS, rows), 0)
    chosen = arc == a_ref[...]
    weights = []
    for j in range(blocks):
        live = (lane >= j * length) & (lane < j * length + jnp.minimum(n_ref[j], length)) & chosen
        for c in range(STATE):
            weights.append(jnp.where(live, p_ref[c : c + 1, :], 0.0))
    weights = jnp.concatenate(weights, 0)
    for j in range(blocks):
        coefficient = coefficients(d_ref[j])
        for z in range(Z):
            at = slice(z * 128, (z + 1) * 128)
            before = i_ref[z] if j == 0 else c_ref[(j - 1) * S : j * S, at]
            parts = zip(moved(coefficient, split(before)), split(f_ref[j, :, at].astype(jnp.float32)))
            c_ref[j * S : (j + 1) * S, at] = jnp.concatenate([u + v for u, v in parts], 0)
    out = dot(weights, c_ref[...], 0, 0)
    o_ref[...] = out
    h_ref[...] = out[:, :PANEL]


def first_factor_kernel(at_ref, g_ref, m_ref, x_ref, o_ref, z_ref):
    n = z_ref.shape[0]
    half = n // C
    for c in range(C):
        source = m_ref if c else g_ref
        row = pl.multiple_of(lax.rem(at_ref[3] + c, C) * half, half)
        for u in range(Y):
            column = pl.multiple_of(lax.rem(at_ref[2] + Y - u, Y) * 128, 128)
            z_ref[pl.ds(row, half), pl.ds(column, 128)] = source[u]
    factor_block(0, x_ref, z_ref, 0, o_ref)


def second_factor_kernel(z_ref, x_ref, o_ref):
    factor_block(1, x_ref, z_ref, 128, o_ref)


def last_factor_kernel(z_ref, x_ref, y_ref, o_ref):
    factor_block(2, x_ref, z_ref, 256, o_ref)
    factor_block(3, y_ref, o_ref, 384, None)


def factor_block(k, x_ref, z_ref, top, o_ref):
    lo, hi = k * 128, k * 128 + 128
    sub = lax.broadcasted_iota(jnp.int32, (8, 128), 0)
    lane = lax.broadcasted_iota(jnp.int32, (8, 128), 1)
    i128 = lax.broadcasted_iota(jnp.int32, (128, 128), 0)
    j128 = lax.broadcasted_iota(jnp.int32, (128, 128), 1)
    wide = lambda v: jnp.broadcast_to(v, (1, 128))
    tile = lambda v: jnp.broadcast_to(v, (8, 128))
    here = slice(lo - top, hi - top)
    block = z_ref[here, lo:hi]
    part = [block[8 * g : 8 * g + 8] for g in range(16)]
    for q in range(0, 128, 2):
        gq, sq = q // 8, q % 8
        first, second = part[gq][sq : sq + 1, :], part[gq][sq + 1 : sq + 2, :]
        a, b, c = wide(first[:, q : q + 1]), wide(second[:, q : q + 1]), wide(second[:, q + 1 : q + 2])
        inverse = 1.0 / (a * c - b * b)
        l1 = lane[:1]
        one = jnp.where(l1 == q, c, jnp.where(l1 == q + 1, -b, c * first - b * second)) * inverse
        two = jnp.where(l1 == q, -b, jnp.where(l1 == q + 1, a, a * second - b * first)) * inverse
        one, two = tile(one), tile(two)
        pair = (lane == q) | (lane == q + 1)
        for g in range(gq, 16):
            if g == gq and sq == 6:
                continue
            left, right = tile(part[g][:, q : q + 1]), tile(part[g][:, q + 1 : q + 2])
            if g == gq:
                below = sub > sq + 1
                left, right = jnp.where(below, left, 0.0), jnp.where(below, right, 0.0)
                kept = jnp.where(pair & below, 0.0, part[g])
            else:
                kept = jnp.where(pair, 0.0, part[g])
            part[g] = (kept - left * one) - right * two
    done = jnp.concatenate(part, 0)
    odd = lax.rem(i128, 2) == 1
    diag = jnp.sum(jnp.where(i128 == j128, done, 0.0), axis=1, keepdims=True)
    beside = jnp.sum(jnp.where((j128 == i128 - 1) & odd, done, 0.0), axis=1, keepdims=True)
    unit = jnp.where(i128 == j128, 1.0, jnp.where(j128 < i128 - jnp.where(odd, 1, 0), done, 0.0))
    above = pltpu.roll(unit, 1, 0)
    ratio = jnp.where(odd[:, :1], beside / pltpu.roll(diag, 1, 0), 0.0)
    unit = unit - ratio * above
    pivots = diag - ratio * beside
    scale = lax.rsqrt(pivots)
    scale = scale * (1.5 - 0.5 * pivots * scale * scale)
    own = unit * scale
    x_ref[:, lo:hi] = own
    if lo:
        left = dot(own, z_ref[here, :lo])
        x_ref[:, :lo] = left
    if hi < PANEL:
        down = dot(z_ref[hi - top :, lo:hi], own, 1, 1)
        if lo:
            o_ref[:, :lo] = z_ref[hi - top :, :lo] - dot(down, left)
        o_ref[:, lo:hi] = -dot(down, own)
        o_ref[:, hi:] = z_ref[hi - top :, hi:] - dot(down, dot(own, z_ref[here, hi:]))


def factor_inverse(at, gram, mate):
    n = PANEL
    shape = lambda r, c: jax.ShapeDtypeStruct((r, c), jnp.float32)
    step = lambda kernel, out, ins, scratch, k: pl.pallas_call(
        kernel,
        out_shape=out,
        in_specs=ins,
        out_specs=[VMEM] * len(out),
        scratch_shapes=scratch,
        compiler_params=pltpu.CompilerParams(vmem_limit_bytes=LIMIT),
        cost_estimate=pl.CostEstimate(flops=k * 10**10, bytes_accessed=n * n * 4, transcendentals=0),
    )
    square = [pltpu.VMEM((n, n), jnp.float32)]
    l0, z = step(first_factor_kernel, [shape(128, 128), shape(384, n)], [SMEM, VMEM, VMEM], square, 1)(at, gram, mate)
    l1, z = step(second_factor_kernel, [shape(128, 256), shape(256, n)], [VMEM], [], 1)(z)
    rest = [pltpu.VMEM((128, n), jnp.float32)]
    l2, l3 = step(last_factor_kernel, [shape(128, 384), shape(128, n)], [VMEM], rest, 2)(z)
    return l0, l1, l2, l3


def final_kernel(at_ref, l0, l1, l2, l3, p_ref, m_ref, a_ref, b0, b1, b2, b3, o_ref, r_ref, g_ref, q_ref):
    root = math.sqrt(X * Z * p_ref.shape[0])
    x, p = at_ref[0], at_ref[2] * C + at_ref[3]
    mid, width = a_ref.shape[3], m_ref.shape[1]
    step = PANEL // X
    tile = step // Z
    inverse = [l0[...], l1[...], l2[...], l3[...]]
    basis = [dot(p_ref[:, : row.shape[1]], row, 1, 1) for row in inverse]
    q_ref[...] = jnp.concatenate(basis, 1)
    for s, ref in enumerate((b0, b1, b2, b3)):
        row = pl.multiple_of(lax.rem(x + X - s, X) * step, step)
        g_ref[pl.ds(row, step), mid:] = ref[...]
        for z in range(Z):
            g_ref[pl.ds(pl.multiple_of(row + z * tile, tile), tile), :mid] = a_ref[z, s]

    def columns(t, _):
        at = pl.ds(pl.multiple_of(t * 256, 256), 256)
        rows = jnp.concatenate([dot(l[...], g_ref[: l.shape[1], at]) for l in (l0, l1, l2, l3)], 0)
        r_ref[:, at] = rows * (1.0 / root)
        updated = m_ref[:, at] - dot(q_ref[...], rows)
        head = q_ref[:, pl.ds(pl.multiple_of(lax.rem(t, PANEL // 256) * 256, 256), 256)] * root
        o_ref[:, at] = jnp.where((p == 0) & (t < PANEL // 256), head, updated)
        return 0

    lax.fori_loop(0, width // 256, columns, 0)


def exchanged(blocks, axis):
    return lax.all_to_all(blocks, axis, 0, 0, tiled=False)


def everywhere(block, axis, size):
    return exchanged(jnp.broadcast_to(block[None], (size,) + block.shape), axis)


def shift(block, axis, size, by):
    return lax.ppermute(block, axis, [(i, (i + by) % size) for i in range(size)])


def collected(block, axis, size):
    return jnp.stack([block] + [shift(block, axis, size, k) for k in range(1, size)], 0)


def local(initial_carry, forcing, transition, partials, arc_of_row, counts):
    f32 = jnp.float32
    x, z = lax.axis_index("x"), lax.axis_index("z")
    p = lax.axis_index(("y", "core"))
    width = initial_carry.shape[1]
    rows = partials.shape[1]
    blocks = transition.shape[0]
    core, y = lax.axis_index("core"), lax.axis_index("y")
    at = jnp.stack([x, z, y, core])
    maps = transition.transpose(0, 3, 1, 2).reshape(blocks, ARCS, STATE * STATE)
    maps = jnp.pad(maps, ((0, 0), (0, 0), (0, 128 - STATE * STATE)))

    packed = call(offsets_kernel, jax.ShapeDtypeStruct((Z, PACK, 128), f32), 2, (10**7, 10**6))(maps, forcing)
    received = exchanged(packed, "z")
    total = call(totals_kernel, jax.ShapeDtypeStruct((PACK, 128), f32), 1, (10**6, 10**5))(received)
    totals = [shift(total, "x", X, k) for k in range(1, X)]
    incoming = call(incoming_kernel, jax.ShapeDtypeStruct((Z, S, 128), f32), 6, (10**6, 10**5), (0,))(
        at, *totals, received, initial_carry
    )
    incoming = exchanged(incoming, "z")
    matrix, panel = pl.pallas_call(
        design_kernel,
        out_shape=[jax.ShapeDtypeStruct((rows, width), f32), jax.ShapeDtypeStruct((rows, PANEL), f32)],
        in_specs=[SMEM] + [VMEM] * 5,
        out_specs=[VMEM, VMEM],
        scratch_shapes=[pltpu.VMEM((blocks * S, width), f32)],
        compiler_params=pltpu.CompilerParams(vmem_limit_bytes=LIMIT),
        cost_estimate=pl.CostEstimate(flops=10**8, bytes_accessed=10**6, transcendentals=0),
    )(counts, incoming, maps, forcing, partials, arc_of_row[None, :])

    both = ("y", "core")
    right, far, left = [lax.ppermute(panel, both, [(0, k)]) for k in (2, 4, 6)]
    panel = jnp.where(p == 2, right, jnp.where(p == 4, far, jnp.where(p == 6, left, panel)))
    other = lax.ppermute(panel, both, [(0, 1), (2, 3), (4, 5), (6, 7)])
    panel = jnp.where(lax.axis_index("core") == 1, other, panel)

    half, quarter, step = PANEL // C, PANEL // Y, PANEL // X
    tile, mid = step // Z, width // 4
    gram = dot(
        lax.dynamic_slice(panel, (0, core * half), (rows, half)),
        lax.dynamic_slice(panel, (0, y * quarter), (rows, quarter)),
        0, 0,
    )
    gram, panel = lax.optimization_barrier((gram, panel))
    gram = exchanged(gram.reshape(X * Z, half // X // Z, quarter), ("x", "z"))
    gram = gram.sum(0)
    turned = lax.dynamic_slice(jnp.concatenate([panel, panel], 1), (0, x * step), (rows, PANEL))
    parts = [dot(turned[:, k * step : (k + 1) * step], matrix, 0, 0) for k in range(X)]
    sent = [shift(parts[k], "x", X, k) for k in (2, 1, 3)]
    gram = everywhere(gram, ("x", "z"), X * Z).reshape(half, quarter)
    gram, sent = lax.optimization_barrier((gram, sent))
    gram = [gram] + [shift(gram, "y", Y, k) for k in (1, 2, 3)]
    gram = jnp.stack(gram, 0)
    mate = lax.ppermute(gram, "core", [(0, 1), (1, 0)])

    products = parts[0] + sent[0] + sent[1] + sent[2]
    products = exchanged(products.reshape(Z, tile, width), "z")
    products = products.sum(0)
    a, b = products[:, :mid], products[:, mid:]
    b = everywhere(b, "z", Z)
    b = b.reshape(step, width - mid)
    a = collected(a, "x", X)
    a = everywhere(a, "z", Z)
    b = [b] + [shift(b, "x", X, k) for k in (1, 2, 3)]

    inverse = factor_inverse(at, gram, mate)
    return pl.pallas_call(
        final_kernel,
        out_shape=[jax.ShapeDtypeStruct((rows, width), f32), jax.ShapeDtypeStruct((PANEL, width), f32)],
        in_specs=[SMEM] + [VMEM] * 11,
        out_specs=[VMEM, VMEM],
        scratch_shapes=[pltpu.VMEM((PANEL, width), f32), pltpu.VMEM((rows, PANEL), f32)],
        compiler_params=pltpu.CompilerParams(vmem_limit_bytes=LIMIT),
        cost_estimate=pl.CostEstimate(flops=4 * 10**9, bytes_accessed=6 * 10**6, transcendentals=0),
    )(at, *inverse, panel, matrix, a, *b)


def solution(mesh):
    mesh = Mesh(mesh.devices.reshape(X, Z, Y, C), ("x", "z", "y", "core"))
    e, q = ("x", "z"), ("y", "core")
    return jax.shard_map(
        local,
        mesh=mesh,
        in_specs=(P(None, q), P(e, None, q), P(e, None, None, None), P(None, e), P(e), P(e)),
        out_specs=(P(e, q), P(None, q)),
        check_vma=False,
    )
```

time: 208 us -> 204 us (0.981)
  blocking collectives: 29.4 us -> 49.6 us
  Pallas kernels: 54.5 us -> 41.6 us
  starting transfers between devices: 51.3 us -> 42.4 us
    all_to_all x2 -> x3, blocking collectives: 29.4 us -> 49.6 us  [exchanged(): return lax.all_to_all(blocks, axis, 0, 0, tiled=False)]
    all_to_all x5 -> x4, starting transfers between devices: 26.5 us -> 19.6 us  [exchanged(): return lax.all_to_all(blocks, axis, 0, 0, tiled=False)]
    pallas_call x2 -> x3, Pallas kernels: 34.7 us -> 28.8 us  [the longest x1 13.2 us: factor_inverse(): step(last_factor_kernel, [shape(128, 384), shape(128, n)], [VMEM], rest, 2)]
    all_to_all x5 -> x4, waiting for transfers between devices: 26.6 us -> 28.2 us  [exchanged(): return lax.all_to_all(blocks, axis, 0, 0, tiled=False)]
    ppermute x16 -> x15, starting transfers between devices: 19.9 us -> 18.8 us  [shift(): lax.ppermute(block, axis, [(i, (i + by) % size) for i in range(size)])]
    ppermute x16 -> x15, waiting for transfers between devices: 14.4 us -> 13.6 us  [shift(): lax.ppermute(block, axis, [(i, (i + by) % size) for i in range(size)])]
  transfers between devices with their start and end apart: 26 -> 24, of which waited for: 14 -> 10; matrix products, arithmetic and copies ran while one was open for 2% -> 2% of each run, Pallas kernels for 17% -> 14%
where the time goes in v1:
time: 204 us; the launch traced here: 201 us
  waiting for transfers between devices  54.1 us (27%)
  blocking collectives  49.6 us (24%)
  starting transfers between devices  42.4 us (21%)
  Pallas kernels  41.6 us (20%)
  local copies, waits for them, and re-layouts  5.63 us (3%)
  matrix products  4.97 us (2%)
    all_to_all x3, blocking collectives, exchanged(): return lax.all_to_all(blocks, axis, 0, 0, tiled=False)  49.6 us
    all_to_all x4, waiting for transfers between devices, exchanged(): return lax.all_to_all(blocks, axis, 0, 0, tiled=False)  28.2 us
    all_to_all x4, starting transfers between devices, exchanged(): return lax.all_to_all(blocks, axis, 0, 0, tiled=False)  19.6 us
    ppermute x15, starting transfers between devices, shift(): lax.ppermute(block, axis, [(i, (i + by) % size) for i in range(size)])  18.8 us
    ppermute x15, waiting for transfers between devices, shift(): lax.ppermute(block, axis, [(i, (i + by) % size) for i in range(size)])  13.6 us
    pallas_call x1, Pallas kernels, factor_inverse(): step(last_factor_kernel, [shape(128, 384), shape(128, n)], [VMEM], rest, 2)  13.2 us
    ppermute x3, waiting for transfers between devices, local(): right, far, left = [lax.ppermute(panel, both, [(0, k)]) for k in (2, 4, 6)]  11.1 us
    pallas_call x1, Pallas kernels, factor_inverse(): step(first_factor_kernel, [shape(128, 128), shape(384, n)], [SMEM, VMEM,...  8.35 us
  transfers between devices with their start and end apart: 24, of which 10 were waited for; matrix products, arithmetic and copies ran while one was open for 2% of the time, Pallas kernels for 14%

profile of v1, /device:TPU:8, one launch (start us, length us, event | category | flops | bytes accessed | tf_op | source)
XLA Modules:
  0.0 200.7 jit_solution(4623672866138942512)
XLA Ops:
  0.7 1.0 copy.10
  1.7 1.0 copy-done
  2.7 1.1 shard_map.77
  3.8 8.5 %all-to-all-start = ((f32[8,56,128]{2,1,0:T(8,128)}), f32[8,56,128]{2,1,0:T(8,128)S(1)}, u32[]{:S(2)}, u32[]{:S(2)}) async-start(f32[8,56,128]{2,1,0:T(8,128)} %shard_map.77), calls=%async_computation | async-start | bytes 458752 | tf_op jit(solution)/shard_map/all_to_all | solution.py:260
  12.3 11.2 %all-to-all-done.r_ref = f32[8,56,128]{2,1,0:T(8,128)S(1)} async-done(((f32[8,56,128]{2,1,0:T(8,128)}), f32[8,56,128]{2,1,0:T(8,128)S(1)}, u32[]{:S(2)}, u32[]{:S(2)}) %all-to-all-start) | async-done | bytes 229408 | tf_op jit(solution)/shard_map/all_to_all | solution.py:260
  24.0 2.8 %collective-permute-start.2 = (f32[56,128]{1,0:T(8,128)S(1)}, f32[56,128]{1,0:T(8,128)S(1)}, u32[]{:S(2)}, u32[]{:S(2)}) collective-permute-start(f32[56,128]{1,0:T(8,128)S(1)} %shard_map.78), channel_id=1, source_target_pairs={{0,192},{64,0},{128,64},{192,128},{1,193},{65,1},{129,65},{193,129... | collective-permute-start | bytes 86024 | tf_op jit(solution)/shard_map/ppermute | solution.py:268
  26.8 0.8 collective-permute-start.1
  27.6 0.9 collective-permute-start
  28.6 3.6 %collective-permute-done.1.t2 = f32[56,128]{1,0:T(8,128)S(1)} collective-permute-done((f32[56,128]{1,0:T(8,128)S(1)}, f32[56,128]{1,0:T(8,128)S(1)}, u32[]{:S(2)}, u32[]{:S(2)}) %collective-permute-start.1) | collective-permute-done | bytes 28704 | tf_op jit(solution)/shard_map/ppermute | solution.py:268
  32.7 0.9 copy-done.2
  33.6 1.2 shard_map.79
  34.8 12.2 %all_to_all.35.i_ref = f32[8,48,128]{2,1,0:T(8,128)S(1)} all-to-all(f32[8,48,128]{2,1,0:T(8,128)S(1)} %shard_map.79), channel_id=1, replica_groups=mesh['x'=4,'z'=8,'y'=4,'core'=2] {'z'}, dimensions={0} | all-to-all | bytes 393216 | tf_op jit(solution)/shard_map/all_to_all | solution.py:260
  47.0 1.6 shard_map.80
  48.6 0.7 collective-permute-start.5
  49.3 0.7 collective-permute-start.4
  50.0 1.3 collective-permute-start.3
  51.4 11.1 %collective-permute-done.3 = f32[128,512]{1,0:T(8,128)S(1)} collective-permute-done((f32[128,512]{1,0:T(8,128)S(1)}, f32[128,512]{1,0:T(8,128)S(1)}, u32[]{:S(2)}, u32[]{:S(2)}) %collective-permute-start.3) | collective-permute-done | bytes 262176 | tf_op jit(solution)/shard_map/ppermute | solution.py:306
  62.6 1.3 collective-permute-start.6
  63.9 1.1 collective-permute-done.6
  65.5 0.6 fusion.6
  66.8 0.6 fusion.10
  67.4 1.6 collective-permute-start.7
  69.0 3.2 %collective-permute-start.9 = (f32[128,1024]{1,0:T(8,128)S(1)}, f32[128,1024]{1,0:T(8,128)}, u32[]{:S(2)}, u32[]{:S(2)}) collective-permute-start(f32[128,1024]{1,0:T(8,128)S(1)} %fusion.6), channel_id=1, source_target_pairs={{0,192},{64,0},{128,64},{192,128},{1,193},{65,1},{129,65},{193,129... | collective-permute-start | bytes 1572872 | tf_op jit(solution)/shard_map/ppermute | solution.py:268
  72.3 23.6 %all_to_all.36 = f32[32,8,128]{2,1,0:T(8,128)S(1)} all-to-all(f32[32,8,128]{2,1,0:T(8,128)S(1)} %bitcast.30), channel_id=1, replica_groups=mesh['x'=4,'z'=8,'y'=4,'core'=2] {'x','z'}, dimensions={0} | all-to-all | bytes 262144 | tf_op jit(solution)/shard_map/all_to_all | solution.py:260
  96.0 13.8 %all_to_all.37 = f32[32,8,128]{2,1,0:T(8,128)S(1)} all-to-all(f32[32,8,128]{2,1,0:T(8,128)S(1)} %broadcast_in_dim.9), channel_id=1, replica_groups=mesh['x'=4,'z'=8,'y'=4,'core'=2] {'x','z'}, dimensions={0} | all-to-all | bytes 262144 | tf_op jit(solution)/shard_map/all_to_all | solution.py:260
  110.0 1.9 collective-permute-start.10
  111.9 5.2 %collective-permute-done.12 = f32[256,128]{1,0:T(8,128)S(1)} collective-permute-done((f32[256,128]{1,0:T(8,128)S(1)}, f32[256,128]{1,0:T(8,128)S(1)}, u32[]{:S(2)}, u32[]{:S(2)}) %collective-permute-start.12) | collective-permute-done | bytes 131104 | tf_op jit(solution)/shard_map/ppermute | solution.py:268
  117.1 1.2 collective-permute-done.10
  118.4 2.7 %fusion.1 = f32[128,1024]{1,0:T(8,128)} fusion(f32[128,1024]{1,0:T(8,128)} %collective-permute-done.9, f32[128,1024]{1,0:T(8,128)} %collective-permute-done.8, f32[128,1024]{1,0:T(8,128)S(1)} %collective-permute-done.7, f32[128,1024]{1,0:T(8,128)S(1)} %get-tuple-element.19.m_ref, f32[128,512]{1,0:T(8,128)S(1)} %fusion.2), kind=kOutput, calls=%fused_computation.2 | convolution fusion | flops 201719808 | bytes 2686976 | tf_op jit(solution)/shard_map/dot_general | solution.py:36
  121.1 4.1 %all-to-all-start.4 = ((f32[8,16,1024]{2,1,0:T(8,128)}), f32[8,16,1024]{2,1,0:T(8,128)}, u32[]{:S(2)}, u32[]{:S(2)}) async-start(f32[8,16,1024]{2,1,0:T(8,128)} %bitcast.13), calls=%async_computation.4 | async-start | bytes 1048576 | tf_op jit(solution)/shard_map/all_to_all | solution.py:260
  125.3 8.4 %shard_map.81 = (f32[128,128]{1,0:T(8,128)S(1)}, f32[384,512]{1,0:T(8,128)S(1)}) custom-call(s32[4]{0:T(128)S(1)} %pad_add_fusion.at_ref, f32[4,256,128]{2,1,0:T(8,128)S(1)} %pad_maximum_fusion.g_ref, f32[4,256,128]{2,1,0:T(8,128)S(1)} %collective-permute-done.13.m_ref), custom_call_target="tpu_custom_call" | custom-call | flops 10000000000 | bytes 1048576 | tf_op jit(solution)/shard_map/pallas_call | solution.py:225
  133.6 10.1 %all-to-all-done.4 = f32[8,16,1024]{2,1,0:T(8,128)} async-done(((f32[8,16,1024]{2,1,0:T(8,128)}), f32[8,16,1024]{2,1,0:T(8,128)}, u32[]{:S(2)}, u32[]{:S(2)}) %all-to-all-start.4) | async-done | bytes 524320 | tf_op jit(solution)/shard_map/all_to_all | solution.py:260
  143.7 1.1 reduce_sum.19
  144.8 1.6 collective-permute-start.15
  147.0 2.6 %collective-permute-start.16 = (f32[16,256]{1,0:T(8,128)S(1)}, f32[16,256]{1,0:T(8,128)S(1)}, u32[]{:S(2)}, u32[]{:S(2)}) collective-permute-start(f32[16,256]{1,0:T(8,128)S(1)} %get-tuple-element.31), channel_id=1, source_target_pairs={{0,192},{64,0},{128,64},{192,128},{1,193},{65,1},{129,65},{193,129... | collective-permute-start | bytes 49160 | tf_op jit(solution)/shard_map/ppermute | solution.py:268
  149.6 0.8 broadcast_in_dim.11
  150.4 3.5 %all-to-all-start.6 = ((f32[8,16,768]{2,1,0:T(8,128)}), f32[8,16,768]{2,1,0:T(8,128)S(1)}, u32[]{:S(2)}, u32[]{:S(2)}) async-start(f32[8,16,768]{2,1,0:T(8,128)} %broadcast_in_dim.11), calls=%async_computation.6 | async-start | bytes 786432 | tf_op jit(solution)/shard_map/all_to_all | solution.py:260
  153.9 7.3 %shard_map.82 = (f32[128,256]{1,0:T(8,128)S(1)}, f32[256,512]{1,0:T(8,128)S(1)}) custom-call(f32[384,512]{1,0:T(8,128)S(1)} %get-tuple-element.22.z_ref), custom_call_target="tpu_custom_call" | custom-call | flops 10000000000 | bytes 1048576 | tf_op jit(solution)/shard_map/pallas_call | solution.py:226
  161.2 6.9 %all-to-all-done.6 = f32[8,16,768]{2,1,0:T(8,128)S(1)} async-done(((f32[8,16,768]{2,1,0:T(8,128)}), f32[8,16,768]{2,1,0:T(8,128)S(1)}, u32[]{:S(2)}, u32[]{:S(2)}) %all-to-all-start.6) | async-done | bytes 393248 | tf_op jit(solution)/shard_map/all_to_all | solution.py:260
  168.1 0.9 broadcast_in_dim.10
  169.0 3.5 %all-to-all-start.5 = ((f32[8,4,16,256]{3,2,1,0:T(8,128)}), f32[8,4,16,256]{3,2,1,0:T(8,128)S(1)}, u32[]{:S(2)}, u32[]{:S(2)}) async-start(f32[8,4,16,256]{3,2,1,0:T(8,128)} %broadcast_in_dim.10), calls=%async_computation.5 | async-start | bytes 1048576 | tf_op jit(solution)/shard_map/all_to_all | solution.py:260
  172.5 0.9 collective-permute-start.19
  173.4 0.8 collective-permute-start.18
  174.2 0.8 collective-permute-start.17
  175.1 1.0 copy-done.7
  176.1 13.2 %shard_map.83 = (f32[128,384]{1,0:T(8,128)S(1)}, f32[128,512]{1,0:T(8,128)S(1)}) custom-call(f32[256,512]{1,0:T(8,128)S(1)} %copy-done.7), custom_call_target="tpu_custom_call" | custom-call | flops 20000000000 | bytes 1048576 | tf_op jit(solution)/shard_map/pallas_call | solution.py:228
  189.4 3.1 %collective-permute-done.17.b1 = f32[128,768]{1,0:T(8,128)S(1)} collective-permute-done((f32[128,768]{1,0:T(8,128)S(1)}, f32[128,768]{1,0:T(8,128)S(1)}, u32[]{:S(2)}, u32[]{:S(2)}) %collective-permute-start.17) | collective-permute-done | bytes 393248 | tf_op jit(solution)/shard_map/ppermute | solution.py:268
  192.4 8.3 %shard_map.84 = (f32[128,1024]{1,0:T(8,128)}, f32[512,1024]{1,0:T(8,128)}) custom-call(s32[4]{0:T(128)S(1)} %pad_add_fusion.at_ref, f32[128,128]{1,0:T(8,128)S(1)} %get-tuple-element.21.l0, f32[128,256]{1,0:T(8,128)S(1)} %get-tuple-element.23.l1, f32[128,384]{1,0:T(8,128)S(1)} %get-tuple-element.25.l2, f32[128,512]{1,0:T(8,128)S(1)} %get-tuple-element.26.l3, ...), custom_call_target="tpu_custom_call" | custom-call | flops 4000000000 | bytes 6000000 | tf_op jit(solution)/shard_map/pallas_call | solution.py:341
  (47 shorter events, 3.4 us)
Async XLA Ops:
  0.6 46.4 %copy-start.4 = (s32[4]{0:T(128)S(1)}, s32[4]{0:T(128)}, u32[]{:S(2)}) copy-start(s32[4]{0:T(128)} %n_ref.1) | copy-start | bytes 52
  0.6 46.4 %copy-start.5 = (s32[128]{0:T(128)S(1)}, s32[128]{0:T(128)}, u32[]{:S(2)}) copy-start(s32[128]{0:T(128)} %param.10) | copy-start | bytes 1540
  0.7 46.4 %copy-start.3 = (f32[6,128]{1,0:T(8,128)S(1)}, f32[6,128]{1,0:T(8,128)}, u32[]{:S(2)}) copy-start(f32[6,128]{1,0:T(8,128)} %p_ref.1) | copy-start | bytes 9220
  1.7 1.0 copy-start
  2.7 44.4 %copy-start.1 = (bf16[4,48,1024]{2,1,0:T(8,128)(2,1)S(1)}, bf16[4,48,1024]{2,1,0:T(8,128)(2,1)}, u32[]{:S(2)}) copy-start(bf16[4,48,1024]{2,1,0:T(8,128)(2,1)} %f_ref.3) | copy-start | bytes 1179652
  3.8 19.6 %all-to-all-start = ((f32[8,56,128]{2,1,0:T(8,128)}), f32[8,56,128]{2,1,0:T(8,128)S(1)}, u32[]{:S(2)}, u32[]{:S(2)}) async-start(f32[8,56,128]{2,1,0:T(8,128)} %shard_map.77), calls=%async_computation | async-start | bytes 458752 | tf_op jit(solution)/shard_map/all_to_all | solution.py:260
  24.0 4.6 %collective-permute-start.2 = (f32[56,128]{1,0:T(8,128)S(1)}, f32[56,128]{1,0:T(8,128)S(1)}, u32[]{:S(2)}, u32[]{:S(2)}) collective-permute-start(f32[56,128]{1,0:T(8,128)S(1)} %shard_map.78), channel_id=1, source_target_pairs={{0,192},{64,0},{128,64},{192,128},{1,193},{65,1},{129,65},{193,129... | collective-permute-start | bytes 86024 | tf_op jit(solution)/shard_map/ppermute | solution.py:268
  26.8 5.4 %collective-permute-start.1 = (f32[56,128]{1,0:T(8,128)S(1)}, f32[56,128]{1,0:T(8,128)S(1)}, u32[]{:S(2)}, u32[]{:S(2)}) collective-permute-start(f32[56,128]{1,0:T(8,128)S(1)} %shard_map.78), channel_id=1, source_target_pairs={{0,128},{64,192},{128,0},{192,64},{1,129},{65,193},{129,1},{193,65... | collective-permute-start | bytes 86024 | tf_op jit(solution)/shard_map/ppermute | solution.py:268
  27.6 5.1 %collective-permute-start = (f32[56,128]{1,0:T(8,128)S(1)}, f32[56,128]{1,0:T(8,128)S(1)}, u32[]{:S(2)}, u32[]{:S(2)}) collective-permute-start(f32[56,128]{1,0:T(8,128)S(1)} %shard_map.78), channel_id=1, source_target_pairs={{0,64},{64,128},{128,192},{192,0},{1,65},{65,129},{129,193},{193,1... | collective-permute-start | bytes 86024 | tf_op jit(solution)/shard_map/ppermute | solution.py:268
  32.7 0.9 copy-start.2
  48.6 2.7 %collective-permute-start.5 = (f32[128,512]{1,0:T(8,128)S(1)}, f32[128,512]{1,0:T(8,128)S(1)}, u32[]{:S(2)}, u32[]{:S(2)}) collective-permute-start(f32[128,512]{1,0:T(8,128)S(1)} %get-tuple-element.16), channel_id=1, source_target_pairs={{0,6},{8,14},{16,22},{24,30},{32,38},{40,46},{48,54},{56,62},{64,7... | collective-permute-start | bytes 786440 | tf_op jit(solution)/shard_map/ppermute | solution.py:306
  49.3 2.0 %collective-permute-start.4 = (f32[128,512]{1,0:T(8,128)S(1)}, f32[128,512]{1,0:T(8,128)S(1)}, u32[]{:S(2)}, u32[]{:S(2)}) collective-permute-start(f32[128,512]{1,0:T(8,128)S(1)} %get-tuple-element.16), channel_id=1, source_target_pairs={{0,4},{8,12},{16,20},{24,28},{32,36},{40,44},{48,52},{56,60},{64,6... | collective-permute-start | bytes 786440 | tf_op jit(solution)/shard_map/ppermute | solution.py:306
  50.0 12.5 %collective-permute-start.3 = (f32[128,512]{1,0:T(8,128)S(1)}, f32[128,512]{1,0:T(8,128)S(1)}, u32[]{:S(2)}, u32[]{:S(2)}) collective-permute-start(f32[128,512]{1,0:T(8,128)S(1)} %get-tuple-element.16), channel_id=1, source_target_pairs={{0,2},{8,10},{16,18},{24,26},{32,34},{40,42},{48,50},{56,58},{64,6... | collective-permute-start | bytes 786440 | tf_op jit(solution)/shard_map/ppermute | solution.py:306
  62.6 2.4 %collective-permute-start.6 = (f32[128,512]{1,0:T(8,128)S(1)}, f32[128,512]{1,0:T(8,128)S(1)}, u32[]{:S(2)}, u32[]{:S(2)}) collective-permute-start(f32[128,512]{1,0:T(8,128)S(1)} %select_select_fusion), channel_id=1, source_target_pairs={{0,1},{2,3},{4,5},{6,7},{8,9},{10,11},{12,13},{14,15},{16,17},{18,... | collective-permute-start | bytes 786440 | tf_op jit(solution)/shard_map/ppermute | solution.py:308
  67.4 42.3 %collective-permute-start.7 = (f32[128,1024]{1,0:T(8,128)S(1)}, f32[128,1024]{1,0:T(8,128)S(1)}, u32[]{:S(2)}, u32[]{:S(2)}) collective-permute-start(f32[128,1024]{1,0:T(8,128)S(1)} %fusion.10), channel_id=1, source_target_pairs={{0,128},{64,192},{128,0},{192,64},{1,129},{65,193},{129,1},{193,65... | collective-permute-start | bytes 1572872 | tf_op jit(solution)/shard_map/ppermute | solution.py:268
  69.0 40.7 %collective-permute-start.8 = (f32[128,1024]{1,0:T(8,128)S(1)}, f32[128,1024]{1,0:T(8,128)}, u32[]{:S(2)}, u32[]{:S(2)}) collective-permute-start(f32[128,1024]{1,0:T(8,128)S(1)} %fusion.8), channel_id=1, source_target_pairs={{0,64},{64,128},{128,192},{192,0},{1,65},{65,129},{129,193},{193,1... | collective-permute-start | bytes 1572872 | tf_op jit(solution)/shard_map/ppermute | solution.py:268
  69.0 40.7 %collective-permute-start.9 = (f32[128,1024]{1,0:T(8,128)S(1)}, f32[128,1024]{1,0:T(8,128)}, u32[]{:S(2)}, u32[]{:S(2)}) collective-permute-start(f32[128,1024]{1,0:T(8,128)S(1)} %fusion.6), channel_id=1, source_target_pairs={{0,192},{64,0},{128,64},{192,128},{1,193},{65,1},{129,65},{193,129... | collective-permute-start | bytes 1572872 | tf_op jit(solution)/shard_map/ppermute | solution.py:268
  109.8 7.4 %collective-permute-start.12 = (f32[256,128]{1,0:T(8,128)S(1)}, f32[256,128]{1,0:T(8,128)S(1)}, u32[]{:S(2)}, u32[]{:S(2)}) collective-permute-start(f32[256,128]{1,0:T(8,128)S(1)} %bitcast.31), channel_id=1, source_target_pairs={{0,6},{2,0},{4,2},{6,4},{1,7},{3,1},{5,3},{7,5},{8,14},{10,8},{12,... | collective-permute-start | bytes 393224 | tf_op jit(solution)/shard_map/ppermute | solution.py:268
  109.8 7.3 %collective-permute-start.11 = (f32[256,128]{1,0:T(8,128)S(1)}, f32[256,128]{1,0:T(8,128)S(1)}, u32[]{:S(2)}, u32[]{:S(2)}) collective-permute-start(f32[256,128]{1,0:T(8,128)S(1)} %bitcast.32), channel_id=1, source_target_pairs={{0,4},{2,6},{4,0},{6,2},{1,5},{3,7},{5,1},{7,3},{8,12},{10,14},{12... | collective-permute-start | bytes 393224 | tf_op jit(solution)/shard_map/ppermute | solution.py:268
  110.0 8.3 %collective-permute-start.10 = (f32[256,128]{1,0:T(8,128)S(1)}, f32[256,128]{1,0:T(8,128)S(1)}, u32[]{:S(2)}, u32[]{:S(2)}) collective-permute-start(f32[256,128]{1,0:T(8,128)S(1)} %bitcast.33), channel_id=1, source_target_pairs={{0,2},{2,4},{4,6},{6,0},{1,3},{3,5},{5,7},{7,1},{8,10},{10,12},{12... | collective-permute-start | bytes 393224 | tf_op jit(solution)/shard_map/ppermute | solution.py:268
  118.3 6.9 %collective-permute-start.13 = (f32[4,256,128]{2,1,0:T(8,128)S(1)}, f32[4,256,128]{2,1,0:T(8,128)S(1)}, u32[]{:S(2)}, u32[]{:S(2)}) collective-permute-start(f32[4,256,128]{2,1,0:T(8,128)S(1)} %pad_maximum_fusion.g_ref), channel_id=1, source_target_pairs={{0,1},{1,0},{2,3},{3,2},{4,5},{5,4},{6,7},{7,6},{8,9},{9,8},{10,11... | collective-permute-start | bytes 1572872 | tf_op jit(solution)/shard_map/ppermute | solution.py:328
  121.1 22.6 %all-to-all-start.4 = ((f32[8,16,1024]{2,1,0:T(8,128)}), f32[8,16,1024]{2,1,0:T(8,128)}, u32[]{:S(2)}, u32[]{:S(2)}) async-start(f32[8,16,1024]{2,1,0:T(8,128)} %bitcast.13), calls=%async_computation.4 | async-start | bytes 1048576 | tf_op jit(solution)/shard_map/all_to_all | solution.py:260
  144.8 16.3 %collective-permute-start.15 = (f32[16,256]{1,0:T(8,128)S(1)}, f32[16,256]{1,0:T(8,128)S(1)}, u32[]{:S(2)}, u32[]{:S(2)}) collective-permute-start(f32[16,256]{1,0:T(8,128)S(1)} %get-tuple-element.31), channel_id=1, source_target_pairs={{0,128},{64,192},{128,0},{192,64},{1,129},{65,193},{129,1},{193,65... | collective-permute-start | bytes 49160 | tf_op jit(solution)/shard_map/ppermute | solution.py:268
  146.4 14.8 %collective-permute-start.14 = (f32[16,256]{1,0:T(8,128)S(1)}, f32[16,256]{1,0:T(8,128)S(1)}, u32[]{:S(2)}, u32[]{:S(2)}) collective-permute-start(f32[16,256]{1,0:T(8,128)S(1)} %get-tuple-element.31), channel_id=1, source_target_pairs={{0,64},{64,128},{128,192},{192,0},{1,65},{65,129},{129,193},{193,1... | collective-permute-start | bytes 49160 | tf_op jit(solution)/shard_map/ppermute | solution.py:268
  147.0 14.2 %collective-permute-start.16 = (f32[16,256]{1,0:T(8,128)S(1)}, f32[16,256]{1,0:T(8,128)S(1)}, u32[]{:S(2)}, u32[]{:S(2)}) collective-permute-start(f32[16,256]{1,0:T(8,128)S(1)} %get-tuple-element.31), channel_id=1, source_target_pairs={{0,192},{64,0},{128,64},{192,128},{1,193},{65,1},{129,65},{193,129... | collective-permute-start | bytes 49160 | tf_op jit(solution)/shard_map/ppermute | solution.py:268
  150.4 17.7 %all-to-all-start.6 = ((f32[8,16,768]{2,1,0:T(8,128)}), f32[8,16,768]{2,1,0:T(8,128)S(1)}, u32[]{:S(2)}, u32[]{:S(2)}) async-start(f32[8,16,768]{2,1,0:T(8,128)} %broadcast_in_dim.11), calls=%async_computation.6 | async-start | bytes 786432 | tf_op jit(solution)/shard_map/all_to_all | solution.py:260
  161.1 7.9 %copy-start.6 = (f32[256,512]{1,0:T(8,128)}, f32[256,512]{1,0:T(8,128)S(1)}, u32[]{:S(2)}) copy-start(f32[256,512]{1,0:T(8,128)S(1)} %get-tuple-element.24.z_ref) | copy-start | bytes 1572868
  169.0 20.3 %all-to-all-start.5 = ((f32[8,4,16,256]{3,2,1,0:T(8,128)}), f32[8,4,16,256]{3,2,1,0:T(8,128)S(1)}, u32[]{:S(2)}, u32[]{:S(2)}) async-start(f32[8,4,16,256]{3,2,1,0:T(8,128)} %broadcast_in_dim.10), calls=%async_computation.5 | async-start | bytes 1048576 | tf_op jit(solution)/shard_map/all_to_all | solution.py:260
  172.5 16.8 %collective-permute-start.19 = (f32[128,768]{1,0:T(8,128)S(1)}, f32[128,768]{1,0:T(8,128)S(1)}, u32[]{:S(2)}, u32[]{:S(2)}) collective-permute-start(f32[128,768]{1,0:T(8,128)S(1)} %bitcast.25), channel_id=1, source_target_pairs={{0,192},{64,0},{128,64},{192,128},{1,193},{65,1},{129,65},{193,129... | collective-permute-start | bytes 1179656 | tf_op jit(solution)/shard_map/ppermute | solution.py:268
  173.4 15.9 %collective-permute-start.18 = (f32[128,768]{1,0:T(8,128)S(1)}, f32[128,768]{1,0:T(8,128)S(1)}, u32[]{:S(2)}, u32[]{:S(2)}) collective-permute-start(f32[128,768]{1,0:T(8,128)S(1)} %bitcast.26), channel_id=1, source_target_pairs={{0,128},{64,192},{128,0},{192,64},{1,129},{65,193},{129,1},{193,65... | collective-permute-start | bytes 1179656 | tf_op jit(solution)/shard_map/ppermute | solution.py:268
  174.2 18.2 %collective-permute-start.17 = (f32[128,768]{1,0:T(8,128)S(1)}, f32[128,768]{1,0:T(8,128)S(1)}, u32[]{:S(2)}, u32[]{:S(2)}) collective-permute-start(f32[128,768]{1,0:T(8,128)S(1)} %bitcast.27), channel_id=1, source_target_pairs={{0,64},{64,128},{128,192},{192,0},{1,65},{65,129},{129,193},{193,1... | collective-permute-start | bytes 1179656 | tf_op jit(solution)/shard_map/ppermute | solution.py:268
  175.1 1.0 copy-start.7

commit v2 on v1

--- a/solution.py
+++ b/solution.py
@@ -1,3 +1,4 @@
+import functools
 import math
 
 import jax
@@ -229,31 +230,42 @@
     return l0, l1, l2, l3
 
 
-def final_kernel(at_ref, l0, l1, l2, l3, p_ref, m_ref, a_ref, b0, b1, b2, b3, o_ref, r_ref, g_ref, q_ref):
+def assembled(at_ref, refs, g_ref):
+    step = PANEL // X
+    for s, ref in zip((0, 2, 1, 3), refs):
+        row = pl.multiple_of(lax.rem(at_ref[0] + X - s, X) * step, step)
+        g_ref[pl.ds(row, step), :] = ref[...]
+
+
+def first_final_kernel(mid, at_ref, l0, l1, l2, l3, p_ref, m_ref, b0, b1, b2, b3, o_ref, r_ref, q_ref, g_ref):
     root = math.sqrt(X * Z * p_ref.shape[0])
-    x, p = at_ref[0], at_ref[2] * C + at_ref[3]
-    mid, width = a_ref.shape[3], m_ref.shape[1]
-    step = PANEL // X
-    tile = step // Z
-    inverse = [l0[...], l1[...], l2[...], l3[...]]
-    basis = [dot(p_ref[:, : row.shape[1]], row, 1, 1) for row in inverse]
-    q_ref[...] = jnp.concatenate(basis, 1)
-    for s, ref in enumerate((b0, b1, b2, b3)):
-        row = pl.multiple_of(lax.rem(x + X - s, X) * step, step)
-        g_ref[pl.ds(row, step), mid:] = ref[...]
-        for z in range(Z):
-            g_ref[pl.ds(pl.multiple_of(row + z * tile, tile), tile), :mid] = a_ref[z, s]
+    p = at_ref[2] * C + at_ref[3]
+    q_ref[...] = jnp.concatenate([dot(p_ref[:, : l.shape[1]], l[...], 1, 1) for l in (l0, l1, l2, l3)], 1)
+    assembled(at_ref, (b0, b1, b2, b3), g_ref)
 
     def columns(t, _):
         at = pl.ds(pl.multiple_of(t * 256, 256), 256)
         rows = jnp.concatenate([dot(l[...], g_ref[: l.shape[1], at]) for l in (l0, l1, l2, l3)], 0)
         r_ref[:, at] = rows * (1.0 / root)
         updated = m_ref[:, at] - dot(q_ref[...], rows)
-        head = q_ref[:, pl.ds(pl.multiple_of(lax.rem(t, PANEL // 256) * 256, 256), 256)] * root
-        o_ref[:, at] = jnp.where((p == 0) & (t < PANEL // 256), head, updated)
+        o_ref[:, at] = jnp.where(p == 0, q_ref[:, at] * root, updated)
         return 0
 
-    lax.fori_loop(0, width // 256, columns, 0)
+    lax.fori_loop(0, mid // 256, columns, 0)
+
+
+def second_final_kernel(at_ref, l0, l1, l2, l3, q_ref, m_ref, b0, b1, b2, b3, o_in, r_in, o_ref, r_ref, g_ref):
+    root = math.sqrt(X * Z * q_ref.shape[0])
+    assembled(at_ref, (b0, b1, b2, b3), g_ref)
+
+    def columns(t, _):
+        at = pl.ds(pl.multiple_of(t * 256, 256), 256)
+        rows = jnp.concatenate([dot(l[...], g_ref[: l.shape[1], at]) for l in (l0, l1, l2, l3)], 0)
+        r_ref[:, at] = rows * (1.0 / root)
+        o_ref[:, at] = m_ref[:, at] - dot(q_ref[...], rows)
+        return 0
+
+    lax.fori_loop(0, m_ref.shape[1] // 256, columns, 0)
 
 
 def exchanged(blocks, axis):
@@ -266,10 +278,6 @@
 
 def shift(block, axis, size, by):
     return lax.ppermute(block, axis, [(i, (i + by) % size) for i in range(size)])
-
-
-def collected(block, axis, size):
-    return jnp.stack([block] + [shift(block, axis, size, k) for k in range(1, size)], 0)
 
 
 def local(initial_carry, forcing, transition, partials, arc_of_row, counts):
@@ -309,7 +317,7 @@
     panel = jnp.where(lax.axis_index("core") == 1, other, panel)
 
     half, quarter, step = PANEL // C, PANEL // Y, PANEL // X
-    tile, mid = step // Z, width // 4
+    tile, mid = step // Z, PANEL
     gram = dot(
         lax.dynamic_slice(panel, (0, core * half), (rows, half)),
         lax.dynamic_slice(panel, (0, y * quarter), (rows, quarter)),
@@ -330,23 +338,35 @@
     products = parts[0] + sent[0] + sent[1] + sent[2]
     products = exchanged(products.reshape(Z, tile, width), "z")
     products = products.sum(0)
-    a, b = products[:, :mid], products[:, mid:]
-    b = everywhere(b, "z", Z)
-    b = b.reshape(step, width - mid)
-    a = collected(a, "x", X)
-    a = everywhere(a, "z", Z)
-    b = [b] + [shift(b, "x", X, k) for k in (1, 2, 3)]
+    products = everywhere(products, "z", Z).reshape(step, width)
+    a = [products[:, :mid]]
+    a += [shift(a[0], "x", X, k) for k in (2, 1, 3)]
+    b = [products[:, mid:]]
+    b += [shift(b[0], "x", X, k) for k in (2, 1, 3)]
 
     inverse = factor_inverse(at, gram, mate)
+    half = jax.ShapeDtypeStruct((rows, width), f32), jax.ShapeDtypeStruct((PANEL, width), f32)
+    packed, r_rows, basis = pl.pallas_call(
+        functools.partial(first_final_kernel, mid),
+        grid=(1,),
+        out_shape=[*half, jax.ShapeDtypeStruct((rows, PANEL), f32)],
+        in_specs=[SMEM] + [VMEM] * 10,
+        out_specs=[pl.BlockSpec((rows, mid), lambda i: (0, 0)), pl.BlockSpec((PANEL, mid), lambda i: (0, 0)), VMEM],
+        scratch_shapes=[pltpu.VMEM((PANEL, mid), f32)],
+        compiler_params=pltpu.CompilerParams(vmem_limit_bytes=LIMIT),
+        cost_estimate=pl.CostEstimate(flops=2 * 10**9, bytes_accessed=3 * 10**6, transcendentals=0),
+    )(at, *inverse, panel, matrix[:, :mid], *a)
     return pl.pallas_call(
-        final_kernel,
-        out_shape=[jax.ShapeDtypeStruct((rows, width), f32), jax.ShapeDtypeStruct((PANEL, width), f32)],
-        in_specs=[SMEM] + [VMEM] * 11,
-        out_specs=[VMEM, VMEM],
-        scratch_shapes=[pltpu.VMEM((PANEL, width), f32), pltpu.VMEM((rows, PANEL), f32)],
-        compiler_params=pltpu.CompilerParams(vmem_limit_bytes=LIMIT),
-        cost_estimate=pl.CostEstimate(flops=4 * 10**9, bytes_accessed=6 * 10**6, transcendentals=0),
-    )(at, *inverse, panel, matrix, a, *b)
+        second_final_kernel,
+        grid=(1,),
+        out_shape=half,
+        in_specs=[SMEM] + [VMEM] * 10 + [pl.BlockSpec(memory_space=pl.ANY)] * 2,
+        out_specs=[pl.BlockSpec((rows, width - mid), lambda i: (0, 1)), pl.BlockSpec((PANEL, width - mid), lambda i: (0, 1))],
+        scratch_shapes=[pltpu.VMEM((PANEL, width - mid), f32)],
+        input_output_aliases={11: 0, 12: 1},
+        compiler_params=pltpu.CompilerParams(vmem_limit_bytes=LIMIT),
+        cost_estimate=pl.CostEstimate(flops=2 * 10**9, bytes_accessed=3 * 10**6, transcendentals=0),
+    )(at, *inverse, basis, matrix[:, mid:], *b, packed, r_rows)
 
 
 def solution(mesh):

time: 204 us -> 196 us (0.961); the launches traced: 201 us -> 195 us
  starting transfers between devices: 42.4 us -> 39.9 us
    all_to_all x4 -> x3, starting transfers between devices: 19.6 us -> 16.1 us  [exchanged(): return lax.all_to_all(blocks, axis, 0, 0, tiled=False)]
    all_to_all x4 -> x3, waiting for transfers between devices: 28.2 us -> 26.1 us  [exchanged(): return lax.all_to_all(blocks, axis, 0, 0, tiled=False)]
    pallas_call x1 -> x2, Pallas kernels: 8.26 us -> 9.04 us  [the longest x1 4.88 us: local(): pl.pallas_call(functools.partial(first_final_kernel, mid), grid=(1,), out...]
  transfers between devices with their start and end apart: 24 -> 23, of which waited for: 10 -> 10; matrix products, arithmetic and copies ran while one was open for 2% -> 1% of each run, Pallas kernels for 14% -> 17%
where the time goes in v2:
time: 196 us; the launch traced here: 195 us
  waiting for transfers between devices  52.4 us (27%)
  blocking collectives  49.6 us (25%)
  Pallas kernels  42.4 us (22%)
  starting transfers between devices  39.9 us (20%)
  matrix products  4.97 us (3%)
  local copies, waits for them, and re-layouts  4.89 us (2%)
    all_to_all x3, blocking collectives, exchanged(): return lax.all_to_all(blocks, axis, 0, 0, tiled=False)  49.6 us
    all_to_all x3, waiting for transfers between devices, exchanged(): return lax.all_to_all(blocks, axis, 0, 0, tiled=False)  26.1 us
    ppermute x15, starting transfers between devices, shift(): lax.ppermute(block, axis, [(i, (i + by) % size) for i in range(size)])  19.8 us
    all_to_all x3, starting transfers between devices, exchanged(): return lax.all_to_all(blocks, axis, 0, 0, tiled=False)  16.1 us
    ppermute x15, waiting for transfers between devices, shift(): lax.ppermute(block, axis, [(i, (i + by) % size) for i in range(size)])  14.1 us
    pallas_call x1, Pallas kernels, factor_inverse(): step(last_factor_kernel, [shape(128, 384), shape(128, n)], [VMEM], rest, 2)  13.2 us
    ppermute x3, waiting for transfers between devices, local(): right, far, left = [lax.ppermute(panel, both, [(0, k)]) for k in (2, 4, 6)]  11.1 us
    pallas_call x1, Pallas kernels, factor_inverse(): step(first_factor_kernel, [shape(128, 128), shape(384, n)], [SMEM, VMEM,...  8.35 us
  transfers between devices with their start and end apart: 23, of which 10 were waited for; matrix products, arithmetic and copies ran while one was open for 1% of the time, Pallas kernels for 17%

profile of v2, /device:TPU:8, one launch (start us, length us, event | category | flops | bytes accessed | tf_op | source)
XLA Modules:
  0.0 195.5 jit_solution(2438540490285055580)
XLA Ops:
  0.7 1.0 copy.12
  1.7 1.0 copy-done
  2.7 1.1 shard_map.77
  3.8 8.5 %all-to-all-start = ((f32[8,56,128]{2,1,0:T(8,128)}), f32[8,56,128]{2,1,0:T(8,128)S(1)}, u32[]{:S(2)}, u32[]{:S(2)}) async-start(f32[8,56,128]{2,1,0:T(8,128)} %shard_map.77), calls=%async_computation | async-start | bytes 458752 | tf_op jit(solution)/shard_map/all_to_all | solution.py:272
  12.3 11.2 %all-to-all-done.r_ref = f32[8,56,128]{2,1,0:T(8,128)S(1)} async-done(((f32[8,56,128]{2,1,0:T(8,128)}), f32[8,56,128]{2,1,0:T(8,128)S(1)}, u32[]{:S(2)}, u32[]{:S(2)}) %all-to-all-start) | async-done | bytes 229408 | tf_op jit(solution)/shard_map/all_to_all | solution.py:272
  24.0 2.8 %collective-permute-start.2 = (f32[56,128]{1,0:T(8,128)S(1)}, f32[56,128]{1,0:T(8,128)S(1)}, u32[]{:S(2)}, u32[]{:S(2)}) collective-permute-start(f32[56,128]{1,0:T(8,128)S(1)} %shard_map.78), channel_id=1, source_target_pairs={{0,192},{64,0},{128,64},{192,128},{1,193},{65,1},{129,65},{193,129... | collective-permute-start | bytes 86024 | tf_op jit(solution)/shard_map/ppermute | solution.py:280
  26.8 0.8 collective-permute-start.1
  27.6 0.9 collective-permute-start
  28.6 3.6 %collective-permute-done.1.t2 = f32[56,128]{1,0:T(8,128)S(1)} collective-permute-done((f32[56,128]{1,0:T(8,128)S(1)}, f32[56,128]{1,0:T(8,128)S(1)}, u32[]{:S(2)}, u32[]{:S(2)}) %collective-permute-start.1) | collective-permute-done | bytes 28704 | tf_op jit(solution)/shard_map/ppermute | solution.py:280
  32.7 0.9 copy-done.2
  33.6 1.2 shard_map.79
  34.8 12.2 %all_to_all.30.i_ref = f32[8,48,128]{2,1,0:T(8,128)S(1)} all-to-all(f32[8,48,128]{2,1,0:T(8,128)S(1)} %shard_map.79), channel_id=1, replica_groups=mesh['x'=4,'z'=8,'y'=4,'core'=2] {'z'}, dimensions={0} | all-to-all | bytes 393216 | tf_op jit(solution)/shard_map/all_to_all | solution.py:272
  47.0 1.6 shard_map.80
  48.6 0.7 collective-permute-start.5
  49.3 0.7 collective-permute-start.4
  50.0 1.3 collective-permute-start.3
  51.4 11.1 %collective-permute-done.3 = f32[128,512]{1,0:T(8,128)S(1)} collective-permute-done((f32[128,512]{1,0:T(8,128)S(1)}, f32[128,512]{1,0:T(8,128)S(1)}, u32[]{:S(2)}, u32[]{:S(2)}) %collective-permute-start.3) | collective-permute-done | bytes 262176 | tf_op jit(solution)/shard_map/ppermute | solution.py:314
  62.6 1.3 collective-permute-start.6
  63.9 1.1 collective-permute-done.6
  65.5 0.6 fusion.6
  66.2 0.6 fusion.8
  66.8 0.6 fusion.10
  67.4 1.6 collective-permute-start.7
  69.0 3.2 %collective-permute-start.9 = (f32[128,1024]{1,0:T(8,128)S(1)}, f32[128,1024]{1,0:T(8,128)}, u32[]{:S(2)}, u32[]{:S(2)}) collective-permute-start(f32[128,1024]{1,0:T(8,128)S(1)} %fusion.6), channel_id=1, source_target_pairs={{0,192},{64,0},{128,64},{192,128},{1,193},{65,1},{129,65},{193,129... | collective-permute-start | bytes 1572872 | tf_op jit(solution)/shard_map/ppermute | solution.py:280
  72.3 23.6 %all_to_all.31 = f32[32,8,128]{2,1,0:T(8,128)S(1)} all-to-all(f32[32,8,128]{2,1,0:T(8,128)S(1)} %bitcast.21), channel_id=1, replica_groups=mesh['x'=4,'z'=8,'y'=4,'core'=2] {'x','z'}, dimensions={0} | all-to-all | bytes 262144 | tf_op jit(solution)/shard_map/all_to_all | solution.py:272
  96.0 13.8 %all_to_all.32 = f32[32,8,128]{2,1,0:T(8,128)S(1)} all-to-all(f32[32,8,128]{2,1,0:T(8,128)S(1)} %broadcast_in_dim.7), channel_id=1, replica_groups=mesh['x'=4,'z'=8,'y'=4,'core'=2] {'x','z'}, dimensions={0} | all-to-all | bytes 262144 | tf_op jit(solution)/shard_map/all_to_all | solution.py:272
  109.8 2.7 %fusion.1 = f32[128,1024]{1,0:T(8,128)} fusion(f32[128,1024]{1,0:T(8,128)} %collective-permute-done.9, f32[128,1024]{1,0:T(8,128)} %collective-permute-done.8, f32[128,1024]{1,0:T(8,128)S(1)} %collective-permute-done.7, f32[128,1024]{1,0:T(8,128)S(1)} %get-tuple-element.22, f32[128,512]{1,0:T(8,128)S(1)} %fusion.2), kind=kOutput, calls=%fused_computation.2 | convolution fusion | flops 201719808 | bytes 2686976 | tf_op jit(solution)/shard_map/dot_general | solution.py:37
  112.4 3.5 %all-to-all-start.4 = ((f32[8,16,1024]{2,1,0:T(8,128)}), f32[8,16,1024]{2,1,0:T(8,128)S(1)}, u32[]{:S(2)}, u32[]{:S(2)}) async-start(f32[8,16,1024]{2,1,0:T(8,128)} %bitcast.13), calls=%async_computation.4 | async-start | bytes 1048576 | tf_op jit(solution)/shard_map/all_to_all | solution.py:272
  116.3 1.7 collective-permute-start.10
  118.1 5.2 %collective-permute-done.12 = f32[256,128]{1,0:T(8,128)S(1)} collective-permute-done((f32[256,128]{1,0:T(8,128)S(1)}, f32[256,128]{1,0:T(8,128)S(1)}, u32[]{:S(2)}, u32[]{:S(2)}) %collective-permute-start.12) | collective-permute-done | bytes 131104 | tf_op jit(solution)/shard_map/ppermute | solution.py:280
  123.3 1.2 collective-permute-done.10
  124.6 7.5 %all-to-all-done.4 = f32[8,16,1024]{2,1,0:T(8,128)S(1)} async-done(((f32[8,16,1024]{2,1,0:T(8,128)}), f32[8,16,1024]{2,1,0:T(8,128)S(1)}, u32[]{:S(2)}, u32[]{:S(2)}) %all-to-all-start.4) | async-done | bytes 524320 | tf_op jit(solution)/shard_map/all_to_all | solution.py:272
  132.2 0.8 broadcast_in_dim.8
  133.1 4.1 %all-to-all-start.5 = ((f32[8,16,1024]{2,1,0:T(8,128)}), f32[8,16,1024]{2,1,0:T(8,128)}, u32[]{:S(2)}, u32[]{:S(2)}) async-start(f32[8,16,1024]{2,1,0:T(8,128)} %broadcast_in_dim.8), calls=%async_computation.5 | async-start | bytes 1048576 | tf_op jit(solution)/shard_map/all_to_all | solution.py:272
  137.2 8.4 %shard_map.81 = (f32[128,128]{1,0:T(8,128)S(1)}, f32[384,512]{1,0:T(8,128)S(1)}) custom-call(s32[4]{0:T(128)S(1)} %pad_add_fusion.at_ref, f32[4,256,128]{2,1,0:T(8,128)S(1)} %pad_maximum_fusion.g_ref, f32[4,256,128]{2,1,0:T(8,128)S(1)} %collective-permute-done.13.m_ref), custom_call_target="tpu_custom_call" | custom-call | flops 10000000000 | bytes 1048576 | tf_op jit(solution)/shard_map/pallas_call | solution.py:226
  145.6 7.4 %all-to-all-done.5 = f32[8,16,1024]{2,1,0:T(8,128)} async-done(((f32[8,16,1024]{2,1,0:T(8,128)}), f32[8,16,1024]{2,1,0:T(8,128)}, u32[]{:S(2)}, u32[]{:S(2)}) %all-to-all-start.5) | async-done | bytes 524320 | tf_op jit(solution)/shard_map/all_to_all | solution.py:272
  152.9 1.1 fusion.14
  154.0 1.5 collective-permute-start.16
  155.5 7.3 %shard_map.82 = (f32[128,256]{1,0:T(8,128)S(1)}, f32[256,512]{1,0:T(8,128)S(1)}) custom-call(f32[384,512]{1,0:T(8,128)S(1)} %get-tuple-element.25.z_ref), custom_call_target="tpu_custom_call" | custom-call | flops 10000000000 | bytes 1048576 | tf_op jit(solution)/shard_map/pallas_call | solution.py:227
  162.8 0.8 collective-permute-start.19
  163.6 1.3 collective-permute-start.18
  164.9 1.2 collective-permute-start.17
  166.2 1.6 collective-permute-start.15
  167.7 1.9 collective-permute-start.14
  169.6 13.2 %shard_map.83 = (f32[128,384]{1,0:T(8,128)S(1)}, f32[128,512]{1,0:T(8,128)S(1)}) custom-call(f32[256,512]{1,0:T(8,128)S(1)} %get-tuple-element.27.z_ref), custom_call_target="tpu_custom_call" | custom-call | flops 20000000000 | bytes 1048576 | tf_op jit(solution)/shard_map/pallas_call | solution.py:229
  182.9 3.6 %collective-permute-done.15.b2 = f32[128,512]{1,0:T(8,128)S(1)} collective-permute-done((f32[128,512]{1,0:T(8,128)S(1)}, f32[128,512]{1,0:T(8,128)S(1)}, u32[]{:S(2)}, u32[]{:S(2)}) %collective-permute-start.15) | collective-permute-done | bytes 262176 | tf_op jit(solution)/shard_map/ppermute | solution.py:280
  186.4 4.9 %shard_map.84 = (f32[128,1024]{1,0:T(8,128)}, f32[512,1024]{1,0:T(8,128)}, f32[128,512]{1,0:T(8,128)S(1)}) custom-call(s32[4]{0:T(128)S(1)} %pad_add_fusion.at_ref, f32[128,128]{1,0:T(8,128)S(1)} %get-tuple-element.24.l0, f32[128,256]{1,0:T(8,128)S(1)} %get-tuple-element.26.l1, f32[128,384]{1,0:T(8,128)S(1)} %get-tuple-element.28.l2, ...), custom_call_target="tpu_custom_call" | custom-call | flops 2000000000 | bytes 3000000 | tf_op jit(solution)/shard_map/pallas_call | solution.py:349
  191.3 4.2 %shard_map.85 = (f32[128,1024]{1,0:T(8,128)}, f32[512,1024]{1,0:T(8,128)}) custom-call(s32[4]{0:T(128)S(1)} %pad_add_fusion.at_ref, f32[128,128]{1,0:T(8,128)S(1)} %get-tuple-element.24.l0, f32[128,256]{1,0:T(8,128)S(1)} %get-tuple-element.26.l1, f32[128,384]{1,0:T(8,128)S(1)} %get-tuple-element.28.l2, ...), custom_call_target="tpu_custom_call", output_to_operand_aliasing={{0}: (11, {}), {1}: (12, {})} | custom-call | flops 2000000000 | bytes 3000000 | tf_op jit(solution)/shard_map/pallas_call | solution.py:359
  (40 shorter events, 2.4 us)
Async XLA Ops:
  0.6 46.4 %copy-start.4 = (s32[4]{0:T(128)S(1)}, s32[4]{0:T(128)}, u32[]{:S(2)}) copy-start(s32[4]{0:T(128)} %n_ref.1) | copy-start | bytes 52
  0.6 46.4 %copy-start.5 = (s32[128]{0:T(128)S(1)}, s32[128]{0:T(128)}, u32[]{:S(2)}) copy-start(s32[128]{0:T(128)} %param.10) | copy-start | bytes 1540
  0.7 46.4 %copy-start.3 = (f32[6,128]{1,0:T(8,128)S(1)}, f32[6,128]{1,0:T(8,128)}, u32[]{:S(2)}) copy-start(f32[6,128]{1,0:T(8,128)} %p_ref.1) | copy-start | bytes 9220
  1.7 1.0 copy-start
  2.7 44.4 %copy-start.1 = (bf16[4,48,1024]{2,1,0:T(8,128)(2,1)S(1)}, bf16[4,48,1024]{2,1,0:T(8,128)(2,1)}, u32[]{:S(2)}) copy-start(bf16[4,48,1024]{2,1,0:T(8,128)(2,1)} %f_ref.3) | copy-start | bytes 1179652
  3.8 19.6 %all-to-all-start = ((f32[8,56,128]{2,1,0:T(8,128)}), f32[8,56,128]{2,1,0:T(8,128)S(1)}, u32[]{:S(2)}, u32[]{:S(2)}) async-start(f32[8,56,128]{2,1,0:T(8,128)} %shard_map.77), calls=%async_computation | async-start | bytes 458752 | tf_op jit(solution)/shard_map/all_to_all | solution.py:272
  24.0 4.6 %collective-permute-start.2 = (f32[56,128]{1,0:T(8,128)S(1)}, f32[56,128]{1,0:T(8,128)S(1)}, u32[]{:S(2)}, u32[]{:S(2)}) collective-permute-start(f32[56,128]{1,0:T(8,128)S(1)} %shard_map.78), channel_id=1, source_target_pairs={{0,192},{64,0},{128,64},{192,128},{1,193},{65,1},{129,65},{193,129... | collective-permute-start | bytes 86024 | tf_op jit(solution)/shard_map/ppermute | solution.py:280
  26.8 5.4 %collective-permute-start.1 = (f32[56,128]{1,0:T(8,128)S(1)}, f32[56,128]{1,0:T(8,128)S(1)}, u32[]{:S(2)}, u32[]{:S(2)}) collective-permute-start(f32[56,128]{1,0:T(8,128)S(1)} %shard_map.78), channel_id=1, source_target_pairs={{0,128},{64,192},{128,0},{192,64},{1,129},{65,193},{129,1},{193,65... | collective-permute-start | bytes 86024 | tf_op jit(solution)/shard_map/ppermute | solution.py:280
  27.6 5.1 %collective-permute-start = (f32[56,128]{1,0:T(8,128)S(1)}, f32[56,128]{1,0:T(8,128)S(1)}, u32[]{:S(2)}, u32[]{:S(2)}) collective-permute-start(f32[56,128]{1,0:T(8,128)S(1)} %shard_map.78), channel_id=1, source_target_pairs={{0,64},{64,128},{128,192},{192,0},{1,65},{65,129},{129,193},{193,1... | collective-permute-start | bytes 86024 | tf_op jit(solution)/shard_map/ppermute | solution.py:280
  32.7 0.9 copy-start.2
  48.6 2.7 %collective-permute-start.5 = (f32[128,512]{1,0:T(8,128)S(1)}, f32[128,512]{1,0:T(8,128)S(1)}, u32[]{:S(2)}, u32[]{:S(2)}) collective-permute-start(f32[128,512]{1,0:T(8,128)S(1)} %get-tuple-element.19), channel_id=1, source_target_pairs={{0,6},{8,14},{16,22},{24,30},{32,38},{40,46},{48,54},{56,62},{64,7... | collective-permute-start | bytes 786440 | tf_op jit(solution)/shard_map/ppermute | solution.py:314
  49.3 2.0 %collective-permute-start.4 = (f32[128,512]{1,0:T(8,128)S(1)}, f32[128,512]{1,0:T(8,128)S(1)}, u32[]{:S(2)}, u32[]{:S(2)}) collective-permute-start(f32[128,512]{1,0:T(8,128)S(1)} %get-tuple-element.19), channel_id=1, source_target_pairs={{0,4},{8,12},{16,20},{24,28},{32,36},{40,44},{48,52},{56,60},{64,6... | collective-permute-start | bytes 786440 | tf_op jit(solution)/shard_map/ppermute | solution.py:314
  50.0 12.5 %collective-permute-start.3 = (f32[128,512]{1,0:T(8,128)S(1)}, f32[128,512]{1,0:T(8,128)S(1)}, u32[]{:S(2)}, u32[]{:S(2)}) collective-permute-start(f32[128,512]{1,0:T(8,128)S(1)} %get-tuple-element.19), channel_id=1, source_target_pairs={{0,2},{8,10},{16,18},{24,26},{32,34},{40,42},{48,50},{56,58},{64,6... | collective-permute-start | bytes 786440 | tf_op jit(solution)/shard_map/ppermute | solution.py:314
  62.6 2.4 %collective-permute-start.6 = (f32[128,512]{1,0:T(8,128)S(1)}, f32[128,512]{1,0:T(8,128)S(1)}, u32[]{:S(2)}, u32[]{:S(2)}) collective-permute-start(f32[128,512]{1,0:T(8,128)S(1)} %select_select_fusion), channel_id=1, source_target_pairs={{0,1},{2,3},{4,5},{6,7},{8,9},{10,11},{12,13},{14,15},{16,17},{18,... | collective-permute-start | bytes 786440 | tf_op jit(solution)/shard_map/ppermute | solution.py:316
  67.4 42.3 %collective-permute-start.7 = (f32[128,1024]{1,0:T(8,128)S(1)}, f32[128,1024]{1,0:T(8,128)S(1)}, u32[]{:S(2)}, u32[]{:S(2)}) collective-permute-start(f32[128,1024]{1,0:T(8,128)S(1)} %fusion.10), channel_id=1, source_target_pairs={{0,128},{64,192},{128,0},{192,64},{1,129},{65,193},{129,1},{193,65... | collective-permute-start | bytes 1572872 | tf_op jit(solution)/shard_map/ppermute | solution.py:280
  69.0 40.7 %collective-permute-start.8 = (f32[128,1024]{1,0:T(8,128)S(1)}, f32[128,1024]{1,0:T(8,128)}, u32[]{:S(2)}, u32[]{:S(2)}) collective-permute-start(f32[128,1024]{1,0:T(8,128)S(1)} %fusion.8), channel_id=1, source_target_pairs={{0,64},{64,128},{128,192},{192,0},{1,65},{65,129},{129,193},{193,1... | collective-permute-start | bytes 1572872 | tf_op jit(solution)/shard_map/ppermute | solution.py:280
  69.0 40.7 %collective-permute-start.9 = (f32[128,1024]{1,0:T(8,128)S(1)}, f32[128,1024]{1,0:T(8,128)}, u32[]{:S(2)}, u32[]{:S(2)}) collective-permute-start(f32[128,1024]{1,0:T(8,128)S(1)} %fusion.6), channel_id=1, source_target_pairs={{0,192},{64,0},{128,64},{192,128},{1,193},{65,1},{129,65},{193,129... | collective-permute-start | bytes 1572872 | tf_op jit(solution)/shard_map/ppermute | solution.py:280
  112.4 19.7 %all-to-all-start.4 = ((f32[8,16,1024]{2,1,0:T(8,128)}), f32[8,16,1024]{2,1,0:T(8,128)S(1)}, u32[]{:S(2)}, u32[]{:S(2)}) async-start(f32[8,16,1024]{2,1,0:T(8,128)} %bitcast.13), calls=%async_computation.4 | async-start | bytes 1048576 | tf_op jit(solution)/shard_map/all_to_all | solution.py:272
  115.9 7.4 %collective-permute-start.12 = (f32[256,128]{1,0:T(8,128)S(1)}, f32[256,128]{1,0:T(8,128)S(1)}, u32[]{:S(2)}, u32[]{:S(2)}) collective-permute-start(f32[256,128]{1,0:T(8,128)S(1)} %bitcast.22), channel_id=1, source_target_pairs={{0,6},{2,0},{4,2},{6,4},{1,7},{3,1},{5,3},{7,5},{8,14},{10,8},{12,... | collective-permute-start | bytes 393224 | tf_op jit(solution)/shard_map/ppermute | solution.py:280
  116.0 7.3 %collective-permute-start.11 = (f32[256,128]{1,0:T(8,128)S(1)}, f32[256,128]{1,0:T(8,128)S(1)}, u32[]{:S(2)}, u32[]{:S(2)}) collective-permute-start(f32[256,128]{1,0:T(8,128)S(1)} %bitcast.23), channel_id=1, source_target_pairs={{0,4},{2,6},{4,0},{6,2},{1,5},{3,7},{5,1},{7,3},{8,12},{10,14},{12... | collective-permute-start | bytes 393224 | tf_op jit(solution)/shard_map/ppermute | solution.py:280
  116.3 8.1 %collective-permute-start.10 = (f32[256,128]{1,0:T(8,128)S(1)}, f32[256,128]{1,0:T(8,128)S(1)}, u32[]{:S(2)}, u32[]{:S(2)}) collective-permute-start(f32[256,128]{1,0:T(8,128)S(1)} %bitcast.24), channel_id=1, source_target_pairs={{0,2},{2,4},{4,6},{6,0},{1,3},{3,5},{5,7},{7,1},{8,10},{10,12},{12... | collective-permute-start | bytes 393224 | tf_op jit(solution)/shard_map/ppermute | solution.py:280
  124.5 12.7 %collective-permute-start.13 = (f32[4,256,128]{2,1,0:T(8,128)S(1)}, f32[4,256,128]{2,1,0:T(8,128)S(1)}, u32[]{:S(2)}, u32[]{:S(2)}) collective-permute-start(f32[4,256,128]{2,1,0:T(8,128)S(1)} %pad_maximum_fusion.g_ref), channel_id=1, source_target_pairs={{0,1},{1,0},{2,3},{3,2},{4,5},{5,4},{6,7},{7,6},{8,9},{9,8},{10,11... | collective-permute-start | bytes 1572872 | tf_op jit(solution)/shard_map/ppermute | solution.py:336
  133.1 19.9 %all-to-all-start.5 = ((f32[8,16,1024]{2,1,0:T(8,128)}), f32[8,16,1024]{2,1,0:T(8,128)}, u32[]{:S(2)}, u32[]{:S(2)}) async-start(f32[8,16,1024]{2,1,0:T(8,128)} %broadcast_in_dim.8), calls=%async_computation.5 | async-start | bytes 1048576 | tf_op jit(solution)/shard_map/all_to_all | solution.py:272
  154.0 13.7 %collective-permute-start.16 = (f32[128,512]{1,0:T(8,128)S(1)}, f32[128,512]{1,0:T(8,128)S(1)}, u32[]{:S(2)}, u32[]{:S(2)}) collective-permute-start(f32[128,512]{1,0:T(8,128)S(1)} %get-tuple-element.37.b0), channel_id=1, source_target_pairs={{0,192},{64,0},{128,64},{192,128},{1,193},{65,1},{129,65},{193,129... | collective-permute-start | bytes 786440 | tf_op jit(solution)/shard_map/ppermute | solution.py:280
  162.8 28.5 %collective-permute-start.19 = (f32[128,512]{1,0:T(8,128)S(1)}, f32[128,512]{1,0:T(8,128)S(1)}, u32[]{:S(2)}, u32[]{:S(2)}) collective-permute-start(f32[128,512]{1,0:T(8,128)S(1)} %get-tuple-element.36.b0), channel_id=1, source_target_pairs={{0,192},{64,0},{128,64},{192,128},{1,193},{65,1},{129,65},{193,129... | collective-permute-start | bytes 786440 | tf_op jit(solution)/shard_map/ppermute | solution.py:280
  163.6 27.7 %collective-permute-start.18 = (f32[128,512]{1,0:T(8,128)S(1)}, f32[128,512]{1,0:T(8,128)S(1)}, u32[]{:S(2)}, u32[]{:S(2)}) collective-permute-start(f32[128,512]{1,0:T(8,128)S(1)} %get-tuple-element.36.b0), channel_id=1, source_target_pairs={{0,64},{64,128},{128,192},{192,0},{1,65},{65,129},{129,193},{193,1... | collective-permute-start | bytes 786440 | tf_op jit(solution)/shard_map/ppermute | solution.py:280
  164.9 26.4 %collective-permute-start.17 = (f32[128,512]{1,0:T(8,128)S(1)}, f32[128,512]{1,0:T(8,128)S(1)}, u32[]{:S(2)}, u32[]{:S(2)}) collective-permute-start(f32[128,512]{1,0:T(8,128)S(1)} %get-tuple-element.36.b0), channel_id=1, source_target_pairs={{0,128},{64,192},{128,0},{192,64},{1,129},{65,193},{129,1},{193,65... | collective-permute-start | bytes 786440 | tf_op jit(solution)/shard_map/ppermute | solution.py:280
  166.2 20.3 %collective-permute-start.15 = (f32[128,512]{1,0:T(8,128)S(1)}, f32[128,512]{1,0:T(8,128)S(1)}, u32[]{:S(2)}, u32[]{:S(2)}) collective-permute-start(f32[128,512]{1,0:T(8,128)S(1)} %get-tuple-element.37.b0), channel_id=1, source_target_pairs={{0,64},{64,128},{128,192},{192,0},{1,65},{65,129},{129,193},{193,1... | collective-permute-start | bytes 786440 | tf_op jit(solution)/shard_map/ppermute | solution.py:280
  167.7 18.7 %collective-permute-start.14 = (f32[128,512]{1,0:T(8,128)S(1)}, f32[128,512]{1,0:T(8,128)S(1)}, u32[]{:S(2)}, u32[]{:S(2)}) collective-permute-start(f32[128,512]{1,0:T(8,128)S(1)} %get-tuple-element.37.b0), channel_id=1, source_target_pairs={{0,128},{64,192},{128,0},{192,64},{1,129},{65,193},{129,1},{193,65... | collective-permute-start | bytes 786440 | tf_op jit(solution)/shard_map/ppermute | solution.py:280

commit v3 on v2

--- a/solution.py
+++ b/solution.py
@@ -149,9 +149,12 @@
     factor_block(1, x_ref, z_ref, 128, o_ref)
 
 
-def last_factor_kernel(z_ref, x_ref, y_ref, o_ref):
+def third_factor_kernel(z_ref, x_ref, o_ref):
     factor_block(2, x_ref, z_ref, 256, o_ref)
-    factor_block(3, y_ref, o_ref, 384, None)
+
+
+def last_factor_kernel(z_ref, x_ref):
+    factor_block(3, x_ref, z_ref, 384, None)
 
 
 def factor_block(k, x_ref, z_ref, top, o_ref):
@@ -225,8 +228,8 @@
     square = [pltpu.VMEM((n, n), jnp.float32)]
     l0, z = step(first_factor_kernel, [shape(128, 128), shape(384, n)], [SMEM, VMEM, VMEM], square, 1)(at, gram, mate)
     l1, z = step(second_factor_kernel, [shape(128, 256), shape(256, n)], [VMEM], [], 1)(z)
-    rest = [pltpu.VMEM((128, n), jnp.float32)]
-    l2, l3 = step(last_factor_kernel, [shape(128, 384), shape(128, n)], [VMEM], rest, 2)(z)
+    l2, z = step(third_factor_kernel, [shape(128, 384), shape(128, n)], [VMEM], [], 1)(z)
+    (l3,) = step(last_factor_kernel, [shape(128, n)], [VMEM], [], 1)(z)
     return l0, l1, l2, l3
 
 
@@ -338,7 +341,8 @@
     products = parts[0] + sent[0] + sent[1] + sent[2]
     products = exchanged(products.reshape(Z, tile, width), "z")
     products = products.sum(0)
-    products = everywhere(products, "z", Z).reshape(step, width)
+    products = everywhere(products, "z", Z)
+    products = products.reshape(step, width)
     a = [products[:, :mid]]
     a += [shift(a[0], "x", X, k) for k in (2, 1, 3)]
     b = [products[:, mid:]]

time: 196 us -> 213 us (1.087)
  waiting for transfers between devices: 52.4 us -> 68 us
    ppermute x15, waiting for transfers between devices: 14.1 us -> 23.8 us  [shift(): lax.ppermute(block, axis, [(i, (i + by) % size) for i in range(size)])]
    all_to_all x3, waiting for transfers between devices: 26.1 us -> 31.9 us  [exchanged(): return lax.all_to_all(blocks, axis, 0, 0, tiled=False)]
    pallas_call x1 -> x2, Pallas kernels: 13.2 us -> 13.2 us  [the longest x1 6.95 us: factor_inverse(): step(third_factor_kernel, [shape(128, 384), shape(128, n)], [VMEM], [], 1)]
  transfers between devices with their start and end apart: 23 -> 23, of which waited for: 10 -> 10; matrix products, arithmetic and copies ran while one was open for 1% -> 1% of each run, Pallas kernels for 17% -> 16%
where the time goes in v3:
time: 213 us; the launch traced here: 212 us
  waiting for transfers between devices  68 us (32%)
  blocking collectives  49.6 us (23%)
  Pallas kernels  42.6 us (20%)
  starting transfers between devices  40.1 us (19%)
  matrix products  5.07 us (2%)
  local copies, waits for them, and re-layouts  3.87 us (2%)
    all_to_all x3, blocking collectives, exchanged(): return lax.all_to_all(blocks, axis, 0, 0, tiled=False)  49.6 us
    all_to_all x3, waiting for transfers between devices, exchanged(): return lax.all_to_all(blocks, axis, 0, 0, tiled=False)  31.9 us
    ppermute x15, waiting for transfers between devices, shift(): lax.ppermute(block, axis, [(i, (i + by) % size) for i in range(size)])  23.8 us
    ppermute x15, starting transfers between devices, shift(): lax.ppermute(block, axis, [(i, (i + by) % size) for i in range(size)])  20 us
    all_to_all x3, starting transfers between devices, exchanged(): return lax.all_to_all(blocks, axis, 0, 0, tiled=False)  16.1 us
    ppermute x3, waiting for transfers between devices, local(): right, far, left = [lax.ppermute(panel, both, [(0, k)]) for k in (2, 4, 6)]  11.1 us
    pallas_call x1, Pallas kernels, factor_inverse(): step(first_factor_kernel, [shape(128, 128), shape(384, n)], [SMEM, VMEM,...  8.35 us
    pallas_call x1, Pallas kernels, factor_inverse(): step(second_factor_kernel, [shape(128, 256), shape(256, n)], [VMEM], [], 1)  7.27 us
  transfers between devices with their start and end apart: 23, of which 10 were waited for; matrix products, arithmetic and copies ran while one was open for 1% of the time, Pallas kernels for 16%

profile of v3, /device:TPU:8, one launch (start us, length us, event | category | flops | bytes accessed | tf_op | source)
XLA Modules:
  0.0 211.6 jit_solution(18186571872576225255)
XLA Ops:
  0.7 1.0 copy.12
  1.7 1.0 copy-done
  2.7 1.1 shard_map.77
  3.8 8.5 %all-to-all-start = ((f32[8,56,128]{2,1,0:T(8,128)}), f32[8,56,128]{2,1,0:T(8,128)S(1)}, u32[]{:S(2)}, u32[]{:S(2)}) async-start(f32[8,56,128]{2,1,0:T(8,128)} %shard_map.77), calls=%async_computation | async-start | bytes 458752 | tf_op jit(solution)/shard_map/all_to_all | solution.py:275
  12.3 11.2 %all-to-all-done.r_ref = f32[8,56,128]{2,1,0:T(8,128)S(1)} async-done(((f32[8,56,128]{2,1,0:T(8,128)}), f32[8,56,128]{2,1,0:T(8,128)S(1)}, u32[]{:S(2)}, u32[]{:S(2)}) %all-to-all-start) | async-done | bytes 229408 | tf_op jit(solution)/shard_map/all_to_all | solution.py:275
  24.0 2.8 %collective-permute-start.2 = (f32[56,128]{1,0:T(8,128)S(1)}, f32[56,128]{1,0:T(8,128)S(1)}, u32[]{:S(2)}, u32[]{:S(2)}) collective-permute-start(f32[56,128]{1,0:T(8,128)S(1)} %shard_map.78), channel_id=1, source_target_pairs={{0,192},{64,0},{128,64},{192,128},{1,193},{65,1},{129,65},{193,129... | collective-permute-start | bytes 86024 | tf_op jit(solution)/shard_map/ppermute | solution.py:283
  26.8 0.8 collective-permute-start.1
  27.6 0.9 collective-permute-start
  28.6 3.6 %collective-permute-done.1.t2 = f32[56,128]{1,0:T(8,128)S(1)} collective-permute-done((f32[56,128]{1,0:T(8,128)S(1)}, f32[56,128]{1,0:T(8,128)S(1)}, u32[]{:S(2)}, u32[]{:S(2)}) %collective-permute-start.1) | collective-permute-done | bytes 28704 | tf_op jit(solution)/shard_map/ppermute | solution.py:283
  32.7 0.9 copy-done.2
  33.6 1.2 shard_map.79
  34.8 12.2 %all_to_all.30.i_ref = f32[8,48,128]{2,1,0:T(8,128)S(1)} all-to-all(f32[8,48,128]{2,1,0:T(8,128)S(1)} %shard_map.79), channel_id=1, replica_groups=mesh['x'=4,'z'=8,'y'=4,'core'=2] {'z'}, dimensions={0} | all-to-all | bytes 393216 | tf_op jit(solution)/shard_map/all_to_all | solution.py:275
  47.0 1.6 shard_map.80
  48.7 0.7 collective-permute-start.5
  49.3 0.7 collective-permute-start.4
  50.0 1.3 collective-permute-start.3
  51.4 11.1 %collective-permute-done.3 = f32[128,512]{1,0:T(8,128)S(1)} collective-permute-done((f32[128,512]{1,0:T(8,128)S(1)}, f32[128,512]{1,0:T(8,128)S(1)}, u32[]{:S(2)}, u32[]{:S(2)}) %collective-permute-start.3) | collective-permute-done | bytes 262176 | tf_op jit(solution)/shard_map/ppermute | solution.py:317
  62.6 1.3 collective-permute-start.6
  63.9 1.1 collective-permute-done.6
  66.2 0.6 fusion.8
  66.8 0.6 fusion.10
  67.4 1.6 collective-permute-start.7
  69.0 3.2 %collective-permute-start.9 = (f32[128,1024]{1,0:T(8,128)S(1)}, f32[128,1024]{1,0:T(8,128)}, u32[]{:S(2)}, u32[]{:S(2)}) collective-permute-start(f32[128,1024]{1,0:T(8,128)S(1)} %fusion.6), channel_id=1, source_target_pairs={{0,192},{64,0},{128,64},{192,128},{1,193},{65,1},{129,65},{193,129... | collective-permute-start | bytes 1572872 | tf_op jit(solution)/shard_map/ppermute | solution.py:283
  72.3 23.6 %all_to_all.31 = f32[32,8,128]{2,1,0:T(8,128)S(1)} all-to-all(f32[32,8,128]{2,1,0:T(8,128)S(1)} %bitcast.22), channel_id=1, replica_groups=mesh['x'=4,'z'=8,'y'=4,'core'=2] {'x','z'}, dimensions={0} | all-to-all | bytes 262144 | tf_op jit(solution)/shard_map/all_to_all | solution.py:275
  95.9 13.8 %all_to_all.32 = f32[32,8,128]{2,1,0:T(8,128)S(1)} all-to-all(f32[32,8,128]{2,1,0:T(8,128)S(1)} %broadcast_in_dim.7), channel_id=1, replica_groups=mesh['x'=4,'z'=8,'y'=4,'core'=2] {'x','z'}, dimensions={0} | all-to-all | bytes 262144 | tf_op jit(solution)/shard_map/all_to_all | solution.py:275
  109.9 1.9 collective-permute-start.10
  111.8 5.3 %collective-permute-done.12 = f32[256,128]{1,0:T(8,128)S(1)} collective-permute-done((f32[256,128]{1,0:T(8,128)S(1)}, f32[256,128]{1,0:T(8,128)S(1)}, u32[]{:S(2)}, u32[]{:S(2)}) %collective-permute-start.12) | collective-permute-done | bytes 131104 | tf_op jit(solution)/shard_map/ppermute | solution.py:283
  117.1 1.2 collective-permute-done.10
  118.4 2.8 %fusion.1 = f32[128,1024]{1,0:T(8,128)} fusion(f32[128,1024]{1,0:T(8,128)} %collective-permute-done.9, f32[128,1024]{1,0:T(8,128)} %collective-permute-done.8, f32[128,1024]{1,0:T(8,128)} %copy-done.6, f32[128,1024]{1,0:T(8,128)S(1)} %get-tuple-element.22, f32[128,512]{1,0:T(8,128)S(1)} %fusion.2), kind=kOutput, calls=%fused_computation.2 | convolution fusion | flops 201719808 | bytes 2686976 | tf_op jit(solution)/shard_map/dot_general | solution.py:37
  121.2 4.1 %all-to-all-start.4 = ((f32[8,16,1024]{2,1,0:T(8,128)}), f32[8,16,1024]{2,1,0:T(8,128)}, u32[]{:S(2)}, u32[]{:S(2)}) async-start(f32[8,16,1024]{2,1,0:T(8,128)} %bitcast.13), calls=%async_computation.4 | async-start | bytes 1048576 | tf_op jit(solution)/shard_map/all_to_all | solution.py:275
  125.4 8.4 %shard_map.81 = (f32[128,128]{1,0:T(8,128)S(1)}, f32[384,512]{1,0:T(8,128)S(1)}) custom-call(s32[4]{0:T(128)S(1)} %pad_add_fusion.at_ref, f32[4,256,128]{2,1,0:T(8,128)S(1)} %pad_maximum_fusion.g_ref, f32[4,256,128]{2,1,0:T(8,128)S(1)} %collective-permute-done.13.m_ref), custom_call_target="tpu_custom_call" | custom-call | flops 10000000000 | bytes 1048576 | tf_op jit(solution)/shard_map/pallas_call | solution.py:229
  133.8 10.1 %all-to-all-done.4 = f32[8,16,1024]{2,1,0:T(8,128)} async-done(((f32[8,16,1024]{2,1,0:T(8,128)}), f32[8,16,1024]{2,1,0:T(8,128)}, u32[]{:S(2)}, u32[]{:S(2)}) %all-to-all-start.4) | async-done | bytes 524320 | tf_op jit(solution)/shard_map/all_to_all | solution.py:275
  143.9 1.1 reduce_sum.19
  145.0 0.8 broadcast_in_dim.8
  145.8 3.5 %all-to-all-start.5 = ((f32[8,16,1024]{2,1,0:T(8,128)}), f32[8,16,1024]{2,1,0:T(8,128)S(1)}, u32[]{:S(2)}, u32[]{:S(2)}) async-start(f32[8,16,1024]{2,1,0:T(8,128)} %broadcast_in_dim.8), calls=%async_computation.5 | async-start | bytes 1048576 | tf_op jit(solution)/shard_map/all_to_all | solution.py:275
  149.3 7.3 %shard_map.82 = (f32[128,256]{1,0:T(8,128)S(1)}, f32[256,512]{1,0:T(8,128)S(1)}) custom-call(f32[384,512]{1,0:T(8,128)S(1)} %get-tuple-element.25.z_ref), custom_call_target="tpu_custom_call" | custom-call | flops 10000000000 | bytes 1048576 | tf_op jit(solution)/shard_map/pallas_call | solution.py:230
  156.6 10.6 %all-to-all-done.5 = f32[8,16,1024]{2,1,0:T(8,128)S(1)} async-done(((f32[8,16,1024]{2,1,0:T(8,128)}), f32[8,16,1024]{2,1,0:T(8,128)S(1)}, u32[]{:S(2)}, u32[]{:S(2)}) %all-to-all-start.5) | async-done | bytes 524320 | tf_op jit(solution)/shard_map/all_to_all | solution.py:275
  167.3 1.5 collective-permute-start.16
  168.8 7.0 %shard_map.83 = (f32[128,384]{1,0:T(8,128)S(1)}, f32[128,512]{1,0:T(8,128)S(1)}) custom-call(f32[256,512]{1,0:T(8,128)S(1)} %get-tuple-element.27.z_ref), custom_call_target="tpu_custom_call" | custom-call | flops 10000000000 | bytes 1048576 | tf_op jit(solution)/shard_map/pallas_call | solution.py:231
  175.7 0.9 collective-permute-start.19
  176.6 1.2 collective-permute-start.18
  177.8 1.5 collective-permute-start.17
  179.3 1.4 collective-permute-start.15
  180.7 2.1 collective-permute-start.14
  182.8 6.3 %shard_map.84.l3 = f32[128,512]{1,0:T(8,128)S(1)} custom-call(f32[128,512]{1,0:T(8,128)S(1)} %get-tuple-element.29.z_ref), custom_call_target="tpu_custom_call" | custom-call | flops 10000000000 | bytes 1048576 | tf_op jit(solution)/shard_map/pallas_call | solution.py:232
  189.1 13.3 %collective-permute-done.15.b2 = f32[128,512]{1,0:T(8,128)S(1)} collective-permute-done((f32[128,512]{1,0:T(8,128)S(1)}, f32[128,512]{1,0:T(8,128)S(1)}, u32[]{:S(2)}, u32[]{:S(2)}) %collective-permute-start.15) | collective-permute-done | bytes 262176 | tf_op jit(solution)/shard_map/ppermute | solution.py:283
  202.4 5.0 %shard_map.85 = (f32[128,1024]{1,0:T(8,128)}, f32[512,1024]{1,0:T(8,128)}, f32[128,512]{1,0:T(8,128)S(1)}) custom-call(s32[4]{0:T(128)S(1)} %pad_add_fusion.at_ref, f32[128,128]{1,0:T(8,128)S(1)} %get-tuple-element.24.l0, f32[128,256]{1,0:T(8,128)S(1)} %get-tuple-element.26.l1, f32[128,384]{1,0:T(8,128)S(1)} %get-tuple-element.28.l2, ...), custom_call_target="tpu_custom_call" | custom-call | flops 2000000000 | bytes 3000000 | tf_op jit(solution)/shard_map/pallas_call | solution.py:353
  207.4 4.2 %shard_map.86 = (f32[128,1024]{1,0:T(8,128)}, f32[512,1024]{1,0:T(8,128)}) custom-call(s32[4]{0:T(128)S(1)} %pad_add_fusion.at_ref, f32[128,128]{1,0:T(8,128)S(1)} %get-tuple-element.24.l0, f32[128,256]{1,0:T(8,128)S(1)} %get-tuple-element.26.l1, f32[128,384]{1,0:T(8,128)S(1)} %get-tuple-element.28.l2, ...), custom_call_target="tpu_custom_call", output_to_operand_aliasing={{0}: (11, {}), {1}: (12, {})} | custom-call | flops 2000000000 | bytes 3000000 | tf_op jit(solution)/shard_map/pallas_call | solution.py:363
  (43 shorter events, 2.9 us)
Async XLA Ops:
  0.6 46.4 %copy-start.4 = (s32[4]{0:T(128)S(1)}, s32[4]{0:T(128)}, u32[]{:S(2)}) copy-start(s32[4]{0:T(128)} %n_ref.1) | copy-start | bytes 52
  0.6 46.4 %copy-start.5 = (s32[128]{0:T(128)S(1)}, s32[128]{0:T(128)}, u32[]{:S(2)}) copy-start(s32[128]{0:T(128)} %param.10) | copy-start | bytes 1540
  0.7 46.4 %copy-start.3 = (f32[6,128]{1,0:T(8,128)S(1)}, f32[6,128]{1,0:T(8,128)}, u32[]{:S(2)}) copy-start(f32[6,128]{1,0:T(8,128)} %p_ref.1) | copy-start | bytes 9220
  1.7 1.0 copy-start
  2.7 44.4 %copy-start.1 = (bf16[4,48,1024]{2,1,0:T(8,128)(2,1)S(1)}, bf16[4,48,1024]{2,1,0:T(8,128)(2,1)}, u32[]{:S(2)}) copy-start(bf16[4,48,1024]{2,1,0:T(8,128)(2,1)} %f_ref.3) | copy-start | bytes 1179652
  3.8 19.6 %all-to-all-start = ((f32[8,56,128]{2,1,0:T(8,128)}), f32[8,56,128]{2,1,0:T(8,128)S(1)}, u32[]{:S(2)}, u32[]{:S(2)}) async-start(f32[8,56,128]{2,1,0:T(8,128)} %shard_map.77), calls=%async_computation | async-start | bytes 458752 | tf_op jit(solution)/shard_map/all_to_all | solution.py:275
  24.0 4.6 %collective-permute-start.2 = (f32[56,128]{1,0:T(8,128)S(1)}, f32[56,128]{1,0:T(8,128)S(1)}, u32[]{:S(2)}, u32[]{:S(2)}) collective-permute-start(f32[56,128]{1,0:T(8,128)S(1)} %shard_map.78), channel_id=1, source_target_pairs={{0,192},{64,0},{128,64},{192,128},{1,193},{65,1},{129,65},{193,129... | collective-permute-start | bytes 86024 | tf_op jit(solution)/shard_map/ppermute | solution.py:283
  26.8 5.4 %collective-permute-start.1 = (f32[56,128]{1,0:T(8,128)S(1)}, f32[56,128]{1,0:T(8,128)S(1)}, u32[]{:S(2)}, u32[]{:S(2)}) collective-permute-start(f32[56,128]{1,0:T(8,128)S(1)} %shard_map.78), channel_id=1, source_target_pairs={{0,128},{64,192},{128,0},{192,64},{1,129},{65,193},{129,1},{193,65... | collective-permute-start | bytes 86024 | tf_op jit(solution)/shard_map/ppermute | solution.py:283
  27.6 5.1 %collective-permute-start = (f32[56,128]{1,0:T(8,128)S(1)}, f32[56,128]{1,0:T(8,128)S(1)}, u32[]{:S(2)}, u32[]{:S(2)}) collective-permute-start(f32[56,128]{1,0:T(8,128)S(1)} %shard_map.78), channel_id=1, source_target_pairs={{0,64},{64,128},{128,192},{192,0},{1,65},{65,129},{129,193},{193,1... | collective-permute-start | bytes 86024 | tf_op jit(solution)/shard_map/ppermute | solution.py:283
  32.7 0.9 copy-start.2
  48.7 2.7 %collective-permute-start.5 = (f32[128,512]{1,0:T(8,128)S(1)}, f32[128,512]{1,0:T(8,128)S(1)}, u32[]{:S(2)}, u32[]{:S(2)}) collective-permute-start(f32[128,512]{1,0:T(8,128)S(1)} %get-tuple-element.19), channel_id=1, source_target_pairs={{0,6},{8,14},{16,22},{24,30},{32,38},{40,46},{48,54},{56,62},{64,7... | collective-permute-start | bytes 786440 | tf_op jit(solution)/shard_map/ppermute | solution.py:317
  49.3 2.0 collective-permute-start.4
  50.0 12.5 %collective-permute-start.3 = (f32[128,512]{1,0:T(8,128)S(1)}, f32[128,512]{1,0:T(8,128)S(1)}, u32[]{:S(2)}, u32[]{:S(2)}) collective-permute-start(f32[128,512]{1,0:T(8,128)S(1)} %get-tuple-element.19), channel_id=1, source_target_pairs={{0,2},{8,10},{16,18},{24,26},{32,34},{40,42},{48,50},{56,58},{64,6... | collective-permute-start | bytes 786440 | tf_op jit(solution)/shard_map/ppermute | solution.py:317
  62.6 2.4 %collective-permute-start.6 = (f32[128,512]{1,0:T(8,128)S(1)}, f32[128,512]{1,0:T(8,128)S(1)}, u32[]{:S(2)}, u32[]{:S(2)}) collective-permute-start(f32[128,512]{1,0:T(8,128)S(1)} %select_select_fusion), channel_id=1, source_target_pairs={{0,1},{2,3},{4,5},{6,7},{8,9},{10,11},{12,13},{14,15},{16,17},{18,... | collective-permute-start | bytes 786440 | tf_op jit(solution)/shard_map/ppermute | solution.py:319
  67.4 42.3 %collective-permute-start.7 = (f32[128,1024]{1,0:T(8,128)S(1)}, f32[128,1024]{1,0:T(8,128)S(1)}, u32[]{:S(2)}, u32[]{:S(2)}) collective-permute-start(f32[128,1024]{1,0:T(8,128)S(1)} %fusion.10), channel_id=1, source_target_pairs={{0,128},{64,192},{128,0},{192,64},{1,129},{65,193},{129,1},{193,65... | collective-permute-start | bytes 1572872 | tf_op jit(solution)/shard_map/ppermute | solution.py:283
  69.0 40.7 %collective-permute-start.8 = (f32[128,1024]{1,0:T(8,128)S(1)}, f32[128,1024]{1,0:T(8,128)}, u32[]{:S(2)}, u32[]{:S(2)}) collective-permute-start(f32[128,1024]{1,0:T(8,128)S(1)} %fusion.8), channel_id=1, source_target_pairs={{0,64},{64,128},{128,192},{192,0},{1,65},{65,129},{129,193},{193,1... | collective-permute-start | bytes 1572872 | tf_op jit(solution)/shard_map/ppermute | solution.py:283
  69.0 40.7 %collective-permute-start.9 = (f32[128,1024]{1,0:T(8,128)S(1)}, f32[128,1024]{1,0:T(8,128)}, u32[]{:S(2)}, u32[]{:S(2)}) collective-permute-start(f32[128,1024]{1,0:T(8,128)S(1)} %fusion.6), channel_id=1, source_target_pairs={{0,192},{64,0},{128,64},{192,128},{1,193},{65,1},{129,65},{193,129... | collective-permute-start | bytes 1572872 | tf_op jit(solution)/shard_map/ppermute | solution.py:283
  109.7 8.5 %copy-start.6 = (f32[128,1024]{1,0:T(8,128)}, f32[128,1024]{1,0:T(8,128)S(1)}, u32[]{:S(2)}) copy-start(f32[128,1024]{1,0:T(8,128)S(1)} %collective-permute-done.7) | copy-start | bytes 1572868
  109.7 7.4 %collective-permute-start.12 = (f32[256,128]{1,0:T(8,128)S(1)}, f32[256,128]{1,0:T(8,128)S(1)}, u32[]{:S(2)}, u32[]{:S(2)}) collective-permute-start(f32[256,128]{1,0:T(8,128)S(1)} %bitcast.23), channel_id=1, source_target_pairs={{0,6},{2,0},{4,2},{6,4},{1,7},{3,1},{5,3},{7,5},{8,14},{10,8},{12,... | collective-permute-start | bytes 393224 | tf_op jit(solution)/shard_map/ppermute | solution.py:283
  109.8 7.3 %collective-permute-start.11 = (f32[256,128]{1,0:T(8,128)S(1)}, f32[256,128]{1,0:T(8,128)S(1)}, u32[]{:S(2)}, u32[]{:S(2)}) collective-permute-start(f32[256,128]{1,0:T(8,128)S(1)} %bitcast.24), channel_id=1, source_target_pairs={{0,4},{2,6},{4,0},{6,2},{1,5},{3,7},{5,1},{7,3},{8,12},{10,14},{12... | collective-permute-start | bytes 393224 | tf_op jit(solution)/shard_map/ppermute | solution.py:283
  109.9 8.3 %collective-permute-start.10 = (f32[256,128]{1,0:T(8,128)S(1)}, f32[256,128]{1,0:T(8,128)S(1)}, u32[]{:S(2)}, u32[]{:S(2)}) collective-permute-start(f32[256,128]{1,0:T(8,128)S(1)} %bitcast.25), channel_id=1, source_target_pairs={{0,2},{2,4},{4,6},{6,0},{1,3},{3,5},{5,7},{7,1},{8,10},{10,12},{12... | collective-permute-start | bytes 393224 | tf_op jit(solution)/shard_map/ppermute | solution.py:283
  118.3 7.1 %collective-permute-start.13 = (f32[4,256,128]{2,1,0:T(8,128)S(1)}, f32[4,256,128]{2,1,0:T(8,128)S(1)}, u32[]{:S(2)}, u32[]{:S(2)}) collective-permute-start(f32[4,256,128]{2,1,0:T(8,128)S(1)} %pad_maximum_fusion.g_ref), channel_id=1, source_target_pairs={{0,1},{1,0},{2,3},{3,2},{4,5},{5,4},{6,7},{7,6},{8,9},{9,8},{10,11... | collective-permute-start | bytes 1572872 | tf_op jit(solution)/shard_map/ppermute | solution.py:339
  121.2 22.6 %all-to-all-start.4 = ((f32[8,16,1024]{2,1,0:T(8,128)}), f32[8,16,1024]{2,1,0:T(8,128)}, u32[]{:S(2)}, u32[]{:S(2)}) async-start(f32[8,16,1024]{2,1,0:T(8,128)} %bitcast.13), calls=%async_computation.4 | async-start | bytes 1048576 | tf_op jit(solution)/shard_map/all_to_all | solution.py:275
  145.8 21.4 %all-to-all-start.5 = ((f32[8,16,1024]{2,1,0:T(8,128)}), f32[8,16,1024]{2,1,0:T(8,128)S(1)}, u32[]{:S(2)}, u32[]{:S(2)}) async-start(f32[8,16,1024]{2,1,0:T(8,128)} %broadcast_in_dim.8), calls=%async_computation.5 | async-start | bytes 1048576 | tf_op jit(solution)/shard_map/all_to_all | solution.py:275
  167.3 13.5 %collective-permute-start.16 = (f32[128,512]{1,0:T(8,128)S(1)}, f32[128,512]{1,0:T(8,128)S(1)}, u32[]{:S(2)}, u32[]{:S(2)}) collective-permute-start(f32[128,512]{1,0:T(8,128)S(1)} %get-tuple-element.37.b0), channel_id=1, source_target_pairs={{0,192},{64,0},{128,64},{192,128},{1,193},{65,1},{129,65},{193,129... | collective-permute-start | bytes 786440 | tf_op jit(solution)/shard_map/ppermute | solution.py:283
  175.7 31.6 %collective-permute-start.19 = (f32[128,512]{1,0:T(8,128)S(1)}, f32[128,512]{1,0:T(8,128)S(1)}, u32[]{:S(2)}, u32[]{:S(2)}) collective-permute-start(f32[128,512]{1,0:T(8,128)S(1)} %get-tuple-element.36.b0), channel_id=1, source_target_pairs={{0,192},{64,0},{128,64},{192,128},{1,193},{65,1},{129,65},{193,129... | collective-permute-start | bytes 786440 | tf_op jit(solution)/shard_map/ppermute | solution.py:283
  176.6 30.7 %collective-permute-start.18 = (f32[128,512]{1,0:T(8,128)S(1)}, f32[128,512]{1,0:T(8,128)S(1)}, u32[]{:S(2)}, u32[]{:S(2)}) collective-permute-start(f32[128,512]{1,0:T(8,128)S(1)} %get-tuple-element.36.b0), channel_id=1, source_target_pairs={{0,64},{64,128},{128,192},{192,0},{1,65},{65,129},{129,193},{193,1... | collective-permute-start | bytes 786440 | tf_op jit(solution)/shard_map/ppermute | solution.py:283
  177.8 29.5 %collective-permute-start.17 = (f32[128,512]{1,0:T(8,128)S(1)}, f32[128,512]{1,0:T(8,128)S(1)}, u32[]{:S(2)}, u32[]{:S(2)}) collective-permute-start(f32[128,512]{1,0:T(8,128)S(1)} %get-tuple-element.36.b0), channel_id=1, source_target_pairs={{0,128},{64,192},{128,0},{192,64},{1,129},{65,193},{129,1},{193,65... | collective-permute-start | bytes 786440 | tf_op jit(solution)/shard_map/ppermute | solution.py:283
  179.3 23.1 %collective-permute-start.15 = (f32[128,512]{1,0:T(8,128)S(1)}, f32[128,512]{1,0:T(8,128)S(1)}, u32[]{:S(2)}, u32[]{:S(2)}) collective-permute-start(f32[128,512]{1,0:T(8,128)S(1)} %get-tuple-element.37.b0), channel_id=1, source_target_pairs={{0,64},{64,128},{128,192},{192,0},{1,65},{65,129},{129,193},{193,1... | collective-permute-start | bytes 786440 | tf_op jit(solution)/shard_map/ppermute | solution.py:283
  180.7 21.6 %collective-permute-start.14 = (f32[128,512]{1,0:T(8,128)S(1)}, f32[128,512]{1,0:T(8,128)S(1)}, u32[]{:S(2)}, u32[]{:S(2)}) collective-permute-start(f32[128,512]{1,0:T(8,128)S(1)} %get-tuple-element.37.b0), channel_id=1, source_target_pairs={{0,128},{64,192},{128,0},{192,64},{1,129},{65,193},{129,1},{193,65... | collective-permute-start | bytes 786440 | tf_op jit(solution)/shard_map/ppermute | solution.py:283

commit v4 on v3

--- a/solution.py
+++ b/solution.py
@@ -251,7 +251,8 @@
         rows = jnp.concatenate([dot(l[...], g_ref[: l.shape[1], at]) for l in (l0, l1, l2, l3)], 0)
         r_ref[:, at] = rows * (1.0 / root)
         updated = m_ref[:, at] - dot(q_ref[...], rows)
-        o_ref[:, at] = jnp.where(p == 0, q_ref[:, at] * root, updated)
+        head = q_ref[:, pl.ds(pl.multiple_of(lax.rem(t, PANEL // 256) * 256, 256), 256)] * root
+        o_ref[:, at] = jnp.where((p == 0) & (t < PANEL // 256), head, updated)
         return 0
 
     lax.fori_loop(0, mid // 256, columns, 0)
@@ -320,7 +321,7 @@
     panel = jnp.where(lax.axis_index("core") == 1, other, panel)
 
     half, quarter, step = PANEL // C, PANEL // Y, PANEL // X
-    tile, mid = step // Z, PANEL
+    tile, mid = step // Z, 3 * width // 4
     gram = dot(
         lax.dynamic_slice(panel, (0, core * half), (rows, half)),
         lax.dynamic_slice(panel, (0, y * quarter), (rows, quarter)),
@@ -365,7 +366,7 @@
         grid=(1,),
         out_shape=half,
         in_specs=[SMEM] + [VMEM] * 10 + [pl.BlockSpec(memory_space=pl.ANY)] * 2,
-        out_specs=[pl.BlockSpec((rows, width - mid), lambda i: (0, 1)), pl.BlockSpec((PANEL, width - mid), lambda i: (0, 1))],
+        out_specs=[pl.BlockSpec((rows, width - mid), lambda i: (0, 3)), pl.BlockSpec((PANEL, width - mid), lambda i: (0, 3))],
         scratch_shapes=[pltpu.VMEM((PANEL, width - mid), f32)],
         input_output_aliases={11: 0, 12: 1},
         compiler_params=pltpu.CompilerParams(vmem_limit_bytes=LIMIT),

time: 213 us -> 199 us (0.934)
  waiting for transfers between devices: 68 us -> 56.3 us
    all_to_all x3, waiting for transfers between devices: 31.9 us -> 24.7 us  [exchanged(): return lax.all_to_all(blocks, axis, 0, 0, tiled=False)]
    ppermute x15, waiting for transfers between devices: 23.8 us -> 19.3 us  [shift(): lax.ppermute(block, axis, [(i, (i + by) % size) for i in range(size)])]
  transfers between devices with their start and end apart: 23 -> 23, of which waited for: 10 -> 11; matrix products, arithmetic and copies ran while one was open for 1% -> 1% of each run, Pallas kernels for 16% -> 18%
where the time goes in v4:
time: 199 us; the launch traced here: 198 us
  waiting for transfers between devices  56.3 us (28%)
  blocking collectives  49.6 us (25%)
  Pallas kernels  42.6 us (21%)
  starting transfers between devices  39.6 us (20%)
  matrix products  4.95 us (2%)
  local copies, waits for them, and re-layouts  3.87 us (2%)
    all_to_all x3, blocking collectives, exchanged(): return lax.all_to_all(blocks, axis, 0, 0, tiled=False)  49.6 us
    all_to_all x3, waiting for transfers between devices, exchanged(): return lax.all_to_all(blocks, axis, 0, 0, tiled=False)  24.7 us
    ppermute x15, waiting for transfers between devices, shift(): lax.ppermute(block, axis, [(i, (i + by) % size) for i in range(size)])  19.3 us
    ppermute x15, starting transfers between devices, shift(): lax.ppermute(block, axis, [(i, (i + by) % size) for i in range(size)])  19.1 us
    all_to_all x3, starting transfers between devices, exchanged(): return lax.all_to_all(blocks, axis, 0, 0, tiled=False)  16.5 us
    ppermute x3, waiting for transfers between devices, local(): right, far, left = [lax.ppermute(panel, both, [(0, k)]) for k in (2, 4, 6)]  11.1 us
    pallas_call x1, Pallas kernels, factor_inverse(): step(first_factor_kernel, [shape(128, 128), shape(384, n)], [SMEM, VMEM,...  8.35 us
    pallas_call x1, Pallas kernels, factor_inverse(): step(second_factor_kernel, [shape(128, 256), shape(256, n)], [VMEM], [], 1)  7.27 us
  transfers between devices with their start and end apart: 23, of which 11 were waited for; matrix products, arithmetic and copies ran while one was open for 1% of the time, Pallas kernels for 18%

profile of v4, /device:TPU:8, one launch (start us, length us, event | category | flops | bytes accessed | tf_op | source)
XLA Modules:
  0.0 198.1 jit_solution(3009940760456321501)
XLA Ops:
  0.7 1.0 copy.12
  1.7 1.0 copy-done
  2.7 1.1 shard_map.77
  3.8 8.5 %all-to-all-start = ((f32[8,56,128]{2,1,0:T(8,128)}), f32[8,56,128]{2,1,0:T(8,128)S(1)}, u32[]{:S(2)}, u32[]{:S(2)}) async-start(f32[8,56,128]{2,1,0:T(8,128)} %shard_map.77), calls=%async_computation | async-start | bytes 458752 | tf_op jit(solution)/shard_map/all_to_all | solution.py:276
  12.3 11.2 %all-to-all-done.r_ref = f32[8,56,128]{2,1,0:T(8,128)S(1)} async-done(((f32[8,56,128]{2,1,0:T(8,128)}), f32[8,56,128]{2,1,0:T(8,128)S(1)}, u32[]{:S(2)}, u32[]{:S(2)}) %all-to-all-start) | async-done | bytes 229408 | tf_op jit(solution)/shard_map/all_to_all | solution.py:276
  23.4 0.6 shard_map.78
  24.0 2.8 %collective-permute-start.2 = (f32[56,128]{1,0:T(8,128)S(1)}, f32[56,128]{1,0:T(8,128)S(1)}, u32[]{:S(2)}, u32[]{:S(2)}) collective-permute-start(f32[56,128]{1,0:T(8,128)S(1)} %shard_map.78), channel_id=1, source_target_pairs={{0,192},{64,0},{128,64},{192,128},{1,193},{65,1},{129,65},{193,129... | collective-permute-start | bytes 86024 | tf_op jit(solution)/shard_map/ppermute | solution.py:284
  26.8 0.8 collective-permute-start.1
  27.6 0.9 collective-permute-start
  28.6 3.6 %collective-permute-done.1.t2 = f32[56,128]{1,0:T(8,128)S(1)} collective-permute-done((f32[56,128]{1,0:T(8,128)S(1)}, f32[56,128]{1,0:T(8,128)S(1)}, u32[]{:S(2)}, u32[]{:S(2)}) %collective-permute-start.1) | collective-permute-done | bytes 28704 | tf_op jit(solution)/shard_map/ppermute | solution.py:284
  32.7 0.9 copy-done.2
  33.6 1.2 shard_map.79
  34.8 12.2 %all_to_all.30.i_ref = f32[8,48,128]{2,1,0:T(8,128)S(1)} all-to-all(f32[8,48,128]{2,1,0:T(8,128)S(1)} %shard_map.79), channel_id=1, replica_groups=mesh['x'=4,'z'=8,'y'=4,'core'=2] {'z'}, dimensions={0} | all-to-all | bytes 393216 | tf_op jit(solution)/shard_map/all_to_all | solution.py:276
  47.0 1.6 shard_map.80
  48.6 0.7 collective-permute-start.5
  49.3 0.7 collective-permute-start.4
  50.0 1.3 collective-permute-start.3
  51.4 11.1 %collective-permute-done.3 = f32[128,512]{1,0:T(8,128)S(1)} collective-permute-done((f32[128,512]{1,0:T(8,128)S(1)}, f32[128,512]{1,0:T(8,128)S(1)}, u32[]{:S(2)}, u32[]{:S(2)}) %collective-permute-start.3) | collective-permute-done | bytes 262176 | tf_op jit(solution)/shard_map/ppermute | solution.py:318
  62.6 1.3 collective-permute-start.6
  63.9 1.1 collective-permute-done.6
  65.5 0.6 fusion.6
  66.2 0.6 fusion.8
  66.8 0.6 fusion.10
  67.4 1.6 collective-permute-start.7
  69.0 3.2 %collective-permute-start.9 = (f32[128,1024]{1,0:T(8,128)S(1)}, f32[128,1024]{1,0:T(8,128)}, u32[]{:S(2)}, u32[]{:S(2)}) collective-permute-start(f32[128,1024]{1,0:T(8,128)S(1)} %fusion.6), channel_id=1, source_target_pairs={{0,192},{64,0},{128,64},{192,128},{1,193},{65,1},{129,65},{193,129... | collective-permute-start | bytes 1572872 | tf_op jit(solution)/shard_map/ppermute | solution.py:284
  72.3 23.6 %all_to_all.31 = f32[32,8,128]{2,1,0:T(8,128)S(1)} all-to-all(f32[32,8,128]{2,1,0:T(8,128)S(1)} %bitcast.23), channel_id=1, replica_groups=mesh['x'=4,'z'=8,'y'=4,'core'=2] {'x','z'}, dimensions={0} | all-to-all | bytes 262144 | tf_op jit(solution)/shard_map/all_to_all | solution.py:276
  96.0 13.8 %all_to_all.32 = f32[32,8,128]{2,1,0:T(8,128)S(1)} all-to-all(f32[32,8,128]{2,1,0:T(8,128)S(1)} %broadcast_in_dim.7), channel_id=1, replica_groups=mesh['x'=4,'z'=8,'y'=4,'core'=2] {'x','z'}, dimensions={0} | all-to-all | bytes 262144 | tf_op jit(solution)/shard_map/all_to_all | solution.py:276
  109.9 1.9 collective-permute-start.10
  111.8 5.3 %collective-permute-done.12 = f32[256,128]{1,0:T(8,128)S(1)} collective-permute-done((f32[256,128]{1,0:T(8,128)S(1)}, f32[256,128]{1,0:T(8,128)S(1)}, u32[]{:S(2)}, u32[]{:S(2)}) %collective-permute-start.12) | collective-permute-done | bytes 131104 | tf_op jit(solution)/shard_map/ppermute | solution.py:284
  117.1 1.2 collective-permute-done.10
  118.4 2.7 %fusion.1 = f32[128,1024]{1,0:T(8,128)} fusion(f32[128,1024]{1,0:T(8,128)} %collective-permute-done.9, f32[128,1024]{1,0:T(8,128)} %collective-permute-done.8, f32[128,1024]{1,0:T(8,128)S(1)} %collective-permute-done.7, f32[128,1024]{1,0:T(8,128)S(1)} %get-tuple-element.22, f32[128,512]{1,0:T(8,128)S(1)} %fusion.2), kind=kOutput, calls=%fused_computation.2 | convolution fusion | flops 201719808 | bytes 2686976 | tf_op jit(solution)/shard_map/dot_general | solution.py:37
  121.1 3.5 %all-to-all-start.4 = ((f32[8,16,1024]{2,1,0:T(8,128)}), f32[8,16,1024]{2,1,0:T(8,128)S(1)}, u32[]{:S(2)}, u32[]{:S(2)}) async-start(f32[8,16,1024]{2,1,0:T(8,128)} %bitcast.13), calls=%async_computation.4 | async-start | bytes 1048576 | tf_op jit(solution)/shard_map/all_to_all | solution.py:276
  124.6 8.4 %shard_map.81 = (f32[128,128]{1,0:T(8,128)S(1)}, f32[384,512]{1,0:T(8,128)S(1)}) custom-call(s32[4]{0:T(128)S(1)} %pad_add_fusion.at_ref, f32[4,256,128]{2,1,0:T(8,128)S(1)} %pad_maximum_fusion.g_ref, f32[4,256,128]{2,1,0:T(8,128)S(1)} %collective-permute-done.13.m_ref), custom_call_target="tpu_custom_call" | custom-call | flops 10000000000 | bytes 1048576 | tf_op jit(solution)/shard_map/pallas_call | solution.py:229
  133.0 7.3 %shard_map.82 = (f32[128,256]{1,0:T(8,128)S(1)}, f32[256,512]{1,0:T(8,128)S(1)}) custom-call(f32[384,512]{1,0:T(8,128)S(1)} %get-tuple-element.25.z_ref), custom_call_target="tpu_custom_call" | custom-call | flops 10000000000 | bytes 1048576 | tf_op jit(solution)/shard_map/pallas_call | solution.py:230
  140.3 2.7 %all-to-all-done.4 = f32[8,16,1024]{2,1,0:T(8,128)S(1)} async-done(((f32[8,16,1024]{2,1,0:T(8,128)}), f32[8,16,1024]{2,1,0:T(8,128)S(1)}, u32[]{:S(2)}, u32[]{:S(2)}) %all-to-all-start.4) | async-done | bytes 524320 | tf_op jit(solution)/shard_map/all_to_all | solution.py:276
  143.1 0.8 broadcast_in_dim.8
  143.9 4.5 %all-to-all-start.5 = ((f32[8,16,1024]{2,1,0:T(8,128)}), f32[8,16,1024]{2,1,0:T(8,128)S(1)}, u32[]{:S(2)}, u32[]{:S(2)}) async-start(f32[8,16,1024]{2,1,0:T(8,128)} %broadcast_in_dim.8), calls=%async_computation.5 | async-start | bytes 1048576 | tf_op jit(solution)/shard_map/all_to_all | solution.py:276
  148.4 6.9 %shard_map.83 = (f32[128,384]{1,0:T(8,128)S(1)}, f32[128,512]{1,0:T(8,128)S(1)}) custom-call(f32[256,512]{1,0:T(8,128)S(1)} %get-tuple-element.27.z_ref), custom_call_target="tpu_custom_call" | custom-call | flops 10000000000 | bytes 1048576 | tf_op jit(solution)/shard_map/pallas_call | solution.py:231
  155.3 10.8 %all-to-all-done.5 = f32[8,16,1024]{2,1,0:T(8,128)S(1)} async-done(((f32[8,16,1024]{2,1,0:T(8,128)}), f32[8,16,1024]{2,1,0:T(8,128)S(1)}, u32[]{:S(2)}, u32[]{:S(2)}) %all-to-all-start.5) | async-done | bytes 524320 | tf_op jit(solution)/shard_map/all_to_all | solution.py:276
  166.2 1.3 collective-permute-start.16
  167.5 0.8 collective-permute-start.15
  168.3 1.5 collective-permute-start.14
  169.8 6.3 %shard_map.84.l3 = f32[128,512]{1,0:T(8,128)S(1)} custom-call(f32[128,512]{1,0:T(8,128)S(1)} %get-tuple-element.29.z_ref), custom_call_target="tpu_custom_call" | custom-call | flops 10000000000 | bytes 1048576 | tf_op jit(solution)/shard_map/pallas_call | solution.py:232
  176.1 1.9 collective-permute-start.19
  178.3 2.0 %collective-permute-start.17 = (f32[128,256]{1,0:T(8,128)S(1)}, f32[128,256]{1,0:T(8,128)S(1)}, u32[]{:S(2)}, u32[]{:S(2)}) collective-permute-start(f32[128,256]{1,0:T(8,128)S(1)} %slice.37.b0), channel_id=1, source_target_pairs={{0,128},{64,192},{128,0},{192,64},{1,129},{65,193},{129,1},{193,65... | collective-permute-start | bytes 393224 | tf_op jit(solution)/shard_map/ppermute | solution.py:284
  180.2 8.7 %collective-permute-done.15.b2 = f32[128,768]{1,0:T(8,128)S(1)} collective-permute-done((f32[128,768]{1,0:T(8,128)S(1)}, f32[128,768]{1,0:T(8,128)S(1)}, u32[]{:S(2)}, u32[]{:S(2)}) %collective-permute-start.15) | collective-permute-done | bytes 393248 | tf_op jit(solution)/shard_map/ppermute | solution.py:284
  188.9 6.5 %shard_map.85 = (f32[128,1024]{1,0:T(8,128)}, f32[512,1024]{1,0:T(8,128)}, f32[128,512]{1,0:T(8,128)S(1)}) custom-call(s32[4]{0:T(128)S(1)} %pad_add_fusion.at_ref, f32[128,128]{1,0:T(8,128)S(1)} %get-tuple-element.24.l0, f32[128,256]{1,0:T(8,128)S(1)} %get-tuple-element.26.l1, f32[128,384]{1,0:T(8,128)S(1)} %get-tuple-element.28.l2, ...), custom_call_target="tpu_custom_call" | custom-call | flops 2000000000 | bytes 3000000 | tf_op jit(solution)/shard_map/pallas_call | solution.py:354
  195.5 2.6 %shard_map.86 = (f32[128,1024]{1,0:T(8,128)}, f32[512,1024]{1,0:T(8,128)}) custom-call(s32[4]{0:T(128)S(1)} %pad_add_fusion.at_ref, f32[128,128]{1,0:T(8,128)S(1)} %get-tuple-element.24.l0, f32[128,256]{1,0:T(8,128)S(1)} %get-tuple-element.26.l1, f32[128,384]{1,0:T(8,128)S(1)} %get-tuple-element.28.l2, ...), custom_call_target="tpu_custom_call", output_to_operand_aliasing={{0}: (11, {}), {1}: (12, {})} | custom-call | flops 2000000000 | bytes 3000000 | tf_op jit(solution)/shard_map/pallas_call | solution.py:364
  (43 shorter events, 2.0 us)
Async XLA Ops:
  0.6 46.4 %copy-start.4 = (s32[4]{0:T(128)S(1)}, s32[4]{0:T(128)}, u32[]{:S(2)}) copy-start(s32[4]{0:T(128)} %n_ref.1) | copy-start | bytes 52
  0.6 46.4 %copy-start.5 = (s32[128]{0:T(128)S(1)}, s32[128]{0:T(128)}, u32[]{:S(2)}) copy-start(s32[128]{0:T(128)} %param.10) | copy-start | bytes 1540
  0.7 46.4 %copy-start.3 = (f32[6,128]{1,0:T(8,128)S(1)}, f32[6,128]{1,0:T(8,128)}, u32[]{:S(2)}) copy-start(f32[6,128]{1,0:T(8,128)} %p_ref.1) | copy-start | bytes 9220
  1.7 1.0 copy-start
  2.7 44.4 %copy-start.1 = (bf16[4,48,1024]{2,1,0:T(8,128)(2,1)S(1)}, bf16[4,48,1024]{2,1,0:T(8,128)(2,1)}, u32[]{:S(2)}) copy-start(bf16[4,48,1024]{2,1,0:T(8,128)(2,1)} %f_ref.3) | copy-start | bytes 1179652
  3.8 19.6 %all-to-all-start = ((f32[8,56,128]{2,1,0:T(8,128)}), f32[8,56,128]{2,1,0:T(8,128)S(1)}, u32[]{:S(2)}, u32[]{:S(2)}) async-start(f32[8,56,128]{2,1,0:T(8,128)} %shard_map.77), calls=%async_computation | async-start | bytes 458752 | tf_op jit(solution)/shard_map/all_to_all | solution.py:276
  24.0 4.6 %collective-permute-start.2 = (f32[56,128]{1,0:T(8,128)S(1)}, f32[56,128]{1,0:T(8,128)S(1)}, u32[]{:S(2)}, u32[]{:S(2)}) collective-permute-start(f32[56,128]{1,0:T(8,128)S(1)} %shard_map.78), channel_id=1, source_target_pairs={{0,192},{64,0},{128,64},{192,128},{1,193},{65,1},{129,65},{193,129... | collective-permute-start | bytes 86024 | tf_op jit(solution)/shard_map/ppermute | solution.py:284
  26.8 5.4 %collective-permute-start.1 = (f32[56,128]{1,0:T(8,128)S(1)}, f32[56,128]{1,0:T(8,128)S(1)}, u32[]{:S(2)}, u32[]{:S(2)}) collective-permute-start(f32[56,128]{1,0:T(8,128)S(1)} %shard_map.78), channel_id=1, source_target_pairs={{0,128},{64,192},{128,0},{192,64},{1,129},{65,193},{129,1},{193,65... | collective-permute-start | bytes 86024 | tf_op jit(solution)/shard_map/ppermute | solution.py:284
  27.6 5.1 %collective-permute-start = (f32[56,128]{1,0:T(8,128)S(1)}, f32[56,128]{1,0:T(8,128)S(1)}, u32[]{:S(2)}, u32[]{:S(2)}) collective-permute-start(f32[56,128]{1,0:T(8,128)S(1)} %shard_map.78), channel_id=1, source_target_pairs={{0,64},{64,128},{128,192},{192,0},{1,65},{65,129},{129,193},{193,1... | collective-permute-start | bytes 86024 | tf_op jit(solution)/shard_map/ppermute | solution.py:284
  32.7 0.9 copy-start.2
  48.6 2.7 %collective-permute-start.5 = (f32[128,512]{1,0:T(8,128)S(1)}, f32[128,512]{1,0:T(8,128)S(1)}, u32[]{:S(2)}, u32[]{:S(2)}) collective-permute-start(f32[128,512]{1,0:T(8,128)S(1)} %get-tuple-element.19), channel_id=1, source_target_pairs={{0,6},{8,14},{16,22},{24,30},{32,38},{40,46},{48,54},{56,62},{64,7... | collective-permute-start | bytes 786440 | tf_op jit(solution)/shard_map/ppermute | solution.py:318
  49.3 2.0 %collective-permute-start.4 = (f32[128,512]{1,0:T(8,128)S(1)}, f32[128,512]{1,0:T(8,128)S(1)}, u32[]{:S(2)}, u32[]{:S(2)}) collective-permute-start(f32[128,512]{1,0:T(8,128)S(1)} %get-tuple-element.19), channel_id=1, source_target_pairs={{0,4},{8,12},{16,20},{24,28},{32,36},{40,44},{48,52},{56,60},{64,6... | collective-permute-start | bytes 786440 | tf_op jit(solution)/shard_map/ppermute | solution.py:318
  50.0 12.5 %collective-permute-start.3 = (f32[128,512]{1,0:T(8,128)S(1)}, f32[128,512]{1,0:T(8,128)S(1)}, u32[]{:S(2)}, u32[]{:S(2)}) collective-permute-start(f32[128,512]{1,0:T(8,128)S(1)} %get-tuple-element.19), channel_id=1, source_target_pairs={{0,2},{8,10},{16,18},{24,26},{32,34},{40,42},{48,50},{56,58},{64,6... | collective-permute-start | bytes 786440 | tf_op jit(solution)/shard_map/ppermute | solution.py:318
  62.6 2.4 %collective-permute-start.6 = (f32[128,512]{1,0:T(8,128)S(1)}, f32[128,512]{1,0:T(8,128)S(1)}, u32[]{:S(2)}, u32[]{:S(2)}) collective-permute-start(f32[128,512]{1,0:T(8,128)S(1)} %select_select_fusion), channel_id=1, source_target_pairs={{0,1},{2,3},{4,5},{6,7},{8,9},{10,11},{12,13},{14,15},{16,17},{18,... | collective-permute-start | bytes 786440 | tf_op jit(solution)/shard_map/ppermute | solution.py:320
  67.4 42.3 %collective-permute-start.7 = (f32[128,1024]{1,0:T(8,128)S(1)}, f32[128,1024]{1,0:T(8,128)S(1)}, u32[]{:S(2)}, u32[]{:S(2)}) collective-permute-start(f32[128,1024]{1,0:T(8,128)S(1)} %fusion.10), channel_id=1, source_target_pairs={{0,128},{64,192},{128,0},{192,64},{1,129},{65,193},{129,1},{193,65... | collective-permute-start | bytes 1572872 | tf_op jit(solution)/shard_map/ppermute | solution.py:284
  69.0 40.7 %collective-permute-start.8 = (f32[128,1024]{1,0:T(8,128)S(1)}, f32[128,1024]{1,0:T(8,128)}, u32[]{:S(2)}, u32[]{:S(2)}) collective-permute-start(f32[128,1024]{1,0:T(8,128)S(1)} %fusion.8), channel_id=1, source_target_pairs={{0,64},{64,128},{128,192},{192,0},{1,65},{65,129},{129,193},{193,1... | collective-permute-start | bytes 1572872 | tf_op jit(solution)/shard_map/ppermute | solution.py:284
  69.0 40.7 %collective-permute-start.9 = (f32[128,1024]{1,0:T(8,128)S(1)}, f32[128,1024]{1,0:T(8,128)}, u32[]{:S(2)}, u32[]{:S(2)}) collective-permute-start(f32[128,1024]{1,0:T(8,128)S(1)} %fusion.6), channel_id=1, source_target_pairs={{0,192},{64,0},{128,64},{192,128},{1,193},{65,1},{129,65},{193,129... | collective-permute-start | bytes 1572872 | tf_op jit(solution)/shard_map/ppermute | solution.py:284
  109.7 7.4 %collective-permute-start.12 = (f32[256,128]{1,0:T(8,128)S(1)}, f32[256,128]{1,0:T(8,128)S(1)}, u32[]{:S(2)}, u32[]{:S(2)}) collective-permute-start(f32[256,128]{1,0:T(8,128)S(1)} %bitcast.24), channel_id=1, source_target_pairs={{0,6},{2,0},{4,2},{6,4},{1,7},{3,1},{5,3},{7,5},{8,14},{10,8},{12,... | collective-permute-start | bytes 393224 | tf_op jit(solution)/shard_map/ppermute | solution.py:284
  109.8 7.3 %collective-permute-start.11 = (f32[256,128]{1,0:T(8,128)S(1)}, f32[256,128]{1,0:T(8,128)S(1)}, u32[]{:S(2)}, u32[]{:S(2)}) collective-permute-start(f32[256,128]{1,0:T(8,128)S(1)} %bitcast.25), channel_id=1, source_target_pairs={{0,4},{2,6},{4,0},{6,2},{1,5},{3,7},{5,1},{7,3},{8,12},{10,14},{12... | collective-permute-start | bytes 393224 | tf_op jit(solution)/shard_map/ppermute | solution.py:284
  109.9 8.3 %collective-permute-start.10 = (f32[256,128]{1,0:T(8,128)S(1)}, f32[256,128]{1,0:T(8,128)S(1)}, u32[]{:S(2)}, u32[]{:S(2)}) collective-permute-start(f32[256,128]{1,0:T(8,128)S(1)} %bitcast.26), channel_id=1, source_target_pairs={{0,2},{2,4},{4,6},{6,0},{1,3},{3,5},{5,7},{7,1},{8,10},{10,12},{12... | collective-permute-start | bytes 393224 | tf_op jit(solution)/shard_map/ppermute | solution.py:284
  118.3 6.4 %collective-permute-start.13 = (f32[4,256,128]{2,1,0:T(8,128)S(1)}, f32[4,256,128]{2,1,0:T(8,128)S(1)}, u32[]{:S(2)}, u32[]{:S(2)}) collective-permute-start(f32[4,256,128]{2,1,0:T(8,128)S(1)} %pad_maximum_fusion.g_ref), channel_id=1, source_target_pairs={{0,1},{1,0},{2,3},{3,2},{4,5},{5,4},{6,7},{7,6},{8,9},{9,8},{10,11... | collective-permute-start | bytes 1572872 | tf_op jit(solution)/shard_map/ppermute | solution.py:340
  121.1 21.9 %all-to-all-start.4 = ((f32[8,16,1024]{2,1,0:T(8,128)}), f32[8,16,1024]{2,1,0:T(8,128)S(1)}, u32[]{:S(2)}, u32[]{:S(2)}) async-start(f32[8,16,1024]{2,1,0:T(8,128)} %bitcast.13), calls=%async_computation.4 | async-start | bytes 1048576 | tf_op jit(solution)/shard_map/all_to_all | solution.py:276
  143.9 22.3 %all-to-all-start.5 = ((f32[8,16,1024]{2,1,0:T(8,128)}), f32[8,16,1024]{2,1,0:T(8,128)S(1)}, u32[]{:S(2)}, u32[]{:S(2)}) async-start(f32[8,16,1024]{2,1,0:T(8,128)} %broadcast_in_dim.8), calls=%async_computation.5 | async-start | bytes 1048576 | tf_op jit(solution)/shard_map/all_to_all | solution.py:276
  166.2 12.1 %collective-permute-start.16 = (f32[128,768]{1,0:T(8,128)S(1)}, f32[128,768]{1,0:T(8,128)S(1)}, u32[]{:S(2)}, u32[]{:S(2)}) collective-permute-start(f32[128,768]{1,0:T(8,128)S(1)} %slice.36.b0), channel_id=1, source_target_pairs={{0,192},{64,0},{128,64},{192,128},{1,193},{65,1},{129,65},{193,129... | collective-permute-start | bytes 1179656 | tf_op jit(solution)/shard_map/ppermute | solution.py:284
  167.5 21.4 %collective-permute-start.15 = (f32[128,768]{1,0:T(8,128)S(1)}, f32[128,768]{1,0:T(8,128)S(1)}, u32[]{:S(2)}, u32[]{:S(2)}) collective-permute-start(f32[128,768]{1,0:T(8,128)S(1)} %slice.36.b0), channel_id=1, source_target_pairs={{0,64},{64,128},{128,192},{192,0},{1,65},{65,129},{129,193},{193,1... | collective-permute-start | bytes 1179656 | tf_op jit(solution)/shard_map/ppermute | solution.py:284
  168.3 20.6 %collective-permute-start.14 = (f32[128,768]{1,0:T(8,128)S(1)}, f32[128,768]{1,0:T(8,128)S(1)}, u32[]{:S(2)}, u32[]{:S(2)}) collective-permute-start(f32[128,768]{1,0:T(8,128)S(1)} %slice.36.b0), channel_id=1, source_target_pairs={{0,128},{64,192},{128,0},{192,64},{1,129},{65,193},{129,1},{193,65... | collective-permute-start | bytes 1179656 | tf_op jit(solution)/shard_map/ppermute | solution.py:284
  176.1 19.4 %collective-permute-start.19 = (f32[128,256]{1,0:T(8,128)S(1)}, f32[128,256]{1,0:T(8,128)S(1)}, u32[]{:S(2)}, u32[]{:S(2)}) collective-permute-start(f32[128,256]{1,0:T(8,128)S(1)} %slice.37.b0), channel_id=1, source_target_pairs={{0,192},{64,0},{128,64},{192,128},{1,193},{65,1},{129,65},{193,129... | collective-permute-start | bytes 393224 | tf_op jit(solution)/shard_map/ppermute | solution.py:284
  178.0 17.5 %collective-permute-start.18 = (f32[128,256]{1,0:T(8,128)S(1)}, f32[128,256]{1,0:T(8,128)S(1)}, u32[]{:S(2)}, u32[]{:S(2)}) collective-permute-start(f32[128,256]{1,0:T(8,128)S(1)} %slice.37.b0), channel_id=1, source_target_pairs={{0,64},{64,128},{128,192},{192,0},{1,65},{65,129},{129,193},{193,1... | collective-permute-start | bytes 393224 | tf_op jit(solution)/shard_map/ppermute | solution.py:284
  178.3 17.2 %collective-permute-start.17 = (f32[128,256]{1,0:T(8,128)S(1)}, f32[128,256]{1,0:T(8,128)S(1)}, u32[]{:S(2)}, u32[]{:S(2)}) collective-permute-start(f32[128,256]{1,0:T(8,128)S(1)} %slice.37.b0), channel_id=1, source_target_pairs={{0,128},{64,192},{128,0},{192,64},{1,129},{65,193},{129,1},{193,65... | collective-permute-start | bytes 393224 | tf_op jit(solution)/shard_map/ppermute | solution.py:284

commit v5 on v3

--- a/solution.py
+++ b/solution.py
@@ -271,6 +271,14 @@
     lax.fori_loop(0, m_ref.shape[1] // 256, columns, 0)
 
 
+def sum_tile_kernel(a_ref, o_ref):
+    total = a_ref[0]
+    for z in range(1, Z):
+        total = total + a_ref[z]
+    for z in range(Z):
+        o_ref[z] = total
+
+
 def exchanged(blocks, axis):
     return lax.all_to_all(blocks, axis, 0, 0, tiled=False)
 
@@ -340,8 +348,8 @@
 
     products = parts[0] + sent[0] + sent[1] + sent[2]
     products = exchanged(products.reshape(Z, tile, width), "z")
-    products = products.sum(0)
-    products = everywhere(products, "z", Z)
+    products = call(sum_tile_kernel, jax.ShapeDtypeStruct((Z, tile, width), f32), 1, (10**6, 10**6))(products)
+    products = exchanged(products, "z")
     products = products.reshape(step, width)
     a = [products[:, :mid]]
     a += [shift(a[0], "x", X, k) for k in (2, 1, 3)]

time: 213 us -> 213 us (level)
  no operation moved by 1% of the time
where the time goes in v5:
time: 213 us; the launch traced here: 211 us
  waiting for transfers between devices  68 us (32%)
  blocking collectives  49.6 us (23%)
  Pallas kernels  43.4 us (20%)
  starting transfers between devices  40.2 us (19%)
  matrix products  4.95 us (2%)
  local copies, waits for them, and re-layouts  4.05 us (2%)
    all_to_all x3, blocking collectives, exchanged(): return lax.all_to_all(blocks, axis, 0, 0, tiled=False)  49.6 us
    all_to_all x3, waiting for transfers between devices, exchanged(): return lax.all_to_all(blocks, axis, 0, 0, tiled=False)  31.9 us
    ppermute x15, waiting for transfers between devices, shift(): lax.ppermute(block, axis, [(i, (i + by) % size) for i in range(size)])  23.8 us
    ppermute x15, starting transfers between devices, shift(): lax.ppermute(block, axis, [(i, (i + by) % size) for i in range(size)])  20 us
    all_to_all x3, starting transfers between devices, exchanged(): return lax.all_to_all(blocks, axis, 0, 0, tiled=False)  16.1 us
    ppermute x3, waiting for transfers between devices, local(): right, far, left = [lax.ppermute(panel, both, [(0, k)]) for k in (2, 4, 6)]  11.1 us
    pallas_call x1, Pallas kernels, factor_inverse(): step(first_factor_kernel, [shape(128, 128), shape(384, n)], [SMEM, VMEM,...  8.35 us
    pallas_call x1, Pallas kernels, factor_inverse(): step(second_factor_kernel, [shape(128, 256), shape(256, n)], [VMEM], [], 1)  7.27 us
  transfers between devices with their start and end apart: 23, of which 10 were waited for; matrix products, arithmetic and copies ran while one was open for 1% of the time, Pallas kernels for 16%

profile of v5, /device:TPU:8, one launch (start us, length us, event | category | flops | bytes accessed | tf_op | source)
XLA Modules:
  0.0 211.3 jit_solution(10291223270596663026)
XLA Ops:
  0.7 1.0 copy.12
  1.7 1.0 copy-done
  2.7 1.1 shard_map.77
  3.8 8.5 %all-to-all-start = ((f32[8,56,128]{2,1,0:T(8,128)}), f32[8,56,128]{2,1,0:T(8,128)S(1)}, u32[]{:S(2)}, u32[]{:S(2)}) async-start(f32[8,56,128]{2,1,0:T(8,128)} %shard_map.77), calls=%async_computation | async-start | bytes 458752 | tf_op jit(solution)/shard_map/all_to_all | solution.py:283
  12.3 11.2 %all-to-all-done.r_ref = f32[8,56,128]{2,1,0:T(8,128)S(1)} async-done(((f32[8,56,128]{2,1,0:T(8,128)}), f32[8,56,128]{2,1,0:T(8,128)S(1)}, u32[]{:S(2)}, u32[]{:S(2)}) %all-to-all-start) | async-done | bytes 229408 | tf_op jit(solution)/shard_map/all_to_all | solution.py:283
  24.0 2.8 %collective-permute-start.2 = (f32[56,128]{1,0:T(8,128)S(1)}, f32[56,128]{1,0:T(8,128)S(1)}, u32[]{:S(2)}, u32[]{:S(2)}) collective-permute-start(f32[56,128]{1,0:T(8,128)S(1)} %shard_map.78), channel_id=1, source_target_pairs={{0,192},{64,0},{128,64},{192,128},{1,193},{65,1},{129,65},{193,129... | collective-permute-start | bytes 86024 | tf_op jit(solution)/shard_map/ppermute | solution.py:291
  26.8 0.8 collective-permute-start.1
  27.6 0.9 collective-permute-start
  28.6 3.6 %collective-permute-done.1.t2 = f32[56,128]{1,0:T(8,128)S(1)} collective-permute-done((f32[56,128]{1,0:T(8,128)S(1)}, f32[56,128]{1,0:T(8,128)S(1)}, u32[]{:S(2)}, u32[]{:S(2)}) %collective-permute-start.1) | collective-permute-done | bytes 28704 | tf_op jit(solution)/shard_map/ppermute | solution.py:291
  32.7 0.9 copy-done.2
  33.6 1.2 shard_map.79
  34.8 12.2 %all_to_all.30.i_ref = f32[8,48,128]{2,1,0:T(8,128)S(1)} all-to-all(f32[8,48,128]{2,1,0:T(8,128)S(1)} %shard_map.79), channel_id=1, replica_groups=mesh['x'=4,'z'=8,'y'=4,'core'=2] {'z'}, dimensions={0} | all-to-all | bytes 393216 | tf_op jit(solution)/shard_map/all_to_all | solution.py:283
  47.0 1.6 shard_map.80
  48.6 0.7 collective-permute-start.5
  49.3 0.7 collective-permute-start.4
  50.0 1.3 collective-permute-start.3
  51.4 11.1 %collective-permute-done.3 = f32[128,512]{1,0:T(8,128)S(1)} collective-permute-done((f32[128,512]{1,0:T(8,128)S(1)}, f32[128,512]{1,0:T(8,128)S(1)}, u32[]{:S(2)}, u32[]{:S(2)}) %collective-permute-start.3) | collective-permute-done | bytes 262176 | tf_op jit(solution)/shard_map/ppermute | solution.py:325
  62.6 1.3 collective-permute-start.6
  63.9 1.1 collective-permute-done.6
  65.5 0.6 fusion.6
  66.2 0.6 fusion.8
  67.4 1.6 collective-permute-start.7
  69.0 3.2 %collective-permute-start.9 = (f32[128,1024]{1,0:T(8,128)S(1)}, f32[128,1024]{1,0:T(8,128)}, u32[]{:S(2)}, u32[]{:S(2)}) collective-permute-start(f32[128,1024]{1,0:T(8,128)S(1)} %fusion.6), channel_id=1, source_target_pairs={{0,192},{64,0},{128,64},{192,128},{1,193},{65,1},{129,65},{193,129... | collective-permute-start | bytes 1572872 | tf_op jit(solution)/shard_map/ppermute | solution.py:291
  72.3 23.6 %all_to_all.31 = f32[32,8,128]{2,1,0:T(8,128)S(1)} all-to-all(f32[32,8,128]{2,1,0:T(8,128)S(1)} %bitcast.21), channel_id=1, replica_groups=mesh['x'=4,'z'=8,'y'=4,'core'=2] {'x','z'}, dimensions={0} | all-to-all | bytes 262144 | tf_op jit(solution)/shard_map/all_to_all | solution.py:283
  96.0 13.8 %all_to_all.32 = f32[32,8,128]{2,1,0:T(8,128)S(1)} all-to-all(f32[32,8,128]{2,1,0:T(8,128)S(1)} %broadcast_in_dim.10), channel_id=1, replica_groups=mesh['x'=4,'z'=8,'y'=4,'core'=2] {'x','z'}, dimensions={0} | all-to-all | bytes 262144 | tf_op jit(solution)/shard_map/all_to_all | solution.py:283
  109.9 1.9 collective-permute-start.10
  111.8 5.3 %collective-permute-done.12 = f32[256,128]{1,0:T(8,128)S(1)} collective-permute-done((f32[256,128]{1,0:T(8,128)S(1)}, f32[256,128]{1,0:T(8,128)S(1)}, u32[]{:S(2)}, u32[]{:S(2)}) %collective-permute-start.12) | collective-permute-done | bytes 131104 | tf_op jit(solution)/shard_map/ppermute | solution.py:291
  117.1 1.2 collective-permute-done.10
  118.4 2.7 %fusion.1 = f32[128,1024]{1,0:T(8,128)} fusion(f32[128,1024]{1,0:T(8,128)} %collective-permute-done.9, f32[128,1024]{1,0:T(8,128)} %collective-permute-done.8, f32[128,1024]{1,0:T(8,128)S(1)} %collective-permute-done.7, f32[128,1024]{1,0:T(8,128)S(1)} %get-tuple-element.22, f32[128,512]{1,0:T(8,128)S(1)} %fusion.2), kind=kOutput, calls=%fused_computation.2 | convolution fusion | flops 201719808 | bytes 2686976 | tf_op jit(solution)/shard_map/dot_general | solution.py:37
  121.1 3.5 %all-to-all-start.4 = ((f32[8,16,1024]{2,1,0:T(8,128)}), f32[8,16,1024]{2,1,0:T(8,128)S(1)}, u32[]{:S(2)}, u32[]{:S(2)}) async-start(f32[8,16,1024]{2,1,0:T(8,128)} %bitcast.13), calls=%async_computation.4 | async-start | bytes 1048576 | tf_op jit(solution)/shard_map/all_to_all | solution.py:283
  124.6 8.4 %shard_map.81 = (f32[128,128]{1,0:T(8,128)S(1)}, f32[384,512]{1,0:T(8,128)S(1)}) custom-call(s32[4]{0:T(128)S(1)} %pad_add_fusion.at_ref, f32[4,256,128]{2,1,0:T(8,128)S(1)} %pad_maximum_fusion.g_ref, f32[4,256,128]{2,1,0:T(8,128)S(1)} %collective-permute-done.13.m_ref), custom_call_target="tpu_custom_call" | custom-call | flops 10000000000 | bytes 1048576 | tf_op jit(solution)/shard_map/pallas_call | solution.py:229
  133.0 10.0 %all-to-all-done.4.a_ref = f32[8,16,1024]{2,1,0:T(8,128)S(1)} async-done(((f32[8,16,1024]{2,1,0:T(8,128)}), f32[8,16,1024]{2,1,0:T(8,128)S(1)}, u32[]{:S(2)}, u32[]{:S(2)}) %all-to-all-start.4) | async-done | bytes 524320 | tf_op jit(solution)/shard_map/all_to_all | solution.py:283
  143.0 0.8 shard_map.85
  143.9 4.2 %all-to-all-start.5 = ((f32[8,16,1024]{2,1,0:T(8,128)}), f32[8,16,1024]{2,1,0:T(8,128)}, u32[]{:S(2)}, u32[]{:S(2)}) async-start(f32[8,16,1024]{2,1,0:T(8,128)} %shard_map.85), calls=%async_computation.5 | async-start | bytes 1048576 | tf_op jit(solution)/shard_map/all_to_all | solution.py:283
  148.0 7.3 %shard_map.82 = (f32[128,256]{1,0:T(8,128)S(1)}, f32[256,512]{1,0:T(8,128)S(1)}) custom-call(f32[384,512]{1,0:T(8,128)S(1)} %get-tuple-element.25.z_ref), custom_call_target="tpu_custom_call" | custom-call | flops 10000000000 | bytes 1048576 | tf_op jit(solution)/shard_map/pallas_call | solution.py:230
  155.3 10.7 %all-to-all-done.5 = f32[8,16,1024]{2,1,0:T(8,128)} async-done(((f32[8,16,1024]{2,1,0:T(8,128)}), f32[8,16,1024]{2,1,0:T(8,128)}, u32[]{:S(2)}, u32[]{:S(2)}) %all-to-all-start.5) | async-done | bytes 524320 | tf_op jit(solution)/shard_map/all_to_all | solution.py:283
  166.0 1.1 fusion.14
  167.1 1.5 collective-permute-start.16
  168.6 7.0 %shard_map.83 = (f32[128,384]{1,0:T(8,128)S(1)}, f32[128,512]{1,0:T(8,128)S(1)}) custom-call(f32[256,512]{1,0:T(8,128)S(1)} %get-tuple-element.27.z_ref), custom_call_target="tpu_custom_call" | custom-call | flops 10000000000 | bytes 1048576 | tf_op jit(solution)/shard_map/pallas_call | solution.py:231
  175.6 0.9 collective-permute-start.19
  176.5 1.2 collective-permute-start.18
  177.7 1.4 collective-permute-start.17
  179.1 1.4 collective-permute-start.15
  180.6 2.1 collective-permute-start.14
  182.6 6.3 %shard_map.84.l3 = f32[128,512]{1,0:T(8,128)S(1)} custom-call(f32[128,512]{1,0:T(8,128)S(1)} %get-tuple-element.29.z_ref), custom_call_target="tpu_custom_call" | custom-call | flops 10000000000 | bytes 1048576 | tf_op jit(solution)/shard_map/pallas_call | solution.py:232
  188.9 13.3 %collective-permute-done.15.b2 = f32[128,512]{1,0:T(8,128)S(1)} collective-permute-done((f32[128,512]{1,0:T(8,128)S(1)}, f32[128,512]{1,0:T(8,128)S(1)}, u32[]{:S(2)}, u32[]{:S(2)}) %collective-permute-start.15) | collective-permute-done | bytes 262176 | tf_op jit(solution)/shard_map/ppermute | solution.py:291
  202.2 4.9 %shard_map.86 = (f32[128,1024]{1,0:T(8,128)}, f32[512,1024]{1,0:T(8,128)}, f32[128,512]{1,0:T(8,128)S(1)}) custom-call(s32[4]{0:T(128)S(1)} %pad_add_fusion.at_ref, f32[128,128]{1,0:T(8,128)S(1)} %get-tuple-element.24.l0, f32[128,256]{1,0:T(8,128)S(1)} %get-tuple-element.26.l1, f32[128,384]{1,0:T(8,128)S(1)} %get-tuple-element.28.l2, ...), custom_call_target="tpu_custom_call" | custom-call | flops 2000000000 | bytes 3000000 | tf_op jit(solution)/shard_map/pallas_call | solution.py:361
  207.1 4.2 %shard_map.87 = (f32[128,1024]{1,0:T(8,128)}, f32[512,1024]{1,0:T(8,128)}) custom-call(s32[4]{0:T(128)S(1)} %pad_add_fusion.at_ref, f32[128,128]{1,0:T(8,128)S(1)} %get-tuple-element.24.l0, f32[128,256]{1,0:T(8,128)S(1)} %get-tuple-element.26.l1, f32[128,384]{1,0:T(8,128)S(1)} %get-tuple-element.28.l2, ...), custom_call_target="tpu_custom_call", output_to_operand_aliasing={{0}: (11, {}), {1}: (12, {})} | custom-call | flops 2000000000 | bytes 3000000 | tf_op jit(solution)/shard_map/pallas_call | solution.py:371
  (40 shorter events, 2.8 us)
Async XLA Ops:
  0.6 46.4 %copy-start.4 = (s32[4]{0:T(128)S(1)}, s32[4]{0:T(128)}, u32[]{:S(2)}) copy-start(s32[4]{0:T(128)} %n_ref.1) | copy-start | bytes 52
  0.6 46.4 %copy-start.5 = (s32[128]{0:T(128)S(1)}, s32[128]{0:T(128)}, u32[]{:S(2)}) copy-start(s32[128]{0:T(128)} %param.10) | copy-start | bytes 1540
  0.7 46.4 %copy-start.3 = (f32[6,128]{1,0:T(8,128)S(1)}, f32[6,128]{1,0:T(8,128)}, u32[]{:S(2)}) copy-start(f32[6,128]{1,0:T(8,128)} %p_ref.1) | copy-start | bytes 9220
  1.7 1.0 copy-start
  2.7 44.4 %copy-start.1 = (bf16[4,48,1024]{2,1,0:T(8,128)(2,1)S(1)}, bf16[4,48,1024]{2,1,0:T(8,128)(2,1)}, u32[]{:S(2)}) copy-start(bf16[4,48,1024]{2,1,0:T(8,128)(2,1)} %f_ref.3) | copy-start | bytes 1179652
  3.8 19.6 %all-to-all-start = ((f32[8,56,128]{2,1,0:T(8,128)}), f32[8,56,128]{2,1,0:T(8,128)S(1)}, u32[]{:S(2)}, u32[]{:S(2)}) async-start(f32[8,56,128]{2,1,0:T(8,128)} %shard_map.77), calls=%async_computation | async-start | bytes 458752 | tf_op jit(solution)/shard_map/all_to_all | solution.py:283
  24.0 4.6 %collective-permute-start.2 = (f32[56,128]{1,0:T(8,128)S(1)}, f32[56,128]{1,0:T(8,128)S(1)}, u32[]{:S(2)}, u32[]{:S(2)}) collective-permute-start(f32[56,128]{1,0:T(8,128)S(1)} %shard_map.78), channel_id=1, source_target_pairs={{0,192},{64,0},{128,64},{192,128},{1,193},{65,1},{129,65},{193,129... | collective-permute-start | bytes 86024 | tf_op jit(solution)/shard_map/ppermute | solution.py:291
  26.8 5.4 %collective-permute-start.1 = (f32[56,128]{1,0:T(8,128)S(1)}, f32[56,128]{1,0:T(8,128)S(1)}, u32[]{:S(2)}, u32[]{:S(2)}) collective-permute-start(f32[56,128]{1,0:T(8,128)S(1)} %shard_map.78), channel_id=1, source_target_pairs={{0,128},{64,192},{128,0},{192,64},{1,129},{65,193},{129,1},{193,65... | collective-permute-start | bytes 86024 | tf_op jit(solution)/shard_map/ppermute | solution.py:291
  27.6 5.1 %collective-permute-start = (f32[56,128]{1,0:T(8,128)S(1)}, f32[56,128]{1,0:T(8,128)S(1)}, u32[]{:S(2)}, u32[]{:S(2)}) collective-permute-start(f32[56,128]{1,0:T(8,128)S(1)} %shard_map.78), channel_id=1, source_target_pairs={{0,64},{64,128},{128,192},{192,0},{1,65},{65,129},{129,193},{193,1... | collective-permute-start | bytes 86024 | tf_op jit(solution)/shard_map/ppermute | solution.py:291
  32.7 0.9 copy-start.2
  48.6 2.7 %collective-permute-start.5 = (f32[128,512]{1,0:T(8,128)S(1)}, f32[128,512]{1,0:T(8,128)S(1)}, u32[]{:S(2)}, u32[]{:S(2)}) collective-permute-start(f32[128,512]{1,0:T(8,128)S(1)} %get-tuple-element.19), channel_id=1, source_target_pairs={{0,6},{8,14},{16,22},{24,30},{32,38},{40,46},{48,54},{56,62},{64,7... | collective-permute-start | bytes 786440 | tf_op jit(solution)/shard_map/ppermute | solution.py:325
  49.3 2.0 collective-permute-start.4
  50.0 12.5 %collective-permute-start.3 = (f32[128,512]{1,0:T(8,128)S(1)}, f32[128,512]{1,0:T(8,128)S(1)}, u32[]{:S(2)}, u32[]{:S(2)}) collective-permute-start(f32[128,512]{1,0:T(8,128)S(1)} %get-tuple-element.19), channel_id=1, source_target_pairs={{0,2},{8,10},{16,18},{24,26},{32,34},{40,42},{48,50},{56,58},{64,6... | collective-permute-start | bytes 786440 | tf_op jit(solution)/shard_map/ppermute | solution.py:325
  62.6 2.4 %collective-permute-start.6 = (f32[128,512]{1,0:T(8,128)S(1)}, f32[128,512]{1,0:T(8,128)S(1)}, u32[]{:S(2)}, u32[]{:S(2)}) collective-permute-start(f32[128,512]{1,0:T(8,128)S(1)} %select_select_fusion), channel_id=1, source_target_pairs={{0,1},{2,3},{4,5},{6,7},{8,9},{10,11},{12,13},{14,15},{16,17},{18,... | collective-permute-start | bytes 786440 | tf_op jit(solution)/shard_map/ppermute | solution.py:327
  67.4 42.3 %collective-permute-start.7 = (f32[128,1024]{1,0:T(8,128)S(1)}, f32[128,1024]{1,0:T(8,128)S(1)}, u32[]{:S(2)}, u32[]{:S(2)}) collective-permute-start(f32[128,1024]{1,0:T(8,128)S(1)} %fusion.10), channel_id=1, source_target_pairs={{0,128},{64,192},{128,0},{192,64},{1,129},{65,193},{129,1},{193,65... | collective-permute-start | bytes 1572872 | tf_op jit(solution)/shard_map/ppermute | solution.py:291
  69.0 40.7 %collective-permute-start.8 = (f32[128,1024]{1,0:T(8,128)S(1)}, f32[128,1024]{1,0:T(8,128)}, u32[]{:S(2)}, u32[]{:S(2)}) collective-permute-start(f32[128,1024]{1,0:T(8,128)S(1)} %fusion.8), channel_id=1, source_target_pairs={{0,64},{64,128},{128,192},{192,0},{1,65},{65,129},{129,193},{193,1... | collective-permute-start | bytes 1572872 | tf_op jit(solution)/shard_map/ppermute | solution.py:291
  69.0 40.7 %collective-permute-start.9 = (f32[128,1024]{1,0:T(8,128)S(1)}, f32[128,1024]{1,0:T(8,128)}, u32[]{:S(2)}, u32[]{:S(2)}) collective-permute-start(f32[128,1024]{1,0:T(8,128)S(1)} %fusion.6), channel_id=1, source_target_pairs={{0,192},{64,0},{128,64},{192,128},{1,193},{65,1},{129,65},{193,129... | collective-permute-start | bytes 1572872 | tf_op jit(solution)/shard_map/ppermute | solution.py:291
  109.7 7.4 %collective-permute-start.12 = (f32[256,128]{1,0:T(8,128)S(1)}, f32[256,128]{1,0:T(8,128)S(1)}, u32[]{:S(2)}, u32[]{:S(2)}) collective-permute-start(f32[256,128]{1,0:T(8,128)S(1)} %bitcast.22), channel_id=1, source_target_pairs={{0,6},{2,0},{4,2},{6,4},{1,7},{3,1},{5,3},{7,5},{8,14},{10,8},{12,... | collective-permute-start | bytes 393224 | tf_op jit(solution)/shard_map/ppermute | solution.py:291
  109.8 7.3 %collective-permute-start.11 = (f32[256,128]{1,0:T(8,128)S(1)}, f32[256,128]{1,0:T(8,128)S(1)}, u32[]{:S(2)}, u32[]{:S(2)}) collective-permute-start(f32[256,128]{1,0:T(8,128)S(1)} %bitcast.23), channel_id=1, source_target_pairs={{0,4},{2,6},{4,0},{6,2},{1,5},{3,7},{5,1},{7,3},{8,12},{10,14},{12... | collective-permute-start | bytes 393224 | tf_op jit(solution)/shard_map/ppermute | solution.py:291
  109.9 8.3 %collective-permute-start.10 = (f32[256,128]{1,0:T(8,128)S(1)}, f32[256,128]{1,0:T(8,128)S(1)}, u32[]{:S(2)}, u32[]{:S(2)}) collective-permute-start(f32[256,128]{1,0:T(8,128)S(1)} %bitcast.24), channel_id=1, source_target_pairs={{0,2},{2,4},{4,6},{6,0},{1,3},{3,5},{5,7},{7,1},{8,10},{10,12},{12... | collective-permute-start | bytes 393224 | tf_op jit(solution)/shard_map/ppermute | solution.py:291
  118.3 6.3 %collective-permute-start.13 = (f32[4,256,128]{2,1,0:T(8,128)S(1)}, f32[4,256,128]{2,1,0:T(8,128)S(1)}, u32[]{:S(2)}, u32[]{:S(2)}) collective-permute-start(f32[4,256,128]{2,1,0:T(8,128)S(1)} %pad_maximum_fusion.g_ref), channel_id=1, source_target_pairs={{0,1},{1,0},{2,3},{3,2},{4,5},{5,4},{6,7},{7,6},{8,9},{9,8},{10,11... | collective-permute-start | bytes 1572872 | tf_op jit(solution)/shard_map/ppermute | solution.py:347
  121.1 21.9 %all-to-all-start.4 = ((f32[8,16,1024]{2,1,0:T(8,128)}), f32[8,16,1024]{2,1,0:T(8,128)S(1)}, u32[]{:S(2)}, u32[]{:S(2)}) async-start(f32[8,16,1024]{2,1,0:T(8,128)} %bitcast.13), calls=%async_computation.4 | async-start | bytes 1048576 | tf_op jit(solution)/shard_map/all_to_all | solution.py:283
  143.9 22.2 %all-to-all-start.5 = ((f32[8,16,1024]{2,1,0:T(8,128)}), f32[8,16,1024]{2,1,0:T(8,128)}, u32[]{:S(2)}, u32[]{:S(2)}) async-start(f32[8,16,1024]{2,1,0:T(8,128)} %shard_map.85), calls=%async_computation.5 | async-start | bytes 1048576 | tf_op jit(solution)/shard_map/all_to_all | solution.py:283
  167.1 13.5 %collective-permute-start.16 = (f32[128,512]{1,0:T(8,128)S(1)}, f32[128,512]{1,0:T(8,128)S(1)}, u32[]{:S(2)}, u32[]{:S(2)}) collective-permute-start(f32[128,512]{1,0:T(8,128)S(1)} %get-tuple-element.37.b0), channel_id=1, source_target_pairs={{0,192},{64,0},{128,64},{192,128},{1,193},{65,1},{129,65},{193,129... | collective-permute-start | bytes 786440 | tf_op jit(solution)/shard_map/ppermute | solution.py:291
  175.6 31.6 %collective-permute-start.19 = (f32[128,512]{1,0:T(8,128)S(1)}, f32[128,512]{1,0:T(8,128)S(1)}, u32[]{:S(2)}, u32[]{:S(2)}) collective-permute-start(f32[128,512]{1,0:T(8,128)S(1)} %get-tuple-element.36.b0), channel_id=1, source_target_pairs={{0,192},{64,0},{128,64},{192,128},{1,193},{65,1},{129,65},{193,129... | collective-permute-start | bytes 786440 | tf_op jit(solution)/shard_map/ppermute | solution.py:291
  176.5 30.7 %collective-permute-start.18 = (f32[128,512]{1,0:T(8,128)S(1)}, f32[128,512]{1,0:T(8,128)S(1)}, u32[]{:S(2)}, u32[]{:S(2)}) collective-permute-start(f32[128,512]{1,0:T(8,128)S(1)} %get-tuple-element.36.b0), channel_id=1, source_target_pairs={{0,64},{64,128},{128,192},{192,0},{1,65},{65,129},{129,193},{193,1... | collective-permute-start | bytes 786440 | tf_op jit(solution)/shard_map/ppermute | solution.py:291
  177.7 29.5 %collective-permute-start.17 = (f32[128,512]{1,0:T(8,128)S(1)}, f32[128,512]{1,0:T(8,128)S(1)}, u32[]{:S(2)}, u32[]{:S(2)}) collective-permute-start(f32[128,512]{1,0:T(8,128)S(1)} %get-tuple-element.36.b0), channel_id=1, source_target_pairs={{0,128},{64,192},{128,0},{192,64},{1,129},{65,193},{129,1},{193,65... | collective-permute-start | bytes 786440 | tf_op jit(solution)/shard_map/ppermute | solution.py:291
  179.1 23.1 %collective-permute-start.15 = (f32[128,512]{1,0:T(8,128)S(1)}, f32[128,512]{1,0:T(8,128)S(1)}, u32[]{:S(2)}, u32[]{:S(2)}) collective-permute-start(f32[128,512]{1,0:T(8,128)S(1)} %get-tuple-element.37.b0), channel_id=1, source_target_pairs={{0,64},{64,128},{128,192},{192,0},{1,65},{65,129},{129,193},{193,1... | collective-permute-start | bytes 786440 | tf_op jit(solution)/shard_map/ppermute | solution.py:291
  180.6 21.7 %collective-permute-start.14 = (f32[128,512]{1,0:T(8,128)S(1)}, f32[128,512]{1,0:T(8,128)S(1)}, u32[]{:S(2)}, u32[]{:S(2)}) collective-permute-start(f32[128,512]{1,0:T(8,128)S(1)} %get-tuple-element.37.b0), channel_id=1, source_target_pairs={{0,128},{64,192},{128,0},{192,64},{1,129},{65,193},{129,1},{193,65... | collective-permute-start | bytes 786440 | tf_op jit(solution)/shard_map/ppermute | solution.py:291
